TPU v7x, 32 devices: a whole 2x2x4 slice. The times are simulated.
32 devices in a mesh: seq: 8 (over y, x, core), row: 4 (over z).
Axes of the slice: x: 2, y: 2, z: 4, core: 2. Of those that a mesh axis runs over, the one named last changes fastest.
Arguments:
- long_tokens: bfloat16 [4, 1024, 1024], P('row', 'seq'), may hold values from -6 to 6
- short_tokens: bfloat16 [32, 512, 1024], P(('seq', 'row')), may hold values from -6 to 6
- long_length: int32 [4], P('row'), may hold values from 256 to 1024, as said below
- long_cotangent: bfloat16 [4, 1024, 1024], P('row', 'seq'), may hold values from -6 to 6
- short_cotangent: bfloat16 [32, 512, 1024], P(('seq', 'row')), may hold values from -6 to 6
- first_gain: float32 [1024], replicated, may hold values from 0.1 to 1.9
- gate_weight: bfloat16 [1024, 1536], P(None, ('seq', 'row')), may hold values from -0.1875 to 0.1875
- gate_bias: float32 [1536], replicated, may hold values from -3 to 3
- input_weight: bfloat16 [1024, 1536], P(None, ('seq', 'row')), may hold values from -0.1875 to 0.1875
- input_bias: float32 [1536], replicated, may hold values from -3 to 3
- conv_weight: float32 [4, 1536], replicated, may hold values from -3 to 3
- conv_bias: float32 [1536], replicated, may hold values from -2 to 2
- decay_gate_weight: bfloat16 [8, 192, 192], replicated, may hold values from -0.4375 to 0.4375
- decay_gate_bias: float32 [1536], replicated, may hold values from -3 to 3
- input_gate_weight: bfloat16 [8, 192, 192], replicated, may hold values from -0.4375 to 0.4375
- input_gate_bias: float32 [1536], replicated, may hold values from -3 to 3
- decay_param: float32 [1536], replicated, may hold values from -16 to -4
- out_weight: bfloat16 [1536, 1024], P(('seq', 'row')), may hold values from -0.4375 to 0.4375
- second_gain: float32 [1024], replicated, may hold values from 0.1 to 1.9
- mlp_gate_weight: bfloat16 [1024, 3072], P(None, ('seq', 'row')), may hold values from -0.1875 to 0.1875
- mlp_up_weight: bfloat16 [1024, 3072], P(None, ('seq', 'row')), may hold values from -0.1875 to 0.1875
- mlp_down_weight: bfloat16 [3072, 1024], P(('seq', 'row')), may hold values from -0.21875 to 0.21875
Outputs:
- long_output: bfloat16 [4, 1024, 1024], P('row', 'seq')
- short_output: bfloat16 [32, 512, 1024], P(('seq', 'row'))
- long_input_grad: float32 [4, 1024, 1024], P('row', 'seq')
- short_input_grad: float32 [32, 512, 1024], P(('seq', 'row'))
- first_gain_grad: float32 [1024], replicated
- gate_weight_grad: float32 [1024, 1536], P(None, ('seq', 'row'))
- gate_bias_grad: float32 [1536], replicated
- input_weight_grad: float32 [1024, 1536], P(None, ('seq', 'row'))
- input_bias_grad: float32 [1536], replicated
- conv_weight_grad: float32 [4, 1536], replicated
- conv_bias_grad: float32 [1536], replicated
- decay_gate_weight_grad: float32 [8, 192, 192], replicated
- decay_gate_bias_grad: float32 [1536], replicated
- input_gate_weight_grad: float32 [8, 192, 192], replicated
- input_gate_bias_grad: float32 [1536], replicated
- decay_param_grad: float32 [1536], replicated
- out_weight_grad: float32 [1536, 1024], P(('seq', 'row'))
- second_gain_grad: float32 [1024], replicated
- mlp_gate_weight_grad: float32 [1024, 3072], P(None, ('seq', 'row'))
- mlp_up_weight_grad: float32 [1024, 3072], P(None, ('seq', 'row'))
- mlp_down_weight_grad: float32 [3072, 1024], P(('seq', 'row'))
Inputs may be any that keep to these rules, and one draw needn't show every extreme that they name: Positions at or beyond long_length of a long row carry no cotangent; some long row has all 1024 positions real.
All inputs are finite; a program needn't handle non-finite values.
Results may differ from a plain program's by a relative error of at most 0.014.
Values may be sent and summed in bfloat16 or wider, within the bound.
A program may use at most 320 MiB of HBM per device.

v0:
```python
import jax
import jax.numpy as jnp
from jax import lax
from jax.sharding import PartitionSpec as P

EPSILON = 1e-06


def from_behind(value, axis, steps):
    count = lax.axis_size(axis)
    first, last = (max(0, -steps), min(count, count - steps))
    return lax.ppermute(value, axis, [(source, source + steps) for source in range(first, last)])


def prefix(part, axis, combine, identity, reverse):
    count = lax.axis_size(axis)
    place = lax.axis_index(axis)
    ahead = count - 1 - place if reverse else place
    gathered = jax.tree.map(lambda a: lax.all_gather(a, axis), part)
    state = jax.tree.map(lambda a, e: jnp.zeros_like(a) + jnp.asarray(e, a.dtype), part, identity)

    def one(hop, state):
        source = count - 1 - hop if reverse else hop
        return combine(
            state, jax.tree.map(lambda a: lax.dynamic_index_in_dim(a, source, 0, False), gathered)
        )

    return lax.fori_loop(0, ahead, one, state)


def norm_only(values, norm_gain):
    inverse = lax.rsqrt(jnp.mean(values * values, axis=-1, keepdims=True) + EPSILON)
    return values * inverse * norm_gain


def gelu_tanh(values):
    return jax.nn.gelu(values, approximate=True)


def linear_pair(earlier, later):
    return (earlier[0] * later[0], earlier[1] * later[0] + later[1])


def back_prod(grads, weight):
    return lax.dot_general(
        grads, weight, (((1,), (1,)), ((), ())), preferred_element_type=jnp.float32
    )


def split_columns(values, seq_count, row_count):
    return values.reshape(
        values.shape[0], seq_count, row_count, values.shape[1] // (seq_count * row_count)
    )


def left_share(rows_all, parts_all):
    return jnp.einsum("td,tsrh->dsrh", rows_all, parts_all, preferred_element_type=jnp.float32)


def right_share(parts_all, rows_all):
    return jnp.einsum("tsrh,td->srhd", parts_all, rows_all, preferred_element_type=jnp.float32)


def recurrence_gates(decay_pre, input_pre, conv_out, decay_param):
    gate_rate = jax.nn.sigmoid(decay_pre)
    opening = jax.nn.sigmoid(input_pre)
    log_decay = -8.0 * jax.nn.softplus(decay_param) * (0.25 + gate_rate)
    return (jnp.exp(log_decay), jnp.sqrt(-jnp.expm1(2.0 * log_decay)) * opening * conv_out)


def blockwise(values, weight):
    blocks = weight.shape[0]
    split_vals = values.reshape(values.shape[0], blocks, values.shape[1] // blocks)
    product = jnp.einsum("thi,hij->thj", split_vals, weight, preferred_element_type=jnp.float32)
    return product.reshape(values.shape)


def blockwise_back(grads, weight):
    blocks = weight.shape[0]
    split_grads = grads.reshape(grads.shape[0], blocks, grads.shape[1] // blocks)
    product = jnp.einsum("thj,hij->thi", split_grads, weight, preferred_element_type=jnp.float32)
    return product.reshape(grads.shape)


def blockwise_outer(values, grads, blocks):
    split_vals = values.reshape(values.shape[0], blocks, values.shape[1] // blocks)
    split_grads = grads.reshape(grads.shape[0], blocks, grads.shape[1] // blocks)
    return jnp.einsum("thi,thj->hij", split_vals, split_grads, preferred_element_type=jnp.float32)


def shards(
    long_tokens,
    short_tokens,
    long_length,
    long_cotangent,
    short_cotangent,
    first_gain,
    gate_weight,
    gate_bias,
    input_weight,
    input_bias,
    conv_weight,
    conv_bias,
    decay_gate_weight,
    decay_gate_bias,
    input_gate_weight,
    input_gate_bias,
    decay_param,
    out_weight,
    second_gain,
    mlp_gate_weight,
    mlp_up_weight,
    mlp_down_weight,
):
    gathered = (
        lax.all_gather(gate_weight, ("seq", "row"), axis=1, tiled=True),
        lax.all_gather(input_weight, ("seq", "row"), axis=1, tiled=True),
        lax.all_gather(out_weight, ("seq", "row"), axis=0, tiled=True),
        lax.all_gather(mlp_gate_weight, ("seq", "row"), axis=1, tiled=True),
        lax.all_gather(mlp_up_weight, ("seq", "row"), axis=1, tiled=True),
        lax.all_gather(mlp_down_weight, ("seq", "row"), axis=0, tiled=True),
    )
    full_gate, full_input, full_out, full_mgate, full_mup, full_down = gathered
    seq_count = lax.axis_size("seq")
    row_count = lax.axis_size("row")
    long_rows, piece_len, width_dim = long_tokens.shape
    short_rows, short_len, _ = short_tokens.shape
    long_count = long_rows * piece_len
    conv_taps = conv_weight.shape[0]
    rim_len = conv_taps - 1
    blocks = decay_gate_weight.shape[0]
    values = jnp.concatenate(
        [long_tokens.reshape(long_count, width_dim), short_tokens.reshape(-1, width_dim)], axis=0
    ).astype(jnp.float32)
    normed = norm_only(values, first_gain).astype(jnp.bfloat16)
    gate_pre = jnp.dot(normed, full_gate, preferred_element_type=jnp.float32) + gate_bias
    gate_out = gelu_tanh(gate_pre)
    inner_proj = jnp.dot(normed, full_input, preferred_element_type=jnp.float32) + input_bias
    channels = inner_proj.shape[1]
    inner_long = inner_proj[:long_count].reshape(long_rows, piece_len, channels)
    inner_short = inner_proj[long_count:].reshape(short_rows, short_len, channels)
    before = from_behind(inner_long[:, piece_len - rim_len :], "seq", 1)
    padded_long = jnp.concatenate([before, inner_long], axis=1)
    padded_short = jnp.concatenate(
        [jnp.zeros((short_rows, rim_len, channels), jnp.float32), inner_short], axis=1
    )

    def convolve(padded, length):
        summed = conv_bias + conv_weight[0] * padded[:, rim_len : rim_len + length]
        for tap_index in range(1, conv_taps):
            start = rim_len - tap_index
            summed = summed + conv_weight[tap_index] * padded[:, start : start + length]
        return summed

    conv_out = jnp.concatenate(
        [
            convolve(padded_long, piece_len).reshape(long_count, channels),
            convolve(padded_short, short_len).reshape(-1, channels),
        ],
        axis=0,
    )
    conv_low = conv_out.astype(jnp.bfloat16)
    decay_pre = blockwise(conv_low, decay_gate_weight) + decay_gate_bias
    input_pre = blockwise(conv_low, input_gate_weight) + input_gate_bias
    (decays, drives), gates_back = jax.vjp(
        recurrence_gates, decay_pre, input_pre, conv_out, decay_param
    )
    decay_long = decays[:long_count].reshape(long_rows, piece_len, channels)
    drive_long = drives[:long_count].reshape(long_rows, piece_len, channels)
    decay_short = decays[long_count:].reshape(short_rows, short_len, channels)
    drive_short = drives[long_count:].reshape(short_rows, short_len, channels)
    cumul_long, local_long = lax.associative_scan(linear_pair, (decay_long, drive_long), axis=1)
    ones_row = jnp.ones((long_rows, channels), jnp.float32)
    zeros_row = jnp.zeros((long_rows, channels), jnp.float32)
    entering = prefix(
        (cumul_long[:, -1], local_long[:, -1]), "seq", linear_pair, (ones_row, zeros_row), False
    )
    state_in = entering[1]
    state_long = local_long + cumul_long * state_in[:, None]
    _, state_short = lax.associative_scan(linear_pair, (decay_short, drive_short), axis=1)
    states = jnp.concatenate(
        [state_long.reshape(long_count, channels), state_short.reshape(-1, channels)], axis=0
    )
    mix_out = (states * gate_out).astype(jnp.bfloat16)
    residual = values + jnp.dot(mix_out, full_out, preferred_element_type=jnp.float32)
    normed2 = norm_only(residual, second_gain).astype(jnp.bfloat16)
    mlp_gate_out = jnp.dot(normed2, full_mgate, preferred_element_type=jnp.float32)
    mlp_up_out = jnp.dot(normed2, full_mup, preferred_element_type=jnp.float32)
    hidden = (gelu_tanh(mlp_gate_out) * mlp_up_out).astype(jnp.bfloat16)
    result = residual + jnp.dot(hidden, full_down, preferred_element_type=jnp.float32)
    long_output = result[:long_count].reshape(long_rows, piece_len, width_dim).astype(jnp.bfloat16)
    short_output = (
        result[long_count:].reshape(short_rows, short_len, width_dim).astype(jnp.bfloat16)
    )
    regathered = (
        lax.all_gather(gate_weight, ("seq", "row"), axis=1, tiled=True),
        lax.all_gather(input_weight, ("seq", "row"), axis=1, tiled=True),
        lax.all_gather(out_weight, ("seq", "row"), axis=0, tiled=True),
        lax.all_gather(mlp_gate_weight, ("seq", "row"), axis=1, tiled=True),
        lax.all_gather(mlp_up_weight, ("seq", "row"), axis=1, tiled=True),
        lax.all_gather(mlp_down_weight, ("seq", "row"), axis=0, tiled=True),
    )
    full_gate, full_input, full_out, full_mgate, full_mup, full_down = regathered
    positions = lax.axis_index("seq") * piece_len + jnp.arange(piece_len, dtype=jnp.int32)
    keep_mask = (positions[None, :] < long_length[:, None]).astype(jnp.float32)
    upstream = jnp.concatenate(
        [
            (long_cotangent.astype(jnp.float32) * keep_mask[:, :, None]).reshape(
                long_count, width_dim
            ),
            short_cotangent.astype(jnp.float32).reshape(-1, width_dim),
        ],
        axis=0,
    )
    down_low = upstream.astype(jnp.bfloat16)
    normed_all, normed2_all, down_all = (
        lax.all_gather(normed, "row", axis=0, tiled=True),
        lax.all_gather(normed2, "row", axis=0, tiled=True),
        lax.all_gather(down_low, "row", axis=0, tiled=True),
    )
    d_hidden = back_prod(down_low, full_down)
    _, product_back = jax.vjp(
        lambda first_arg, second_arg: gelu_tanh(first_arg) * second_arg, mlp_gate_out, mlp_up_out
    )
    d_mgate, d_mup = product_back(d_hidden)
    mgate_low = d_mgate.astype(jnp.bfloat16)
    mup_low = d_mup.astype(jnp.bfloat16)
    hidden_all, mgate_all, mup_all = (
        lax.all_to_all(
            split_columns(hidden, seq_count, row_count),
            "row",
            split_axis=2,
            concat_axis=0,
            tiled=True,
        ),
        lax.all_to_all(
            split_columns(mgate_low, seq_count, row_count),
            "row",
            split_axis=2,
            concat_axis=0,
            tiled=True,
        ),
        lax.all_to_all(
            split_columns(mup_low, seq_count, row_count),
            "row",
            split_axis=2,
            concat_axis=0,
            tiled=True,
        ),
    )
    grad_down = right_share(hidden_all, down_all)
    grad_mgate = left_share(normed2_all, mgate_all)
    grad_mup = left_share(normed2_all, mup_all)
    d_normed2 = back_prod(mgate_low, full_mgate) + back_prod(mup_low, full_mup)
    _, second_back = jax.vjp(norm_only, residual, second_gain)
    d_resid_norm, grad_second = second_back(d_normed2)
    d_residual = upstream + d_resid_norm
    resid_low = d_residual.astype(jnp.bfloat16)
    resid_all = lax.all_gather(resid_low, "row", axis=0, tiled=True)
    d_mix = back_prod(resid_low, full_out)
    d_states = d_mix * gate_out
    d_gate_out = d_mix * states
    _, gelu_back = jax.vjp(gelu_tanh, gate_pre)
    (d_gate_pre,) = gelu_back(d_gate_out)
    grad_gate_bias = jnp.sum(d_gate_pre, axis=0)
    gate_low = d_gate_pre.astype(jnp.bfloat16)
    d_state_long = d_states[:long_count].reshape(long_rows, piece_len, channels)
    d_state_short = d_states[long_count:].reshape(short_rows, short_len, channels)
    next_long = jnp.concatenate(
        [decay_long[:, 1:], jnp.ones((long_rows, 1, channels), jnp.float32)], axis=1
    )
    reach_long, local_back = lax.associative_scan(
        linear_pair, (next_long, d_state_long), reverse=True, axis=1
    )
    outgoing = (decay_long[:, 0] * reach_long[:, 0], decay_long[:, 0] * local_back[:, 0])
    arriving = prefix(outgoing, "seq", linear_pair, (ones_row, zeros_row), True)
    total_long = local_back + reach_long * arriving[1][:, None]
    next_short = jnp.concatenate(
        [decay_short[:, 1:], jnp.ones((short_rows, 1, channels), jnp.float32)], axis=1
    )
    _, total_short = lax.associative_scan(
        linear_pair, (next_short, d_state_short), reverse=True, axis=1
    )
    prior_long = jnp.concatenate([state_in[:, None], state_long[:, :-1]], axis=1)
    prior_short = jnp.concatenate(
        [jnp.zeros((short_rows, 1, channels), jnp.float32), state_short[:, :-1]], axis=1
    )
    total_grad = jnp.concatenate(
        [total_long.reshape(long_count, channels), total_short.reshape(-1, channels)], axis=0
    )
    prior_states = jnp.concatenate(
        [prior_long.reshape(long_count, channels), prior_short.reshape(-1, channels)], axis=0
    )
    d_decay_pre, d_input_pre, d_conv, grad_decay_param = gates_back(
        (total_grad * prior_states, total_grad)
    )
    grad_decay_bias = jnp.sum(d_decay_pre, axis=0)
    grad_opening_bias = jnp.sum(d_input_pre, axis=0)
    decay_low = d_decay_pre.astype(jnp.bfloat16)
    opening_low = d_input_pre.astype(jnp.bfloat16)
    grad_decay_weight = blockwise_outer(conv_low, decay_low, blocks)
    grad_opening_weight = blockwise_outer(conv_low, opening_low, blocks)
    d_conv = (
        d_conv
        + blockwise_back(decay_low, decay_gate_weight)
        + blockwise_back(opening_low, input_gate_weight)
    )
    grad_conv_bias = jnp.sum(d_conv, axis=0)
    d_conv_long = d_conv[:long_count].reshape(long_rows, piece_len, channels)
    d_conv_short = d_conv[long_count:].reshape(short_rows, short_len, channels)
    grad_conv_weight = jnp.stack(
        [
            jnp.sum(
                d_conv_long * padded_long[:, rim_len - tap_index : rim_len - tap_index + piece_len],
                axis=(0, 1),
            )
            + jnp.sum(
                d_conv_short
                * padded_short[:, rim_len - tap_index : rim_len - tap_index + short_len],
                axis=(0, 1),
            )
            for tap_index in range(conv_taps)
        ]
    )
    after_rows = from_behind(d_conv_long[:, :rim_len], "seq", -1)
    trail_long = jnp.concatenate([d_conv_long, after_rows], axis=1)
    trail_short = jnp.concatenate(
        [d_conv_short, jnp.zeros((short_rows, rim_len, channels), jnp.float32)], axis=1
    )

    def spread(trail_grads, length):
        summed = conv_weight[0] * trail_grads[:, 0:length]
        for tap_index in range(1, conv_taps):
            summed = (
                summed + conv_weight[tap_index] * trail_grads[:, tap_index : tap_index + length]
            )
        return summed

    d_inner = jnp.concatenate(
        [
            spread(trail_long, piece_len).reshape(long_count, channels),
            spread(trail_short, short_len).reshape(-1, channels),
        ],
        axis=0,
    )
    grad_input_bias = jnp.sum(d_inner, axis=0)
    inner_low = d_inner.astype(jnp.bfloat16)
    mix_all, gate_all, inner_all = (
        lax.all_to_all(
            split_columns(mix_out, seq_count, row_count),
            "row",
            split_axis=2,
            concat_axis=0,
            tiled=True,
        ),
        lax.all_to_all(
            split_columns(gate_low, seq_count, row_count),
            "row",
            split_axis=2,
            concat_axis=0,
            tiled=True,
        ),
        lax.all_to_all(
            split_columns(inner_low, seq_count, row_count),
            "row",
            split_axis=2,
            concat_axis=0,
            tiled=True,
        ),
    )
    grad_out = right_share(mix_all, resid_all)
    grad_gate = left_share(normed_all, gate_all)
    grad_input = left_share(normed_all, inner_all)
    d_normed = back_prod(gate_low, full_gate) + back_prod(inner_low, full_input)
    _, first_back = jax.vjp(norm_only, values, first_gain)
    d_values_norm, grad_first = first_back(d_normed)
    d_values = d_residual + d_values_norm
    weight_grads = (
        lax.psum_scatter(
            grad_gate.astype(jnp.bfloat16), "seq", scatter_dimension=1, tiled=True
        ).astype(jnp.float32),
        lax.psum_scatter(
            grad_input.astype(jnp.bfloat16), "seq", scatter_dimension=1, tiled=True
        ).astype(jnp.float32),
        lax.psum_scatter(
            grad_out.astype(jnp.bfloat16), "seq", scatter_dimension=0, tiled=True
        ).astype(jnp.float32),
        lax.psum_scatter(
            grad_mgate.astype(jnp.bfloat16), "seq", scatter_dimension=1, tiled=True
        ).astype(jnp.float32),
        lax.psum_scatter(
            grad_mup.astype(jnp.bfloat16), "seq", scatter_dimension=1, tiled=True
        ).astype(jnp.float32),
        lax.psum_scatter(
            grad_down.astype(jnp.bfloat16), "seq", scatter_dimension=0, tiled=True
        ).astype(jnp.float32),
    )
    small_grads = lax.psum(
        (
            grad_first,
            grad_gate_bias,
            grad_input_bias,
            grad_conv_weight,
            grad_conv_bias,
            grad_decay_weight,
            grad_decay_bias,
            grad_opening_weight,
            grad_opening_bias,
            grad_decay_param,
            grad_second,
        ),
        ("seq", "row"),
    )
    gate_share = weight_grads[0].reshape(width_dim, -1)
    input_share = weight_grads[1].reshape(width_dim, -1)
    out_share = weight_grads[2].reshape(-1, width_dim)
    mgate_share = weight_grads[3].reshape(width_dim, -1)
    mup_share = weight_grads[4].reshape(width_dim, -1)
    down_share = weight_grads[5].reshape(-1, width_dim)
    long_input_grad = d_values[:long_count].reshape(long_rows, piece_len, width_dim)
    short_input_grad = d_values[long_count:].reshape(short_rows, short_len, width_dim)
    return (
        long_output,
        short_output,
        long_input_grad,
        short_input_grad,
        small_grads[0],
        gate_share,
        small_grads[1],
        input_share,
        small_grads[2],
        small_grads[3],
        small_grads[4],
        small_grads[5],
        small_grads[6],
        small_grads[7],
        small_grads[8],
        small_grads[9],
        out_share,
        small_grads[10],
        mgate_share,
        mup_share,
        down_share,
    )


def solution(mesh):
    placed = (
        P("row", "seq", None),
        P(("seq", "row"), None, None),
        P("row"),
        P("row", "seq", None),
        P(("seq", "row"), None, None),
        P(),
        P(None, ("seq", "row")),
        P(),
        P(None, ("seq", "row")),
        P(),
        P(),
        P(),
        P(),
        P(),
        P(),
        P(),
        P(),
        P(("seq", "row"), None),
        P(),
        P(None, ("seq", "row")),
        P(None, ("seq", "row")),
        P(("seq", "row"), None),
    )
    return jax.shard_map(
        shards,
        mesh=mesh,
        in_specs=placed,
        out_specs=(
            P("row", "seq", None),
            P(("seq", "row"), None, None),
            P("row", "seq", None),
            P(("seq", "row"), None, None),
            P(),
            P(None, ("seq", "row")),
            P(),
            P(None, ("seq", "row")),
            P(),
            P(),
            P(),
            P(),
            P(),
            P(),
            P(),
            P(),
            P(("seq", "row"), None),
            P(),
            P(None, ("seq", "row")),
            P(None, ("seq", "row")),
            P(("seq", "row"), None),
        ),
        check_vma=False,
    )
```

profile of v0, /device:TPU:0, one launch (start us, length us, event | category | flops | bytes accessed | tf_op | source)
XLA Modules:
  0.0 1808.7 jit_solution(649788114214829039)
XLA Ops:
  17.0 55.7 %all-gather.11.cloned.1.call-done = bf16[1024,1536]{0,1:T(8,128)(2,1)} async-done(((bf16[1024,48]{0,1:T(8,128)(2,1)}), bf16[1024,1536]{0,1:T(8,128)(2,1)}) %all-gather.11.cloned.1.call-update) | async-done | bytes 3145744 | tf_op jit(solution)/shard_map/all_gather | solution.py:117
  333.9 10.3 all_gather.52
  350.7 8.3 all_gather.51
  388.5 9.7 pad.333
  414.3 9.5 multiply_convert_fusion.2
  502.3 12.9 slice.1202
  515.2 12.8 slice.1207
  527.9 13.0 slice.1267
  559.1 10.7 fusion.169
  569.7 10.7 fusion.170
  580.4 17.0 multiply_convert_fusion
  597.5 8.9 fusion.171
  614.3 10.0 fusion.138
  654.9 24.7 %reverse.16 = f32[512,1536]{1,0:T(8,128)} reverse(f32[512,1536]{1,0:T(8,128)} %slice.1418), dimensions={0} | reverse | bytes 6291456 | tf_op jit(solution)/shard_map/reverse.7
  798.8 13.2 all_gather.58
  812.0 8.6 all_gather.59
  851.1 9.7 pad.379
  871.6 24.7 %rev.21 = f32[1,512,1536]{2,1,0:T(8,128)} reverse(f32[1,512,1536]{2,1,0:T(8,128)} %add.1024), dimensions={1} | reverse | bytes 6291456 | tf_op jit(solution)/shard_map/rev | solution.py:281
  899.9 12.6 fusion.71
  939.0 8.8 fusion.20
  967.3 17.6 all-to-all-done
  1000.1 34.3 %all-to-all-done.1 = bf16[640,8,4,48]{0,3,1,2:T(8,128)(2,1)} async-done(((bf16[640,8,4,48]{0,3,1,2:T(8,128)(2,1)}), bf16[640,8,4,48]{0,3,1,2:T(8,128)(2,1)}, u32[]{:S(2)}, u32[]{:S(2)}) %all-to-all-start.1) | async-done | bytes 1966112 | tf_op jit(solution)/shard_map/all_to_all | solution.py:363
  1050.5 160.1 %all-to-all-done.4 = bf16[640,8,4,96]{0,3,1,2:T(8,128)(2,1)} async-done(((bf16[640,8,4,96]{0,3,1,2:T(8,128)(2,1)}), bf16[640,8,4,96]{0,3,1,2:T(8,128)(2,1)}, u32[]{:S(2)}, u32[]{:S(2)}) %all-to-all-start.4) | async-done | bytes 3932192 | tf_op jit(solution)/shard_map/all_to_all | solution.py:243
  1242.8 57.6 %all-to-all-done.3 = bf16[640,8,4,96]{0,3,1,2:T(8,128)(2,1)} async-done(((bf16[640,8,4,96]{0,3,1,2:T(8,128)(2,1)}), bf16[640,8,4,96]{0,3,1,2:T(8,128)(2,1)}, u32[]{:S(2)}, u32[]{:S(2)}) %all-to-all-start.3) | async-done | bytes 3932192 | tf_op jit(solution)/shard_map/all_to_all | solution.py:236
  1328.7 8.3 add_convert_fusion
  1363.3 28.9 %all-to-all-done.5 = bf16[640,8,4,96]{0,3,1,2:T(8,128)(2,1)} async-done(((bf16[640,8,4,96]{0,3,1,2:T(8,128)(2,1)}), bf16[640,8,4,96]{0,3,1,2:T(8,128)(2,1)}, u32[]{:S(2)}, u32[]{:S(2)}) %all-to-all-start.5) | async-done | bytes 3932192 | tf_op jit(solution)/shard_map/all_to_all | solution.py:229
  1406.8 9.1 fusion.60
  1416.3 11.0 multiply_reduce_fusion
  1459.4 11.8 reduce-scatter.17.cloned.1.call-done
  1472.9 36.3 %reduce-scatter.11.cloned.1.call-done = bf16[1,1,48,1024]{3,2,0,1:T(8,128)(2,1)} async-done(((bf16[8,1,48,1024]{3,2,0,1:T(8,128)(2,1)}), bf16[1,1,48,1024]{3,2,0,1:T(8,128)(2,1)}) %reduce-scatter.11.cloned.1.call-update) | async-done | bytes 98320 | tf_op jit(solution)/shard_map/reduce_scatter | solution.py:385
  1510.8 131.5 %all-reduce.103.cloned.1.call-done = (f32[1024]{0:T(1024)}, f32[1536]{0:T(1024)}, f32[1536]{0:T(1024)}, f32[4,1536]{1,0:T(4,128)}, f32[1536]{0:T(1024)}, /*index...) async-done(((f32[1024]{0:T(1024)}, f32[1536]{0:T(1024)}, f32[1536]{0:T(1024)}, f32[4,1536]{1,0:T(4,128)}, f32[1536]{0:T(1024)}, /*index=5*/f32[1536]{0:T(1024)}, ...) | async-done | bytes 69648 | tf_op jit(solution)/shard_map/psum | solution.py:398
  1642.3 146.2 %all-reduce.105.cloned.1.call-done = (f32[8,192,192]{2,1,0:T(8,128)}, f32[8,192,192]{2,1,0:T(8,128)}) async-done(((f32[8,192,192]{2,1,0:T(8,128)}, f32[8,192,192]{2,1,0:T(8,128)}), (f32[8,192,192]{2,1,0:T(8,128)}, f32[8,192,192]{2,1,0:T(8,128)})) %all-reduce.105.cloned.1.call-update) | async-done | bytes 2359312 | tf_op jit(solution)/shard_map/psum | solution.py:398
  (926 shorter events, 845.5 us)
Async XLA Ops:
  7.2 84.4 %copy-start = (bf16[8,192,192]{2,1,0:T(8,128)(2,1)S(1)}, bf16[8,192,192]{2,1,0:T(8,128)(2,1)}, u32[]{:S(2)}) copy-start(bf16[8,192,192]{2,1,0:T(8,128)(2,1)} %param.38) | copy-start | bytes 1769476
  7.2 65.5 %all-gather.11.cloned.1.call-start = ((), (), s32[]{:S(2)}) async-start(), calls=%async_computation.12 | async-start | bytes 3244032 | tf_op jit(solution)/shard_map/all_gather | solution.py:117
  8.0 406.3 %all-gather.13.cloned.1.call-start = ((), (), s32[]{:S(2)}) async-start(), calls=%async_computation.13 | async-start | bytes 3244032 | tf_op jit(solution)/shard_map/all_gather | solution.py:116
  8.7 415.1 %all-gather.15.cloned.1.call-start = ((), (), s32[]{:S(2)}) async-start(), calls=%async_computation.14 | async-start | bytes 3244032 | tf_op jit(solution)/shard_map/all_gather | solution.py:118
  9.5 549.6 %all-gather.17.cloned.1.call-start = ((), (), s32[]{:S(2)}) async-start(), calls=%async_computation.15 | async-start | bytes 6488064 | tf_op jit(solution)/shard_map/all_gather | solution.py:119
  10.0 559.7 %all-gather.19.cloned.1.call-start = ((), (), s32[]{:S(2)}) async-start(), calls=%async_computation.16 | async-start | bytes 6488064 | tf_op jit(solution)/shard_map/all_gather | solution.py:120
  10.6 569.8 %all-gather.21.cloned.1.call-start = ((), (), s32[]{:S(2)}) async-start(), calls=%async_computation.17 | async-start | bytes 6488064 | tf_op jit(solution)/shard_map/all_gather | solution.py:121
  11.2 1206.5 %all-gather.23.cloned.1.call-start = ((), (), s32[]{:S(2)}) async-start(), calls=%async_computation.18 | async-start | bytes 6553600 | tf_op jit(solution)/shard_map/all_gather | solution.py:217
  16.8 1302.1 %all-gather.27.cloned.1.call-start = ((), (), s32[]{:S(2)}) async-start(), calls=%async_computation.23 | async-start | bytes 6553600 | tf_op jit(solution)/shard_map/all_gather | solution.py:218
  16.9 70.1 %copy-start.62 = (f32[1536]{0:T(1024)}, f32[1536]{0:T(1024)S(1)}, u32[]{:S(2)}) copy-start(f32[1536]{0:T(1024)S(1)} %get-tuple-element.164) | copy-start | bytes 18436
  16.9 70.1 %copy-start.64 = (f32[1536]{0:T(1024)}, f32[1536]{0:T(1024)S(1)}, u32[]{:S(2)}) copy-start(f32[1536]{0:T(1024)S(1)} %get-tuple-element.165) | copy-start | bytes 18436
  16.9 70.1 %copy-start.66 = (f32[1536]{0:T(1024)}, f32[1536]{0:T(1024)S(1)}, u32[]{:S(2)}) copy-start(f32[1536]{0:T(1024)S(1)} %get-tuple-element.166) | copy-start | bytes 18436
  17.0 418.0 %copy-start.74 = (f32[1536]{0:T(1024)}, f32[1536]{0:T(1024)S(1)}, u32[]{:S(2)}) copy-start(f32[1536]{0:T(1024)S(1)} %fusion.114) | copy-start | bytes 18436
  77.6 9.4 collective-permute-start
  431.5 975.3 %all-gather.29.cloned.1.call-start = ((), (), s32[]{:S(2)}) async-start(), calls=%async_computation.26 | async-start | bytes 6553600 | tf_op jit(solution)/shard_map/all_gather | solution.py:219
  549.9 383.8 %all-to-all-start.2 = ((bf16[640,8,4,48]{0,3,1,2:T(8,128)(2,1)}), bf16[640,8,4,48]{0,3,1,2:T(8,128)(2,1)}, u32[]{:S(2)}, u32[]{:S(2)}) async-start(bf16[640,8,4,48]{0,3,1,2:T(8,128)(2,1)} %copy.108), calls=%async_computation.4 | async-start | bytes 3932160 | tf_op jit(solution)/shard_map/all_to_all | solution.py:349
  933.7 51.1 %all-to-all-start = ((bf16[640,8,4,48]{0,3,1,2:T(8,128)(2,1)}), bf16[640,8,4,48]{0,3,1,2:T(8,128)(2,1)S(1)}, u32[]{:S(2)}, u32[]{:S(2)}) async-start(bf16[640,8,4,48]{0,3,1,2:T(8,128)(2,1)} %copy.101), calls=%async_computation | async-start | bytes 3932160 | tf_op jit(solution)/shard_map/all_to_all | solution.py:356
  950.7 8.3 collective-permute-start.1
  984.9 49.5 %all-to-all-start.1 = ((bf16[640,8,4,48]{0,3,1,2:T(8,128)(2,1)}), bf16[640,8,4,48]{0,3,1,2:T(8,128)(2,1)}, u32[]{:S(2)}, u32[]{:S(2)}) async-start(bf16[640,8,4,48]{0,3,1,2:T(8,128)(2,1)} %copy.105), calls=%async_computation.2 | async-start | bytes 3932160 | tf_op jit(solution)/shard_map/all_to_all | solution.py:363
  1034.4 176.2 %all-to-all-start.4 = ((bf16[640,8,4,96]{0,3,1,2:T(8,128)(2,1)}), bf16[640,8,4,96]{0,3,1,2:T(8,128)(2,1)}, u32[]{:S(2)}, u32[]{:S(2)}) async-start(bf16[640,8,4,96]{0,3,1,2:T(8,128)(2,1)} %copy.114), calls=%async_computation.8 | async-start | bytes 7864320 | tf_op jit(solution)/shard_map/all_to_all | solution.py:243
  1039.2 388.2 %all-gather.25.cloned.1.call-start = ((), (), s32[]{:S(2)}) async-start(), calls=%async_computation.21 | async-start | bytes 6553600 | tf_op jit(solution)/shard_map/all_gather | solution.py:259
  1210.6 89.7 %all-to-all-start.3 = ((bf16[640,8,4,96]{0,3,1,2:T(8,128)(2,1)}), bf16[640,8,4,96]{0,3,1,2:T(8,128)(2,1)}, u32[]{:S(2)}, u32[]{:S(2)}) async-start(bf16[640,8,4,96]{0,3,1,2:T(8,128)(2,1)} %copy.111), calls=%async_computation.6 | async-start | bytes 7864320 | tf_op jit(solution)/shard_map/all_to_all | solution.py:236
  1215.4 237.3 %reduce-scatter.7.cloned.1.call-start = ((), (), s32[]{:S(2)}) async-start(), calls=%async_computation.19 | async-start | bytes 884736 | tf_op jit(solution)/shard_map/reduce_scatter | solution.py:379
  1300.3 91.9 %all-to-all-start.5 = ((bf16[640,8,4,96]{0,3,1,2:T(8,128)(2,1)}), bf16[640,8,4,96]{0,3,1,2:T(8,128)(2,1)}, u32[]{:S(2)}, u32[]{:S(2)}) async-start(bf16[640,8,4,96]{0,3,1,2:T(8,128)(2,1)} %copy.117), calls=%async_computation.10 | async-start | bytes 7864320 | tf_op jit(solution)/shard_map/all_to_all | solution.py:229
  1305.1 149.2 %reduce-scatter.9.cloned.1.call-start = ((), (), s32[]{:S(2)}) async-start(), calls=%async_computation.20 | async-start | bytes 884736 | tf_op jit(solution)/shard_map/reduce_scatter | solution.py:382
  1310.9 145.0 %reduce-scatter.15.cloned.1.call-start = ((), (), s32[]{:S(2)}) async-start(), calls=%async_computation.25 | async-start | bytes 1769472 | tf_op jit(solution)/shard_map/reduce_scatter | solution.py:391
  1327.8 129.9 %reduce-scatter.13.cloned.1.call-start = ((), (), s32[]{:S(2)}) async-start(), calls=%async_computation.24 | async-start | bytes 1769472 | tf_op jit(solution)/shard_map/reduce_scatter | solution.py:388
  1350.6 120.6 %reduce-scatter.17.cloned.1.call-start = ((), (), s32[]{:S(2)}) async-start(), calls=%async_computation.27 | async-start | bytes 1769472 | tf_op jit(solution)/shard_map/reduce_scatter | solution.py:394
  1415.9 93.2 %reduce-scatter.11.cloned.1.call-start = ((), (), s32[]{:S(2)}) async-start(), calls=%async_computation.22 | async-start | bytes 884736 | tf_op jit(solution)/shard_map/reduce_scatter | solution.py:385
  1433.9 208.4 %all-reduce.103.cloned.1.call-start = ((), (), s32[]{:S(2)}) async-start(), calls=%async_computation.28 | async-start | bytes 163840 | tf_op jit(solution)/shard_map/psum | solution.py:398
  1445.8 342.7 %all-reduce.105.cloned.1.call-start = ((), (), s32[]{:S(2)}) async-start(), calls=%async_computation.29 | async-start | bytes 6291456 | tf_op jit(solution)/shard_map/psum | solution.py:398
  1642.3 155.5 %copy-start.139 = (f32[1536]{0:T(1024)S(1)}, f32[1536]{0:T(1024)}, u32[]{:S(2)}) copy-start(f32[1536]{0:T(1024)} %get-tuple-element.479) | copy-start | bytes 18436
  (140 other events, 1526.9 us)
Sparse Core Ops, SparseCore 0:
  11.0 61.7 all-gather.10
  75.6 57.8 all-gather.12
  136.4 57.8 all-gather.14
  197.0 68.3 all-gather.16
  268.2 68.0 all-gather.18
  339.0 68.0 all-gather.20
  408.7 96.5 all-gather.22
  506.8 138.3 all-gather.26
  646.8 96.0 all-gather.28
  1041.3 169.4 all-gather.24
  1223.6 35.0 reduce-scatter.6
  1311.0 35.0 reduce-scatter.8
  1349.4 38.4 reduce-scatter.14
  1391.1 38.4 reduce-scatter.12
  1432.7 38.4 reduce-scatter.16
  1474.2 34.9 reduce-scatter.10
  1517.2 125.0 all-reduce.102
  1649.3 139.1 all-reduce.104
where the time goes:
time: 1830 us; the launch traced here: 1810 us
  waiting for transfers between devices  685 us (37%)
  local copies, waits for them, and re-layouts  662 us (36%)
  other arithmetic  211 us (12%)
  matrix products  157 us (9%)
  blocking collectives  40.4 us (2%)
  starting transfers between devices  33.9 us (2%)
  between operations  18.6 us (1%)
    psum x2, waiting for transfers between devices, shards(): lax.psum((grad_first, grad_gate_bias, grad_input_bias, grad_conv_weight,...  278 us
    all_to_all x1, waiting for transfers between devices, shards(): lax.all_to_all(split_columns(mup_low, seq_count, row_count), 'row', split...  160 us
    slice x56, local copies, waits for them, and re-layouts, shards(): lax.associative_scan(linear_pair, (next_short, d_state_short), reverse=Tr...  160 us
    slice x53, local copies, waits for them, and re-layouts, shards(): lax.associative_scan(linear_pair, (decay_short, drive_short), axis=1)  123 us
    all_to_all x1, waiting for transfers between devices, shards(): lax.all_to_all(split_columns(mgate_low, seq_count, row_count), 'row', spl...  57.6 us
    all_gather x1, waiting for transfers between devices, shards(): lax.all_gather(input_weight, ('seq', 'row'), axis=1, tiled=True)  55.7 us
    dot_general x6, matrix products, back_prod(): lax.dot_general(grads, weight, (((1,), (1,)), ((), ())), preferred_elemen...  55.2 us
    slice x44, local copies, waits for them, and re-layouts, shards(): lax.associative_scan(linear_pair, (decay_long, drive_long), axis=1)  48.2 us
  transfers between devices with their start and end apart: 26, of which 10 were waited for; matrix products, arithmetic and copies ran while one was open for 56% of the time, Pallas kernels for 0%

commit v1 on v0

v1 whole, which is shorter than its diff:
```python
import functools

import jax
import jax.numpy as jnp
from jax import lax
from jax.experimental import pallas as pl
from jax.experimental.pallas import tpu as pltpu
from jax.sharding import PartitionSpec as P

EPSILON = 1e-06
F32 = jnp.float32
BF16 = jnp.bfloat16
SLOTS = 32
TILE = 16
HALO = 16
MIB = 1024 * 1024
GELU_A = 0.7978845608028654
GELU_B = 0.044715


def dot_nn(a, b):
    return lax.dot_general(a, b, (((1,), (0,)), ((), ())), preferred_element_type=F32)


def dot_nt(a, b):
    return lax.dot_general(a, b, (((1,), (1,)), ((), ())), preferred_element_type=F32)


def dot_tn(a, b):
    return lax.dot_general(a, b, (((0,), (0,)), ((), ())), preferred_element_type=F32)


def sigmoid(v):
    return 0.5 * jnp.tanh(0.5 * v) + 0.5


def gelu(v):
    t = jnp.tanh(v * (GELU_A + (GELU_A * GELU_B) * (v * v)))
    h = 0.5 * v
    return h + h * t


def gelu_pair(v):
    w = v * v
    t = jnp.tanh(v * (GELU_A + (GELU_A * GELU_B) * w))
    h = 0.5 * v
    slope = 0.5 + 0.5 * t + (h - h * (t * t)) * (GELU_A + (3.0 * GELU_A * GELU_B) * w)
    return h + h * t, slope


def row_iota(shape):
    return lax.broadcasted_iota(jnp.int32, shape, 0)


def at(j):
    return pl.ds(pl.multiple_of(j * TILE, TILE), TILE)


def scan_tile(a, b, reverse):
    rows = row_iota(a.shape)
    step = 1
    while step < TILE:
        if reverse:
            keep, shift = rows < TILE - step, TILE - step
        else:
            keep, shift = rows >= step, step
        b = jnp.where(keep, a * pltpu.roll(b, shift, 0) + b, b)
        a = jnp.where(keep, a * pltpu.roll(a, shift, 0), a)
        step *= 2
    return a, b


def shift_down(cur, prev, k):
    if k == 0:
        return cur
    rows = row_iota(cur.shape)
    return jnp.where(rows < k, pltpu.roll(prev, k, 0), pltpu.roll(cur, k, 0))


def shift_up(cur, later, k):
    if k == 0:
        return cur
    rows = row_iota(cur.shape)
    return jnp.where(
        rows >= TILE - k, pltpu.roll(later, TILE - k, 0), pltpu.roll(cur, TILE - k, 0)
    )


def fold(v):
    return v[0:8] + v[8:16]


def flat(block):
    return block.reshape(block.shape[0] * block.shape[1], block.shape[2])


def gates(dp, ip, c8):
    rate = sigmoid(dp)
    opening = sigmoid(ip)
    log_decay = -c8 * (0.25 + rate)
    decay = jnp.exp(log_decay)
    square = -jnp.tanh(log_decay) * (1.0 + decay * decay)
    return rate, opening, decay, square


GB, IB, CW, CB, DB, OB, C8, S8 = 0, 1, 2, 6, 7, 8, 9, 10


def conv_tile(in_ref, pc_ref, j, live):
    cur = in_ref[at(j), :]
    prev = in_ref[at(j - 1), :] * live
    out = pc_ref[CB : CB + 1, :] + pc_ref[CW : CW + 1, :] * cur
    moved = [cur]
    for k in range(1, 4):
        m = shift_down(cur, prev, k)
        moved.append(m)
        out = out + pc_ref[CW + k : CW + k + 1, :] * m
    return out, moved


def front_kernel(
    ltiles, tiles, first_ref, x_ref, gain_ref, wg_ref, wi_ref, wd_ref, wo_ref, pc_ref,
    gp_ref, in_ref, dp_ref, ip_ref, st_ref, pr_ref, mix_ref, end_ref, nm_ref, cv_ref, cl_ref,
):
    @pl.when(pl.program_id(0) == 0)
    def _():
        @pl.loop(0, tiles)
        def _(j):
            v = x_ref[at(j), :].astype(F32)
            s = lax.rsqrt(jnp.mean(v * v, axis=1, keepdims=True) + EPSILON)
            nm_ref[at(j), :] = (v * s * gain_ref[...]).astype(BF16)

    nm = nm_ref[...]
    gp_ref[...] = dot_nt(nm, flat(wg_ref[...])) + pc_ref[GB : GB + 1, :]
    in_ref[...] = dot_nt(nm, flat(wi_ref[...])) + pc_ref[IB : IB + 1, :]
    in_ref[0:HALO, :] = in_ref[0:HALO, :] * first_ref[0, 0]
    cl_ref[0:HALO, :] = jnp.zeros((HALO, cl_ref.shape[1]), BF16)

    @pl.loop(1, tiles)
    def _(j):
        live = jnp.where(j == 1 + ltiles, 0.0, 1.0)
        out, _ = conv_tile(in_ref, pc_ref, j, live)
        cv_ref[at(j), :] = out
        cl_ref[at(j), :] = out.astype(BF16)

    low = cl_ref[...]
    dp_ref[...] = dot_nn(low, wd_ref[0]) + pc_ref[DB : DB + 1, :]
    ip_ref[...] = dot_nn(low, wo_ref[0]) + pc_ref[OB : OB + 1, :]

    def scanned(j):
        _, opening, a, square = gates(dp_ref[at(j), :], ip_ref[at(j), :], pc_ref[C8 : C8 + 1, :])
        b = (square * lax.rsqrt(square)) * opening * cv_ref[at(j), :]
        return scan_tile(a, b, False)

    width = gp_ref.shape[1]

    def long_step(i, carry):
        state, reach = carry
        a, b = scanned(1 + i)
        s = b + a * state
        r = a * reach
        st_ref[at(1 + i), :] = s
        pr_ref[at(1 + i), :] = r
        return s[TILE - 1 : TILE], r[TILE - 1 : TILE]

    state, reach = lax.fori_loop(
        0, ltiles, long_step, (jnp.zeros((1, width), F32), jnp.ones((1, width), F32))
    )
    end_ref[...] = jnp.concatenate([reach, state, jnp.zeros((6, width), F32)], axis=0)

    def short_step(i, state):
        j = 1 + ltiles + i
        a, b = scanned(j)
        s = b + a * state
        st_ref[at(j), :] = s
        mix_ref[at(i), :] = (s * gelu(gp_ref[at(j), :])).astype(BF16)
        return s[TILE - 1 : TILE]

    lax.fori_loop(0, tiles - 1 - ltiles, short_step, jnp.zeros((1, width), F32))


def mlp_kernel(
    ltiles, tiles, x_ref, cot_ref, st_ref, pr_ref, gp_ref, sin_ref, mixs_ref, wo_ref, gain_ref,
    w_ref, out_ref, dres_ref, rlow_ref, mixl_ref, gain_grad_ref, dw_ref,
    n2_ref, acc_o, acc_n, g_ref, u_ref, d_ref, h_ref, dg_ref, du_ref,
):
    step = pl.program_id(0)
    lrows = ltiles * TILE
    half = g_ref.shape[1] // 2
    share = w_ref.shape[1] // 3

    @pl.when(step == 0)
    def _():
        s_in = sin_ref[0:1, :]

        @pl.loop(0, ltiles)
        def _(i):
            s = st_ref[at(1 + i), :] + pr_ref[at(1 + i), :] * s_in
            mixl_ref[at(i), :] = (s * gelu(gp_ref[at(1 + i), :])).astype(BF16)

        wo = flat(wo_ref[...])
        dres_ref[0:lrows, :] = dot_nn(mixl_ref[...], wo)
        dres_ref[lrows:, :] = dot_nn(mixs_ref[...], wo)

        @pl.loop(0, tiles)
        def _(i):
            r = dres_ref[at(i), :] + x_ref[at(1 + i), :].astype(F32)
            dres_ref[at(i), :] = r
            acc_o[at(i), :] = r
            s = lax.rsqrt(jnp.mean(r * r, axis=1, keepdims=True) + EPSILON)
            n2_ref[at(i), :] = (r * s * gain_ref[...]).astype(BF16)

        acc_n[...] = jnp.zeros_like(acc_n)

    n2 = n2_ref[...]
    wg = flat(w_ref[:, 0:share, :])
    wu = flat(w_ref[:, share : 2 * share, :])
    wd = flat(w_ref[:, 2 * share :, :])
    g_ref[...] = dot_nt(n2, wg)
    u_ref[...] = dot_nt(n2, wu)
    d_ref[...] = dot_nt(cot_ref[...], wd)

    @pl.loop(0, tiles)
    def _(i):
        for k in range(2):
            cols = slice(k * half, (k + 1) * half)
            ge, slope = gelu_pair(g_ref[at(i), cols])
            u = u_ref[at(i), cols]
            d = d_ref[at(i), cols]
            h_ref[at(i), cols] = (ge * u).astype(BF16)
            dg_ref[at(i), cols] = (d * u * slope).astype(BF16)
            du_ref[at(i), cols] = (d * ge).astype(BF16)

    acc_o[...] += dot_nn(h_ref[...], wd)
    acc_n[...] += dot_nn(dg_ref[...], wg) + dot_nn(du_ref[...], wu)
    shape = (dw_ref.shape[0], share, dw_ref.shape[2])
    dw_ref[:, 0:share, :] = dot_tn(dg_ref[...], n2).astype(BF16).reshape(shape)
    dw_ref[:, share : 2 * share, :] = dot_tn(du_ref[...], n2).astype(BF16).reshape(shape)
    dw_ref[:, 2 * share :, :] = dot_tn(h_ref[...], cot_ref[...]).astype(BF16).reshape(shape)

    @pl.when(step == pl.num_programs(0) - 1)
    def _():
        def one(i, total):
            r = dres_ref[at(i), :]
            out_ref[at(i), :] = acc_o[at(i), :].astype(BF16)
            dn = acc_n[at(i), :]
            s = lax.rsqrt(jnp.mean(r * r, axis=1, keepdims=True) + EPSILON)
            e = dn * gain_ref[...]
            inner = jnp.mean(e * r, axis=1, keepdims=True)
            dr = cot_ref[at(i), :].astype(F32) + s * e - r * (s * s * s * inner)
            dres_ref[at(i), :] = dr
            rlow_ref[at(i), :] = dr.astype(BF16)
            return total + fold(dn * (r * s))

        gain_grad_ref[...] = lax.fori_loop(0, tiles, one, jnp.zeros(gain_grad_ref.shape, F32))


def back_kernel(
    ltiles, tiles, rlow_ref, wo_ref, mixl_ref, mixs_ref, gp_ref, st_ref, pr_ref, sin_ref, dp_ref,
    pc_ref, dwo_ref, gl_ref, tot_ref, rch_ref, end_ref, bias_ref, dm_ref,
):
    lrows = ltiles * TILE
    width = gp_ref.shape[1]
    rlow = rlow_ref[...]
    dm_ref[...] = dot_nt(rlow, flat(wo_ref[...]))
    grad = dot_tn(mixl_ref[...], rlow_ref[0:lrows, :]) + dot_tn(mixs_ref[...], rlow_ref[lrows:, :])
    dwo_ref[...] = grad.astype(BF16).reshape(dwo_ref.shape)
    gl_ref[0:HALO, :] = jnp.zeros((HALO, width), BF16)
    last = row_iota((TILE, width)) == TILE - 1

    def local(j, states):
        dm = dm_ref[at(j - 1), :]
        ge, slope = gelu_pair(gp_ref[at(j), :])
        dgate = dm * states * slope
        gl_ref[at(j), :] = dgate.astype(BF16)
        ds = dm * ge
        rate = sigmoid(dp_ref[at(j), :])
        decay = jnp.exp(-pc_ref[C8 : C8 + 1, :] * (0.25 + rate))
        a, b = scan_tile(decay, decay * ds, True)
        return a, b, ds, fold(dgate)

    def short_step(i, carry):
        c, bias = carry
        j = tiles - 1 - i
        a, b, ds, part = local(j, st_ref[at(j), :])
        cs = b + a * c
        tot_ref[at(j), :] = ds + jnp.where(last, c, pltpu.roll(cs, TILE - 1, 0))
        return cs[0:1], bias + part

    _, bias = lax.fori_loop(
        0,
        tiles - 1 - ltiles,
        short_step,
        (jnp.zeros((1, width), F32), jnp.zeros((8, width), F32)),
    )
    s_in = sin_ref[0:1, :]

    def long_step(i, carry):
        c, reach, bias = carry
        j = ltiles - i
        a, b, ds, part = local(j, st_ref[at(j), :] + pr_ref[at(j), :] * s_in)
        cs = b + a * c
        rs = a * reach
        tot_ref[at(j), :] = ds + jnp.where(last, c, pltpu.roll(cs, TILE - 1, 0))
        rch_ref[at(j), :] = jnp.where(last, reach, pltpu.roll(rs, TILE - 1, 0))
        return cs[0:1], rs[0:1], bias + part

    c, reach, bias = lax.fori_loop(
        0, ltiles, long_step, (jnp.zeros((1, width), F32), jnp.ones((1, width), F32), bias)
    )
    end_ref[...] = jnp.concatenate([reach, c, jnp.zeros((6, width), F32)], axis=0)
    bias_ref[...] = bias


def last_kernel(
    ltiles, tiles, first_ref, x_ref, gain_ref, nm_ref, dres_ref, wg_ref, wi_ref, wd_ref, wo_ref,
    pc_ref, in_ref, dp_ref, ip_ref, st_ref, pr_ref, sin_ref, tot_ref, rch_ref, cin_ref, gl_ref,
    dx_ref, halo_ref, gain_grad_ref, dwg_ref, dwi_ref, gd_ref, go_ref, small_ref,
    acc, dc_ref, cl_ref, dl_ref, ol_ref, il_ref,
):
    width = in_ref.shape[1]
    step = pl.program_id(0)
    zero8 = jnp.zeros((8, width), F32)
    cl_ref[0:HALO, :] = jnp.zeros((HALO, width), BF16)
    dl_ref[0:HALO, :] = jnp.zeros((HALO, width), BF16)
    ol_ref[0:HALO, :] = jnp.zeros((HALO, width), BF16)
    dc_ref[0:HALO, :] = jnp.zeros((HALO, width), F32)

    def gate_step(j, states, total, live, carry):
        before, sum_d, sum_o, sum_p = carry
        rows = row_iota((TILE, width))
        prior = jnp.where(rows == 0, before, pltpu.roll(states, 1, 0))
        conv, _ = conv_tile(in_ref, pc_ref, j, live)
        rate, opening, decay, square = gates(
            dp_ref[at(j), :], ip_ref[at(j), :], pc_ref[C8 : C8 + 1, :]
        )
        inv = lax.rsqrt(square)
        mult = square * inv
        weighted = total * opening
        d_open = total * mult * conv
        d_log = decay * (total * prior - (weighted * conv) * (decay * inv))
        d_rate = -pc_ref[C8 : C8 + 1, :] * d_log
        d_dp = d_rate * (rate - rate * rate)
        d_ip = d_open * (opening - opening * opening)
        cl_ref[at(j), :] = conv.astype(BF16)
        dl_ref[at(j), :] = d_dp.astype(BF16)
        ol_ref[at(j), :] = d_ip.astype(BF16)
        dc_ref[at(j), :] = weighted * mult
        return (
            states[TILE - 1 : TILE],
            sum_d + fold(d_dp),
            sum_o + fold(d_ip),
            sum_p - fold((0.25 + rate) * d_log),
        )

    s_in = sin_ref[0:1, :]
    c_in = cin_ref[0:1, :]

    def long_step(i, carry):
        j = 1 + i
        states = st_ref[at(j), :] + pr_ref[at(j), :] * s_in
        total = tot_ref[at(j), :] + rch_ref[at(j), :] * c_in
        return gate_step(j, states, total, 1.0, carry)

    def short_step(i, carry):
        j = 1 + ltiles + i
        return gate_step(j, st_ref[at(j), :], tot_ref[at(j), :], jnp.where(i == 0, 0.0, 1.0), carry)

    carry = lax.fori_loop(0, ltiles, long_step, (s_in, zero8, zero8, zero8))
    carry = lax.fori_loop(
        0, tiles - 1 - ltiles, short_step, (jnp.zeros((1, width), F32),) + carry[1:]
    )
    _, sum_d, sum_o, sum_p = carry

    low, dlow, olow = cl_ref[...], dl_ref[...], ol_ref[...]
    gd_ref[0] = dot_tn(low, dlow)
    go_ref[0] = dot_tn(low, olow)
    dc_ref[...] += dot_nt(dlow, wd_ref[0]) + dot_nt(olow, wo_ref[0])

    def conv_step(j, carry):
        sum_c, sum_i, sums = carry
        live = jnp.where(j == 1 + ltiles, 0.0, 1.0)
        cur = dc_ref[at(j), :]
        up = jnp.where((j == ltiles) | (j == tiles - 1), 0.0, 1.0)
        later = dc_ref[at(jnp.minimum(j + 1, tiles - 1)), :] * up
        _, moved = conv_tile(in_ref, pc_ref, jnp.maximum(j, 1), live)
        d_in = pc_ref[CW : CW + 1, :] * cur
        for k in range(1, 4):
            d_in = d_in + pc_ref[CW + k : CW + k + 1, :] * shift_up(cur, later, k)
        d_in = d_in * jnp.where(j == 0, first_ref[0, 0], 1.0)
        il_ref[at(j), :] = d_in.astype(BF16)
        return (
            sum_c + fold(cur),
            sum_i + fold(d_in),
            tuple(s + fold(cur * m) for s, m in zip(sums, moved)),
        )

    sum_c, sum_i, sums = lax.fori_loop(0, tiles, conv_step, (zero8, zero8, (zero8,) * 4))
    parts = [sum_i, *sums, sum_c, sum_d, sum_o, sum_p * pc_ref[S8 : S8 + 1, :]]
    rows = [jnp.sum(p, axis=0, keepdims=True) for p in parts]
    small_ref[...] = jnp.concatenate(rows + [jnp.zeros((16 - len(rows), width), F32)], axis=0)

    nm = nm_ref[...]
    dwi_ref[...] = dot_tn(il_ref[...], nm).astype(BF16).reshape(dwi_ref.shape)
    dwg_ref[...] = dot_tn(gl_ref[...], nm).astype(BF16).reshape(dwg_ref.shape)
    part = dot_nn(gl_ref[...], flat(wg_ref[...])) + dot_nn(il_ref[...], flat(wi_ref[...]))

    @pl.when(step == 0)
    def _():
        acc[...] = part

    @pl.when(step > 0)
    def _():
        acc[...] += part

    @pl.when(step == pl.num_programs(0) - 1)
    def _():
        def norm_back(j):
            v = x_ref[at(j), :].astype(F32)
            dn = acc[at(j), :]
            s = lax.rsqrt(jnp.mean(v * v, axis=1, keepdims=True) + EPSILON)
            e = dn * gain_ref[...]
            inner = jnp.mean(e * v, axis=1, keepdims=True)
            return s * e - v * (s * s * s * inner), fold(dn * (v * s))

        halo, total = norm_back(0)
        halo_ref[...] = halo

        def one(i, total):
            d, part = norm_back(1 + i)
            dx_ref[at(i), :] = dres_ref[at(i), :] + d
            return total + part

        gain_grad_ref[...] = lax.fori_loop(0, tiles - 1, one, total)


def shape_of(shape, dtype):
    return jax.ShapeDtypeStruct(shape, dtype)


def whole(shape):
    return pl.BlockSpec(shape, lambda g: (0,) * len(shape), pipeline_mode=pl.Buffered(1))


def kept(shape):
    return pl.BlockSpec(shape, lambda g: (0,) * len(shape))


def columns(rows, width):
    return pl.BlockSpec((rows, width), lambda g: (0, g))


def params(limit):
    return pltpu.CompilerParams(
        dimension_semantics=("arbitrary",), vmem_limit_bytes=int(limit * MIB)
    )


def pair_blocks(weight):
    blocks, width, _ = weight.shape
    pairs = weight.reshape(blocks // 2, 2, width, width)
    zero = jnp.zeros_like(pairs[:, 0])
    top = jnp.concatenate([pairs[:, 0], zero], axis=2)
    low = jnp.concatenate([zero, pairs[:, 1]], axis=2)
    return jnp.concatenate([top, low], axis=1)


def unpair(grads):
    width = grads.shape[1] // 2
    both = jnp.stack([grads[:, :width, :width], grads[:, width:, width:]], axis=1)
    return both.reshape(-1, width, width)


def to_slots(parts, count):
    rows = parts[0].shape[0]
    depth = parts[0].shape[1]
    got = lax.all_gather(jnp.concatenate(parts, axis=0), ("seq", "row"), axis=0, tiled=False)
    if count != SLOTS:
        got = got.reshape(count, len(parts), rows, depth).transpose(1, 0, 2, 3)
        got = got.reshape(len(parts), SLOTS, rows * count // SLOTS, depth).transpose(1, 0, 2, 3)
    return got.reshape(SLOTS, -1, depth)


def scatter_slots(grads, number, count):
    slots, rows, depth = grads.shape
    if count != SLOTS:
        grads = grads.reshape(slots, number, rows // number, depth).transpose(1, 0, 2, 3)
        grads = grads.reshape(number, count, -1, depth).transpose(1, 0, 2, 3)
    flat_grads = grads.reshape(slots * rows, depth)
    own = lax.psum_scatter(flat_grads, ("seq", "row"), scatter_dimension=0, tiled=True)
    own = own.astype(F32).reshape(number, -1, depth)
    return [own[i] for i in range(number)]


def entering(ends, reverse):
    count = lax.axis_size("seq")
    place = lax.axis_index("seq")
    got = lax.all_gather(ends, "seq")
    state = jnp.zeros_like(ends[0])
    for hop in range(count - 1):
        source = count - 1 - hop if reverse else hop
        ahead = source > place if reverse else source < place
        state = jnp.where(ahead, got[source, 0] * state + got[source, 1], state)
    return jnp.broadcast_to(state[None], (8, state.shape[0]))


def hop(value, axis, steps):
    count = lax.axis_size(axis)
    first, last = (max(0, -steps), min(count, count - steps))
    return lax.ppermute(value, axis, [(source, source + steps) for source in range(first, last)])


def shards(
    long_tokens,
    short_tokens,
    long_length,
    long_cotangent,
    short_cotangent,
    first_gain,
    gate_weight,
    gate_bias,
    input_weight,
    input_bias,
    conv_weight,
    conv_bias,
    decay_gate_weight,
    decay_gate_bias,
    input_gate_weight,
    input_gate_bias,
    decay_param,
    out_weight,
    second_gain,
    mlp_gate_weight,
    mlp_up_weight,
    mlp_down_weight,
):
    count = lax.axis_size("seq") * lax.axis_size("row")
    lrows, srows, depth = long_tokens.shape[1], short_tokens.shape[1], long_tokens.shape[2]
    chans = gate_bias.shape[0]
    units = mlp_gate_weight.shape[1] * count
    tokens = lrows + srows
    total = HALO + tokens
    ltiles, tiles = lrows // TILE, total // TILE
    cshare, ushare = chans // SLOTS, units // SLOTS
    groups = 4
    width = chans // groups
    per = SLOTS // groups

    long_x = long_tokens.reshape(lrows, depth)
    halo_x = hop(long_x[lrows - HALO :], "seq", 1)
    mixw = to_slots([gate_weight.T, input_weight.T, out_weight], count)
    mlpw = to_slots([mlp_gate_weight.T, mlp_up_weight.T, mlp_down_weight], count)
    x = jnp.concatenate([halo_x, long_x, short_tokens.reshape(srows, depth)], axis=0)
    place = lax.axis_index("seq")
    first = jnp.where(place > 0, 1.0, 0.0).astype(F32).reshape(1, 1)
    positions = place * lrows + jnp.arange(lrows, dtype=jnp.int32)
    keep = positions[:, None] < long_length[0]
    masked = jnp.where(keep, long_cotangent.reshape(lrows, depth), jnp.zeros((), BF16))
    cot = jnp.concatenate([masked, short_cotangent.reshape(srows, depth)], axis=0)
    chan = jnp.concatenate(
        [
            jnp.stack([gate_bias, input_bias]),
            conv_weight,
            jnp.stack(
                [
                    conv_bias,
                    decay_gate_bias,
                    input_gate_bias,
                    8.0 * jax.nn.softplus(decay_param),
                    8.0 * jax.nn.sigmoid(decay_param),
                ]
            ),
            jnp.zeros((5, chans), F32),
        ],
        axis=0,
    )
    pair_d = pair_blocks(decay_gate_weight)
    pair_o = pair_blocks(input_gate_weight)
    gain1 = first_gain[None]
    gain2 = second_gain[None]
    scalar = pl.BlockSpec(memory_space=pltpu.SMEM)

    def mix_part(which):
        return pl.BlockSpec((per, cshare, depth), lambda g: (g, which, 0))

    pair_spec = pl.BlockSpec((1, width, width), lambda g: (g, 0, 0))
    col = columns(total, width)
    col_long = columns(HALO + lrows, width)
    pc_spec = columns(16, width)
    col8 = columns(8, width)

    wide = shape_of((total, chans), F32)
    narrow = shape_of((HALO + lrows, chans), F32)
    gp, inner, dp, ip, states, reach, mix_s, ends, normed = pl.pallas_call(
        functools.partial(front_kernel, ltiles, tiles),
        grid=(groups,),
        in_specs=[
            scalar, whole((total, depth)), whole((1, depth)), mix_part(0), mix_part(1),
            pair_spec, pair_spec, pc_spec,
        ],
        out_specs=[
            col, col, col, col, col, col_long, columns(srows, width), col8,
            kept((total, depth)),
        ],
        out_shape=[
            wide, wide, wide, wide, wide, narrow, shape_of((srows, chans), BF16),
            shape_of((8, chans), F32), shape_of((total, depth), BF16),
        ],
        scratch_shapes=[pltpu.VMEM((total, width), F32), pltpu.VMEM((total, width), BF16)],
        compiler_params=params(48),
        name="front",
    )(first, x, gain1, mixw, mixw, pair_d, pair_o, chan)

    s_in = entering(ends[0:2], False)

    steps = 4
    hid = units // steps
    slots = SLOTS // steps
    share = 3 * ushare
    out, d_res, rlow, mix_l, gain2_grad, dmlp = pl.pallas_call(
        functools.partial(mlp_kernel, ltiles, tokens // TILE),
        grid=(steps,),
        in_specs=[
            whole((total, depth)), whole((tokens, depth)), whole((HALO + lrows, chans)),
            whole((HALO + lrows, chans)), whole((HALO + lrows, chans)), whole((8, chans)),
            whole((srows, chans)),
            pl.BlockSpec((SLOTS, cshare, depth), lambda g: (0, 2, 0), pipeline_mode=pl.Buffered(1)),
            whole((1, depth)),
            pl.BlockSpec((slots, share, depth), lambda g: (g, 0, 0)),
        ],
        out_specs=[
            whole((tokens, depth)), whole((tokens, depth)), whole((tokens, depth)),
            whole((lrows, chans)), whole((8, depth)),
            pl.BlockSpec((slots, share, depth), lambda g: (g, 0, 0)),
        ],
        out_shape=[
            shape_of((tokens, depth), BF16), shape_of((tokens, depth), F32),
            shape_of((tokens, depth), BF16), shape_of((lrows, chans), BF16),
            shape_of((8, depth), F32), shape_of((SLOTS, share, depth), BF16),
        ],
        scratch_shapes=[
            pltpu.VMEM((tokens, depth), BF16), pltpu.VMEM((tokens, depth), F32),
            pltpu.VMEM((tokens, depth), F32), pltpu.VMEM((tokens, hid), F32),
            pltpu.VMEM((tokens, hid), F32), pltpu.VMEM((tokens, hid), F32),
            pltpu.VMEM((tokens, hid), BF16), pltpu.VMEM((tokens, hid), BF16),
            pltpu.VMEM((tokens, hid), BF16),
        ],
        compiler_params=params(60),
        name="mlp",
    )(x, cot, states, reach, gp, s_in, mix_s, mixw, gain2, mlpw)

    slot_spec = pl.BlockSpec((per, cshare, depth), lambda g: (g, 0, 0))
    slot_shape = shape_of((SLOTS, cshare, depth), BF16)
    d_out, gate_low, total_grad, back_reach, back_ends, gate_bias_part = pl.pallas_call(
        functools.partial(back_kernel, ltiles, tiles),
        grid=(groups,),
        in_specs=[
            whole((tokens, depth)), mix_part(2), columns(lrows, width), columns(srows, width),
            col, col, col_long, col8, col, pc_spec,
        ],
        out_specs=[slot_spec, col, col, col_long, col8, col8],
        out_shape=[
            slot_shape, shape_of((total, chans), BF16), wide, narrow,
            shape_of((8, chans), F32), shape_of((8, chans), F32),
        ],
        scratch_shapes=[pltpu.VMEM((tokens, width), F32)],
        compiler_params=params(48),
        name="back",
    )(rlow, mixw, mix_l, mix_s, gp, states, reach, s_in, dp, chan)

    c_in = entering(back_ends[0:2], True)

    grad_pair = shape_of((groups, width, width), F32)
    d_x, d_halo, gain1_grad, d_gate, d_input, d_decay, d_open, small = pl.pallas_call(
        functools.partial(last_kernel, ltiles, tiles),
        grid=(groups,),
        in_specs=[
            scalar, whole((total, depth)), whole((1, depth)), whole((total, depth)),
            whole((tokens, depth)), mix_part(0), mix_part(1), pair_spec, pair_spec, pc_spec,
            col, col, col, col, col_long, col8, col, col_long, col8, col,
        ],
        out_specs=[
            whole((tokens, depth)), whole((HALO, depth)), whole((8, depth)), slot_spec, slot_spec,
            pair_spec, pair_spec, pc_spec,
        ],
        out_shape=[
            shape_of((tokens, depth), F32), shape_of((HALO, depth), F32), shape_of((8, depth), F32),
            slot_shape, slot_shape, grad_pair, grad_pair, shape_of((16, chans), F32),
        ],
        scratch_shapes=[
            pltpu.VMEM((total, depth), F32), pltpu.VMEM((total, width), F32),
            pltpu.VMEM((total, width), BF16), pltpu.VMEM((total, width), BF16),
            pltpu.VMEM((total, width), BF16), pltpu.VMEM((total, width), BF16),
        ],
        compiler_params=params(60),
        name="last",
    )(
        first, x, gain1, normed, d_res, mixw, mixw, pair_d, pair_o, chan,
        inner, dp, ip, states, reach, s_in, total_grad, back_reach, c_in, gate_low,
    )

    late = hop(d_halo, "seq", -1)
    long_grad = d_x[:lrows].at[lrows - HALO :].add(late)
    short_grad = d_x[lrows:]

    g_mgate, g_mup, g_down = scatter_slots(dmlp, 3, count)
    dmix = jnp.concatenate([d_gate, d_input, d_out], axis=1)
    g_gate, g_input, g_out = scatter_slots(dmix, 3, count)
    sums = lax.psum(
        (
            jnp.sum(gain1_grad, axis=0),
            jnp.sum(gain2_grad, axis=0),
            jnp.sum(gate_bias_part, axis=0),
            small[0:9],
            unpair(d_decay),
            unpair(d_open),
        ),
        ("seq", "row"),
    )
    gain1_sum, gain2_sum, gate_bias_sum, rows, decay_sum, open_sum = sums
    return (
        out[:lrows].reshape(long_tokens.shape),
        out[lrows:].reshape(short_tokens.shape),
        long_grad.reshape(long_tokens.shape),
        short_grad.reshape(short_tokens.shape),
        gain1_sum,
        g_gate.T,
        gate_bias_sum,
        g_input.T,
        rows[0],
        rows[1:5],
        rows[5],
        decay_sum,
        rows[6],
        open_sum,
        rows[7],
        rows[8],
        g_out,
        gain2_sum,
        g_mgate.T,
        g_mup.T,
        g_down,
    )


def solution(mesh):
    both = ("seq", "row")
    long_spec = P("row", "seq", None)
    short_spec = P(both, None, None)
    cols = P(None, both)
    rows = P(both, None)
    return jax.shard_map(
        shards,
        mesh=mesh,
        in_specs=(
            long_spec, short_spec, P("row"), long_spec, short_spec, P(), cols, P(), cols, P(),
            P(), P(), P(), P(), P(), P(), P(), rows, P(), cols, cols, rows,
        ),
        out_specs=(
            long_spec, short_spec, long_spec, short_spec, P(), cols, P(), cols, P(), P(), P(),
            P(), P(), P(), P(), P(), rows, P(), cols, cols, rows,
        ),
        check_vma=False,
    )
```

time: 1830 us -> 1020 us (0.56)
  local copies, waits for them, and re-layouts: 662 us -> 32.5 us
  other arithmetic: 211 us -> 20.5 us
  Pallas kernels: 0 us -> 176 us
  matrix products: 157 us -> 0 us
  waiting for transfers between devices: 685 us -> 749 us
  starting transfers between devices: 33.9 us -> 3.88 us
  blocking collectives: 40.4 us -> 18.9 us
    slice x207 -> x5, local copies, waits for them, and re-layouts: 372 us -> 6.37 us  [the longest x2 3.29 us: scatter_slots(): return [own[i] for i in range(number)]]
    reduce_scatter x6 -> x2, waiting for transfers between devices: 48.1 us -> 349 us  [scatter_slots(): lax.psum_scatter(flat_grads, ('seq', 'row'), scatter_dimension=0, tiled=T...]
    all_to_all x6 -> x0, waiting for transfers between devices: 299 us -> none  [the longest x1 160 us: shards(): lax.all_to_all(split_columns(mup_low, seq_count, row_count), 'row', split...]
    pallas_call x0 -> x4, Pallas kernels: none -> 176 us  [the longest x1 74.3 us: shards(): pl.pallas_call(functools.partial(mlp_kernel, ltiles, tokens // TILE), gri...]
    dot_general x20 -> x0, matrix products: 136 us -> none  [the longest x6 55.2 us: back_prod(): lax.dot_general(grads, weight, (((1,), (1,)), ((), ())), preferred_elemen...]
    all_gather x10 -> x2, waiting for transfers between devices: 55.8 us -> 159 us  [to_slots(): lax.all_gather(jnp.concatenate(parts, axis=0), ('seq', 'row'), axis=0, ti...]
    add x93 -> x0, other arithmetic: 77.1 us -> none  [the longest x37 28.5 us: linear_pair(): return (earlier[0] * later[0], earlier[1] * later[0] + later[1])]
    pad x80 -> x0, local copies, waits for them, and re-layouts: 60.7 us -> none  [the longest x16 26.8 us: shards(): lax.associative_scan(linear_pair, (decay_short, drive_short), axis=1)]
  transfers between devices with their start and end apart: 26 -> 8, of which waited for: 10 -> 6; matrix products, arithmetic and copies ran while one was open for 56% -> 3% of each run, Pallas kernels for 0% -> 3%
where the time goes in v1:
time: 1020 us
  waiting for transfers between devices  749 us (73%)
  Pallas kernels  176 us (17%)
  local copies, waits for them, and re-layouts  32.5 us (3%)
  other arithmetic  20.5 us (2%)
  blocking collectives  18.9 us (2%)
  between operations  15.3 us (2%)
    reduce_scatter x2, waiting for transfers between devices, scatter_slots(): lax.psum_scatter(flat_grads, ('seq', 'row'), scatter_dimension=0, tiled=T...  349 us
    psum x2, waiting for transfers between devices, shards(): lax.psum((jnp.sum(gain1_grad, axis=0), jnp.sum(gain2_grad, axis=0), jnp.s...  240 us
    all_gather x2, waiting for transfers between devices, to_slots(): lax.all_gather(jnp.concatenate(parts, axis=0), ('seq', 'row'), axis=0, ti...  159 us
    pallas_call x1, Pallas kernels, shards(): pl.pallas_call(functools.partial(mlp_kernel, ltiles, tokens // TILE), gri...  74.3 us
    pallas_call x1, Pallas kernels, shards(): pl.pallas_call(functools.partial(last_kernel, ltiles, tiles), grid=(group...  50.1 us
    pallas_call x1, Pallas kernels, shards(): pl.pallas_call(functools.partial(front_kernel, ltiles, tiles), grid=(grou...  31.6 us
  transfers between devices with their start and end apart: 8, of which 6 were waited for; matrix products, arithmetic and copies ran while one was open for 3% of the time, Pallas kernels for 3%

profile of v1, /device:TPU:0, one launch (start us, length us, event | category | flops | bytes accessed | tf_op | source)
XLA Modules:
  0.0 1015.9 jit_solution(14824952315598341103)
XLA Ops:
  7.3 1.8 pad_maximum_fusion.6
  9.2 2.0 pad_maximum_fusion.5
  11.3 2.4 collective-permute-start
  14.6 1.5 fusion.4
  17.7 1.4 pad_maximum_fusion.3.x_ref
  19.1 77.2 %all-gather.9.cloned.1.call-done = bf16[4608,1024]{1,0:T(8,128)(2,1)} async-done(((bf16[144,1024]{1,0:T(8,128)(2,1)}), bf16[4608,1024]{1,0:T(8,128)(2,1)}) %all-gather.9.cloned.1.call-update) | async-done | bytes 9437200 | tf_op jit(solution)/shard_map/all_gather | solution.py:477
  96.2 1.3 copy-done.2
  97.5 31.6 %front.1 = (f32[656,1536]{1,0:T(8,128)}, f32[656,1536]{1,0:T(8,128)}, f32[656,1536]{1,0:T(8,128)}, f32[656,1536]{1,0:T(8,128)}, f32[656,1536]{1,0:T(8,128)}, /*i...) custom-call(f32[1,1]{1,0:T(1,128)} %bitcast.6.first_ref, ...), custom_call_target="tpu_custom_call" | custom-call | tf_op jit(solution)/shard_map/front/pallas_call | solution.py:594
  131.2 9.5 all-gather.4
  140.9 81.8 %all-gather.11.cloned.1.call-done = bf16[9216,1024]{1,0:T(8,128)(2,1)} async-done(((bf16[288,1024]{1,0:T(8,128)(2,1)}), bf16[9216,1024]{1,0:T(8,128)(2,1)}) %all-gather.11.cloned.1.call-update) | async-done | bytes 18874384 | tf_op jit(solution)/shard_map/all_gather | solution.py:477
  223.4 74.3 %mlp.1 = (bf16[640,1024]{1,0:T(8,128)(2,1)}, f32[640,1024]{1,0:T(8,128)}, bf16[640,1024]{1,0:T(8,128)(2,1)}, bf16[128,1536]{1,0:T(8,128)(2,1)}, f32[8,1024]{1,0:T(8,128)}, /*index=5*/bf16[32,288,1024]{2,1,0:T(8,128)(2,1)}) custom-call(bf16[656,1024]{1,0:T(8,128)(2,1)} %copy-done, bf16[640,1024]{1,0:T(8,128)(2,1)} %pad_maximum_fusion.4.cot_ref, ...), custom_call_target="tpu_custom_call" | custom-call | tf_op jit(solution)/shard_map/mlp/pallas_call | solution.py:620
  297.7 1.3 copy-done.8
  300.0 19.9 %back.1 = (bf16[32,48,1024]{2,1,0:T(8,128)(2,1)}, bf16[656,1536]{1,0:T(8,128)(2,1)}, f32[656,1536]{1,0:T(8,128)}, f32[144,1536]{1,0:T(8,128)S(1)}, f32[8,1536]{1,0:T(8,128)S(1)}, /*index=5*/f32[8,1536]{1,0:T(8,128)S(1)}) custom-call(bf16[640,1024]{1,0:T(8,128)(2,1)S(1)} %copy-done.8, bf16[32,144,1024]{2,1,0:T(8,128)(2,1)} %bitcast.76, ...), custom_call_target="tpu_custom_call" | custom-call | tf_op jit(solution)/shard_map/back/pallas_call | solution.py:654
  320.8 9.4 all-gather.5
  331.1 50.1 %last.1 = (f32[640,1024]{1,0:T(8,128)}, f32[16,1024]{1,0:T(8,128)}, f32[8,1024]{1,0:T(8,128)}, bf16[32,48,1024]{2,1,0:T(8,128)(2,1)}, bf16[32,48,1024]{2,1,0:T(8...) custom-call(f32[1,1]{1,0:T(1,128)} %bitcast.6.first_ref, ...), custom_call_target="tpu_custom_call" | custom-call | tf_op jit(solution)/shard_map/last/pallas_call | solution.py:674
  381.1 1.4 reduce_sum.27
  383.8 7.0 pad_maximum_fusion
  393.0 1.3 copy.54
  395.6 1.3 copy.53
  399.4 1.7 slice_bitcast_fusion.13
  401.1 1.3 collective-permute-start.1
  402.4 1.5 slice_bitcast_fusion
  403.8 100.3 %all-reduce.9.cloned.1.call-done = (f32[1024]{0:T(1024)}, f32[1536]{0:T(1024)}, f32[9,1536]{1,0:T(8,128)}, f32[1024]{0:T(1024)}) async-done(((f32[1024]{0:T(1024)}, f32[1536]{0:T(1024)}, f32[9,1536]{1,0:T(8,128)}, f32[1024]{0:T(1024)}), (f32[1024]{0:T(1024)}, f32[1536]{0:T(1024)}, f32[9,1536]{1,0:T(8,128)}, f32[1024]{0:T(1024)})) %all-reduce.9.cloned.1.call-update) | async-done | bytes 69648 | tf_op jit(solution)/shard_map/psum | solution.py:709
  504.1 1.4 slice.290
  505.5 1.7 slice_reduce_fusion
  507.2 139.0 %reduce-scatter.3.cloned.1.call-done = bf16[144,1024]{1,0:T(8,128)(2,1)} async-done(((bf16[4608,1024]{1,0:T(8,128)(2,1)}), bf16[144,1024]{1,0:T(8,128)(2,1)}) %reduce-scatter.3.cloned.1.call-update) | async-done | bytes 294928 | tf_op jit(solution)/shard_map/reduce_scatter | solution.py:490
  647.2 1.6 slice.295
  649.6 210.0 %reduce-scatter.5.cloned.1.call-done = bf16[288,1024]{1,0:T(8,128)(2,1)} async-done(((bf16[9216,1024]{1,0:T(8,128)(2,1)}), bf16[288,1024]{1,0:T(8,128)(2,1)}) %reduce-scatter.5.cloned.1.call-update) | async-done | bytes 589840 | tf_op jit(solution)/shard_map/reduce_scatter | solution.py:490
  859.6 1.2 convert_element_type.7
  860.7 1.7 slice.298
  863.4 140.1 %all-reduce.11.cloned.1.call-done = (f32[8,192,192]{2,1,0:T(8,128)}, f32[8,192,192]{2,1,0:T(8,128)}) async-done(((f32[8,192,192]{2,1,0:T(8,128)}, f32[8,192,192]{2,1,0:T(8,128)}), (f32[8,192,192]{2,1,0:T(8,128)}, f32[8,192,192]{2,1,0:T(8,128)})) %all-reduce.11.cloned.1.call-update) | async-done | bytes 2359312 | tf_op jit(solution)/shard_map/psum | solution.py:709
  1004.7 2.7 copy.69
  (126 shorter events, 20.2 us)
Async XLA Ops:
  7.2 4.1 copy-start.23
  7.2 7.1 copy-start.27
  7.2 7.2 copy-start.24
  7.2 7.3 copy-start.20
  7.2 89.0 %all-gather.9.cloned.1.call-start = ((), (), s32[]{:S(2)}) async-start(), calls=%async_computation.4 | async-start | bytes 9732096 | tf_op jit(solution)/shard_map/all_gather | solution.py:477
  9.1 5.5 copy-start.21
  9.1 213.6 %all-gather.11.cloned.1.call-start = ((), (), s32[]{:S(2)}) async-start(), calls=%async_computation.5 | async-start | bytes 19464192 | tf_op jit(solution)/shard_map/all_gather | solution.py:477
  11.2 492.9 %all-reduce.9.cloned.1.call-start = ((), (), s32[]{:S(2)}) async-start(), calls=%async_computation.6 | async-start | bytes 229376 | tf_op jit(solution)/shard_map/psum | solution.py:709
  11.3 6.4 collective-permute-start
  14.6 1.6 copy-start.19
  16.2 80.0 %copy-start.1 = (bf16[4,384,384]{2,1,0:T(8,128)(2,1)}, bf16[4,384,384]{2,1,0:T(8,128)(2,1)S(1)}, u32[]{:S(2)}) copy-start(bf16[4,384,384]{2,1,0:T(8,128)(2,1)S(1)} %get-tuple-element.142.wd_ref) | copy-start | bytes 3538948
  17.4 78.8 %copy-start.12 = (f32[1024]{0:T(1024)S(1)}, f32[1024]{0:T(1024)}, u32[]{:S(2)}) copy-start(f32[1024]{0:T(1024)} %param.29) | copy-start | bytes 12292
  17.7 280.0 %copy-start.6 = (f32[16,1536]{1,0:T(8,128)}, f32[16,1536]{1,0:T(8,128)S(1)}, u32[]{:S(2)}) copy-start(f32[16,1536]{1,0:T(8,128)S(1)} %concatenate.47.pc_ref) | copy-start | bytes 294916
  19.0 110.1 %copy-start = (bf16[656,1024]{1,0:T(8,128)(2,1)}, bf16[656,1024]{1,0:T(8,128)(2,1)S(1)}, u32[]{:S(2)}) copy-start(bf16[656,1024]{1,0:T(8,128)(2,1)S(1)} %pad_maximum_fusion.3.x_ref) | copy-start | bytes 4030468
  223.4 74.3 %copy-start.4 = (f32[144,1536]{1,0:T(8,128)S(1)}, f32[144,1536]{1,0:T(8,128)}, u32[]{:S(2)}) copy-start(f32[144,1536]{1,0:T(8,128)} %copy-done.3) | copy-start | bytes 2654212
  223.4 74.3 %copy-start.5 = (bf16[512,1536]{1,0:T(8,128)(2,1)S(1)}, bf16[512,1536]{1,0:T(8,128)(2,1)}, u32[]{:S(2)}) copy-start(bf16[512,1536]{1,0:T(8,128)(2,1)} %get-tuple-element.66.mixs_ref) | copy-start | bytes 4718596
  223.4 74.3 %copy-start.10 = (f32[8,1536]{1,0:T(8,128)S(1)}, f32[8,1536]{1,0:T(8,128)}, u32[]{:S(2)}) copy-start(f32[8,1536]{1,0:T(8,128)} %broadcast_in_dim.38.sin_ref) | copy-start | bytes 147460
  331.1 52.0 %copy-start.25 = (f32[8,1024]{1,0:T(8,128)S(1)}, f32[8,1024]{1,0:T(8,128)}, u32[]{:S(2)}) copy-start(f32[8,1024]{1,0:T(8,128)} %get-tuple-element.89) | copy-start | bytes 98308
  331.1 52.7 %copy-start.13 = (bf16[32,48,1024]{2,1,0:T(8,128)(2,1)S(1)}, bf16[32,48,1024]{2,1,0:T(8,128)(2,1)}, u32[]{:S(2)}) copy-start(bf16[32,48,1024]{2,1,0:T(8,128)(2,1)} %get-tuple-element.84) | copy-start | bytes 9437188
  383.7 262.5 %reduce-scatter.3.cloned.1.call-start = ((), (), s32[]{:S(2)}) async-start(), calls=%async_computation.2 | async-start | bytes 9732096 | tf_op jit(solution)/shard_map/reduce_scatter | solution.py:490
  390.9 468.7 %reduce-scatter.5.cloned.1.call-start = ((), (), s32[]{:S(2)}) async-start(), calls=%async_computation.3 | async-start | bytes 19464192 | tf_op jit(solution)/shard_map/reduce_scatter | solution.py:490
  390.9 1.7 copy-start.18
  391.4 612.0 %all-reduce.11.cloned.1.call-start = ((), (), s32[]{:S(2)}) async-start(), calls=%async_computation.7 | async-start | bytes 6291456 | tf_op jit(solution)/shard_map/psum | solution.py:709
  393.0 2.2 copy-start.17
  395.6 2.3 copy-start.14
  395.6 2.7 copy-start.16
  399.4 1.7 copy-start.36
  401.1 106.1 %collective-permute-start.1 = (f32[16,1024]{1,0:T(8,128)S(1)}, f32[16,1024]{1,0:T(8,128)S(1)}, u32[]{:S(2)}, u32[]{:S(2)}) collective-permute-start(f32[16,1024]{1,0:T(8,128)S(1)} %copy-done.36), channel_id=1, source_target_pairs={{4,0},{8,4},{12,8},{16,12},{20,16},{24,20},{28,24},{5,1},{9,5},{13... | collective-permute-start | bytes 196616 | tf_op jit(solution)/shard_map/ppermute | solution.py:510
  507.2 355.3 %copy-start.22 = (f32[1,128,1024]{2,1,0:T(8,128)}, f32[1,128,1024]{2,1,0:T(8,128)S(1)}, u32[]{:S(2)}) copy-start(f32[1,128,1024]{2,1,0:T(8,128)S(1)} %bitcast_dynamic-update-slice_fusion) | copy-start | bytes 1572868
  649.6 353.9 %copy-start.35 = (f32[1024]{0:T(1024)S(1)}, f32[1024]{0:T(1024)}, u32[]{:S(2)}) copy-start(f32[1024]{0:T(1024)} %get-tuple-element.148) | copy-start | bytes 12292
  649.6 354.5 %copy-start.33 = (f32[1536]{0:T(1024)S(1)}, f32[1536]{0:T(1024)}, u32[]{:S(2)}) copy-start(f32[1536]{0:T(1024)} %get-tuple-element.150) | copy-start | bytes 18436
  1003.5 3.9 copy-start.15
  (13 other events, 15.3 us)
Sparse Core Ops, SparseCore 0:
  11.4 84.7 all-gather.8
  99.0 123.6 all-gather.10
  383.9 120.1 all-reduce.8
  509.8 136.3 reduce-scatter.2
  653.6 205.9 reduce-scatter.4
  866.6 136.8 all-reduce.10

commit v2 on v1

--- a/solution.py
+++ b/solution.py
@@ -315,7 +315,7 @@
 def last_kernel(
     ltiles, tiles, first_ref, x_ref, gain_ref, nm_ref, dres_ref, wg_ref, wi_ref, wd_ref, wo_ref,
     pc_ref, in_ref, dp_ref, ip_ref, st_ref, pr_ref, sin_ref, tot_ref, rch_ref, cin_ref, gl_ref,
-    dx_ref, halo_ref, gain_grad_ref, dwg_ref, dwi_ref, gd_ref, go_ref, small_ref,
+    bias_ref, dx_ref, halo_ref, gain_grad_ref, dwg_ref, dwi_ref, gg_ref, small_ref,
     acc, dc_ref, cl_ref, dl_ref, ol_ref, il_ref,
 ):
     width = in_ref.shape[1]
@@ -373,8 +373,11 @@
     _, sum_d, sum_o, sum_p = carry
 
     low, dlow, olow = cl_ref[...], dl_ref[...], ol_ref[...]
-    gd_ref[0] = dot_tn(low, dlow)
-    go_ref[0] = dot_tn(low, olow)
+    half = width // 2
+    for which, grads in ((0, dlow), (1, olow)):
+        product = dot_tn(low, grads).astype(BF16)
+        gg_ref[which, 0] = product[:half, :half]
+        gg_ref[which, 1] = product[half:, half:]
     dc_ref[...] += dot_nt(dlow, wd_ref[0]) + dot_nt(olow, wo_ref[0])
 
     def conv_step(j, carry):
@@ -396,7 +399,7 @@
         )
 
     sum_c, sum_i, sums = lax.fori_loop(0, tiles, conv_step, (zero8, zero8, (zero8,) * 4))
-    parts = [sum_i, *sums, sum_c, sum_d, sum_o, sum_p * pc_ref[S8 : S8 + 1, :]]
+    parts = [sum_i, *sums, sum_c, sum_d, sum_o, sum_p * pc_ref[S8 : S8 + 1, :], bias_ref[...]]
     rows = [jnp.sum(p, axis=0, keepdims=True) for p in parts]
     small_ref[...] = jnp.concatenate(rows + [jnp.zeros((16 - len(rows), width), F32)], axis=0)
 
@@ -465,10 +468,311 @@
     return jnp.concatenate([top, low], axis=1)
 
 
-def unpair(grads):
-    width = grads.shape[1] // 2
-    both = jnp.stack([grads[:, :width, :width], grads[:, width:, width:]], axis=1)
-    return both.reshape(-1, width, width)
+def place_of():
+    s = lax.axis_index("seq")
+    return s // 4, (s // 2) % 2, s % 2, lax.axis_index("row")
+
+
+def device_at(y, x, c, z):
+    return ((y * 2 + x) * 2 + c, z)
+
+
+class Peers:
+    def __init__(self, zcount):
+        y, x, c, z = self.place = place_of()
+        self.far = [(z + k) % zcount for k in range(1, zcount)]
+        self.along = [device_at(y, x, c, q) for q in self.far]
+        self.near = ((y + c) % 2, (x + 1 - c) % 2)
+        self.first = device_at(*self.near, c, z)
+        self.second = device_at((y + 1 - c) % 2, (x + c) % 2, c, z)
+        self.other = device_at(y, x, 1 - c, z)
+
+    def meet(self):
+        everyone = [*self.along, self.first, self.second, self.other]
+        barrier = pltpu.get_barrier_semaphore()
+        for peer in everyone:
+            pl.semaphore_signal(
+                barrier, inc=1, device_id=peer, device_id_type=pl.DeviceIdType.MESH
+            )
+        pl.semaphore_wait(barrier, len(everyone))
+
+
+def remote(source, target, send, recv, device):
+    return pltpu.make_async_remote_copy(
+        src_ref=source,
+        dst_ref=target,
+        send_sem=send,
+        recv_sem=recv,
+        device_id=device,
+        device_id_type=pl.DeviceIdType.MESH,
+    )
+
+
+class Spread:
+    def __init__(self, peers, own, full, send, recv):
+        self.peers, self.own, self.full, self.send, self.recv = peers, own, full, send, recv
+
+    def go(self, stage, act):
+        y, x, c, z = self.peers.place
+        p, full = self.peers, self.full
+        if stage == 0:
+            for k, device in enumerate(p.along):
+                act(remote(self.own, full(y, x, c, z), self.send(k), self.recv(k), device))
+            return
+        k = len(p.along) + stage - 1
+        if stage == 2:
+
+            @pl.when(c == 0)
+            def _():
+                part = full(y, slice(None), c, slice(None))
+                act(remote(part, part, self.send(k), self.recv(k), p.second))
+
+            @pl.when(c == 1)
+            def _():
+                part = full(slice(None), x, c, slice(None))
+                act(remote(part, part, self.send(k), self.recv(k), p.second))
+
+            return
+        if stage == 1:
+            part, device = full(y, x, c, slice(None)), p.first
+        else:
+            part, device = full(slice(None), slice(None), c, slice(None)), p.other
+        act(remote(part, part, self.send(k), self.recv(k), device))
+
+    def start(self, stage):
+        self.go(stage, lambda d: d.start())
+
+    def arrive(self, stage):
+        self.go(stage, lambda d: d.wait_recv())
+
+    def drain(self):
+        for stage in range(4):
+            self.go(stage, lambda d: d.wait_send())
+
+
+def waves(count, lags):
+    for t in range(count + sum(lags) + 1):
+        for stage in range(len(lags), -1, -1):
+            piece = t - sum(lags[:stage])
+            if 0 <= piece < count:
+                yield piece, stage
+
+
+def gather_kernel(zcount, chunks, lags, number, *refs):
+    ins, outs = refs[:number], refs[number : 2 * number]
+    csem, ssem, rsem = refs[2 * number :]
+    peers = Peers(zcount)
+    y, x, c, z = peers.place
+    peers.meet()
+    spreads, copies = [], []
+    for i, (which, start, size) in enumerate(chunks):
+        rows = pl.ds(start, size)
+        own = ins[which].at[rows]
+
+        def full(a, b, d, e, ref=outs[which], rows=rows):
+            return ref.at[a, b, d, e, rows]
+
+        spreads.append(
+            Spread(peers, own, full, lambda k, i=i: ssem.at[i, k], lambda k, i=i: rsem.at[i, k])
+        )
+        copies.append(pltpu.make_async_copy(own, full(y, x, c, z), csem.at[i]))
+    for i, stage in waves(len(chunks), lags):
+        if stage == 0:
+            copies[i].start()
+        elif stage == 1:
+            copies[i].wait()
+        if stage > 0:
+            spreads[i].arrive(stage - 1)
+        if stage < 4:
+            spreads[i].start(stage)
+    for spread in spreads:
+        spread.drain()
+
+
+def gather_call(parts, zcount):
+    size = 16
+    chunks = [
+        (which, start, size)
+        for which, part in enumerate(parts)
+        for start in range(0, part.shape[0], size)
+    ]
+    hbm = pl.BlockSpec(memory_space=pl.ANY)
+    links = pltpu.SemaphoreType.DMA((len(chunks), zcount + 2))
+    return pl.pallas_call(
+        functools.partial(gather_kernel, zcount, chunks, (2, 2, 3, 2), len(parts)),
+        out_shape=[shape_of((2, 2, 2, zcount) + p.shape, p.dtype) for p in parts],
+        in_specs=[hbm] * len(parts),
+        out_specs=[hbm] * len(parts),
+        scratch_shapes=[pltpu.SemaphoreType.DMA((len(chunks),)), links, links],
+        compiler_params=pltpu.CompilerParams(collective_id=0, has_side_effects=True),
+        name="gather",
+    )(*parts)
+
+
+def scatter_kernel(zcount, chunks, lags, nin, nout, *refs):
+    ins, outs = refs[:nin], refs[nin : nin + nout]
+    scratch = refs[nin + nout :]
+    buffers = [scratch[0:5], scratch[5:10], scratch[10:15]]
+    csem, ssem, rsem, ssem2, rsem2 = scratch[15:]
+    peers = Peers(zcount)
+    y, x, c, z = peers.place
+    peers.meet()
+
+    def add(into, i, part, j):
+        into[i] = (into[i].astype(F32) + part[j].astype(F32)).astype(into.dtype)
+
+    class Piece:
+        def __init__(self, i, kind, slot, which, start, rows, target, offset):
+            self.i, self.kind, self.slot = i, kind, slot
+            self.a, self.r0, self.r1, self.r2, self.r3 = buffers[kind]
+            self.source, self.rows = ins[which], pl.ds(start, rows)
+            self.target, self.span = outs[target], pl.ds(offset, rows)
+            self.spread = None
+            if kind > 0:
+
+                def full(*place):
+                    return self.target.at[place]
+
+                self.spread = Spread(
+                    peers, full(y, x, c, z), full, lambda k: ssem2.at[i, k], lambda k: rsem2.at[i, k]
+                )
+
+        def local(self):
+            mine = self.source.at[:, :, c, :, self.rows]
+            return pltpu.make_async_copy(mine, self.a.at[self.slot], csem.at[self.i])
+
+        def send(self, stage, act):
+            s = self.slot
+
+            def go(source, target, k, device):
+                act(remote(source, target, ssem.at[self.i, k], rsem.at[self.i, k], device))
+
+            if stage == 0:
+                theirs = self.source.at[:, :, 1 - c, :, self.rows]
+                go(theirs, self.r0.at[s], 0, peers.other)
+            elif stage == 1:
+
+                @pl.when(c == 0)
+                def _():
+                    go(self.a.at[s, 1 - y], self.r1.at[s], 1, peers.second)
+
+                @pl.when(c == 1)
+                def _():
+                    go(self.a.at[s, :, 1 - x], self.r1.at[s], 1, peers.second)
+
+            elif stage == 2:
+                go(self.a.at[(s, *peers.near)], self.r2.at[s], 2, peers.first)
+            else:
+                for k, device in enumerate(peers.along):
+                    go(self.a.at[s, y, x, peers.far[k]], self.r3.at[s, k], 3 + k, device)
+
+        def step(self, stage):
+            s = self.slot
+            if stage == 0:
+                self.local().start()
+            elif stage <= 4:
+                self.send(stage - 1, lambda d: d.wait_recv())
+            else:
+                self.spread.arrive(stage - 5)
+            if stage == 1:
+                self.local().wait()
+
+                @pl.loop(0, 4 * zcount)
+                def _(q):
+                    i = (s, q // (2 * zcount), (q // zcount) % 2, q % zcount)
+                    add(self.a, i, self.r0, i)
+
+            elif stage == 2:
+
+                @pl.loop(0, 2 * zcount)
+                def _(q):
+                    h = q // zcount
+                    i = (s, y * (1 - c) + h * c, h * (1 - c) + x * c, q % zcount)
+                    add(self.a, i, self.r1, (s, h, q % zcount))
+
+            elif stage == 3:
+
+                @pl.loop(0, zcount)
+                def _(q):
+                    add(self.a, (s, y, x, q), self.r2, (s, q))
+
+            elif stage == 4:
+                total = self.a[s, y, x, z].astype(F32)
+                for k in range(zcount - 1):
+                    total = total + self.r3[s, k].astype(F32)
+                if self.kind == 0:
+                    self.target[self.span] = total
+                else:
+                    self.target[y, x, c, z] = total.astype(self.target.dtype)
+            if stage < 4:
+                self.send(stage, lambda d: d.start())
+            elif stage < 8 and self.kind > 0:
+                self.spread.start(stage - 4)
+
+        def drain(self):
+            for stage in range(4):
+                self.send(stage, lambda d: d.wait_send())
+            if self.spread is not None:
+                self.spread.drain()
+
+    pieces = [Piece(i, *chunk) for i, chunk in enumerate(chunks)]
+    for i, stage in waves(len(pieces), lags):
+        if stage <= 4 or pieces[i].kind > 0:
+            pieces[i].step(stage)
+    for piece in pieces:
+        piece.drain()
+
+
+def scatter_call(mains, gate_grads, sums, zcount):
+    grid = (2, 2, 2, zcount)
+    rows = 48
+    nmain = len(mains)
+    chunks = [
+        (2, 0, nmain + 1, 0, sums.shape[1], None, 0),
+        (1, 0, nmain, 0, gate_grads.shape[1], None, 0),
+    ]
+    outs = []
+    ins = []
+    for which, (array, number) in enumerate(mains):
+        share, depth = array.shape[1] // number, array.shape[2]
+        ins.append(array.reshape(grid + array.shape[1:]))
+        for part in range(number):
+            for start in range(0, share, rows):
+                chunks.append(
+                    (0, len(chunks) - 2, which, part * share + start, rows, len(outs), start)
+                )
+            outs.append(shape_of((share, depth), F32))
+    chunks[0] = chunks[0][:5] + (len(outs) + 1, 0)
+    chunks[1] = chunks[1][:5] + (len(outs), 0)
+    for array in (gate_grads, sums):
+        ins.append(array.reshape(grid + array.shape[1:]))
+        outs.append(shape_of(ins[-1].shape, array.dtype))
+
+    def five(number, shape, dtype):
+        lead = [(2, 2, zcount), (2, 2, zcount), (2, zcount), (zcount,), (zcount - 1,)]
+        return [pltpu.VMEM((number, *d, *shape), dtype) for d in lead]
+
+    n = len(chunks)
+    links = pltpu.SemaphoreType.DMA((n, zcount + 2))
+    return pl.pallas_call(
+        functools.partial(
+            scatter_kernel, zcount, chunks, (2, 2, 2, 2, 1, 1, 1, 1), len(ins), len(outs)
+        ),
+        out_shape=outs,
+        in_specs=[pl.BlockSpec(memory_space=pl.ANY)] * len(ins),
+        out_specs=[pl.BlockSpec(memory_space=pltpu.VMEM)] * len(outs),
+        scratch_shapes=[
+            *five(n - 2, (rows, mains[0][0].shape[2]), BF16),
+            *five(1, gate_grads.shape[1:], BF16),
+            *five(1, sums.shape[1:], F32),
+            pltpu.SemaphoreType.DMA((n,)),
+            links, links, links, links,
+        ],
+        compiler_params=pltpu.CompilerParams(
+            collective_id=1, has_side_effects=True, vmem_limit_bytes=62 * MIB
+        ),
+        name="scatter",
+    )(*ins)
 
 
 def to_slots(parts, count):
@@ -548,8 +852,15 @@
 
     long_x = long_tokens.reshape(lrows, depth)
     halo_x = hop(long_x[lrows - HALO :], "seq", 1)
-    mixw = to_slots([gate_weight.T, input_weight.T, out_weight], count)
-    mlpw = to_slots([mlp_gate_weight.T, mlp_up_weight.T, mlp_down_weight], count)
+    mix_own = [gate_weight.T, input_weight.T, out_weight]
+    mlp_own = [mlp_gate_weight.T, mlp_up_weight.T, mlp_down_weight]
+    zcount = lax.axis_size("row")
+    fast = lax.axis_size("seq") == 8 and count == SLOTS
+    if fast:
+        own = [jnp.concatenate(mix_own, axis=0), jnp.concatenate(mlp_own, axis=0)]
+        mixw, mlpw = [w.reshape(SLOTS, -1, depth) for w in gather_call(own, zcount)]
+    else:
+        mixw, mlpw = to_slots(mix_own, count), to_slots(mlp_own, count)
     x = jnp.concatenate([halo_x, long_x, short_tokens.reshape(srows, depth)], axis=0)
     place = lax.axis_index("seq")
     first = jnp.where(place > 0, 1.0, 0.0).astype(F32).reshape(1, 1)
@@ -670,22 +981,23 @@
 
     c_in = entering(back_ends[0:2], True)
 
-    grad_pair = shape_of((groups, width, width), F32)
-    d_x, d_halo, gain1_grad, d_gate, d_input, d_decay, d_open, small = pl.pallas_call(
+    blocks, bwidth = decay_gate_weight.shape[0:2]
+    d_x, d_halo, gain1_grad, d_gate, d_input, d_gates, small = pl.pallas_call(
         functools.partial(last_kernel, ltiles, tiles),
         grid=(groups,),
         in_specs=[
             scalar, whole((total, depth)), whole((1, depth)), whole((total, depth)),
             whole((tokens, depth)), mix_part(0), mix_part(1), pair_spec, pair_spec, pc_spec,
-            col, col, col, col, col_long, col8, col, col_long, col8, col,
+            col, col, col, col, col_long, col8, col, col_long, col8, col, col8,
         ],
         out_specs=[
             whole((tokens, depth)), whole((HALO, depth)), whole((8, depth)), slot_spec, slot_spec,
-            pair_spec, pair_spec, pc_spec,
+            pl.BlockSpec((2, 2, bwidth, bwidth), lambda g: (0, g, 0, 0)), pc_spec,
         ],
         out_shape=[
             shape_of((tokens, depth), F32), shape_of((HALO, depth), F32), shape_of((8, depth), F32),
-            slot_shape, slot_shape, grad_pair, grad_pair, shape_of((16, chans), F32),
+            slot_shape, slot_shape, shape_of((2, blocks, bwidth, bwidth), BF16),
+            shape_of((16, chans), F32),
         ],
         scratch_shapes=[
             pltpu.VMEM((total, depth), F32), pltpu.VMEM((total, width), F32),
@@ -697,46 +1009,58 @@
     )(
         first, x, gain1, normed, d_res, mixw, mixw, pair_d, pair_o, chan,
         inner, dp, ip, states, reach, s_in, total_grad, back_reach, c_in, gate_low,
+        gate_bias_part,
     )
 
     late = hop(d_halo, "seq", -1)
     long_grad = d_x[:lrows].at[lrows - HALO :].add(late)
     short_grad = d_x[lrows:]
 
-    g_mgate, g_mup, g_down = scatter_slots(dmlp, 3, count)
-    dmix = jnp.concatenate([d_gate, d_input, d_out], axis=1)
-    g_gate, g_input, g_out = scatter_slots(dmix, 3, count)
-    sums = lax.psum(
-        (
-            jnp.sum(gain1_grad, axis=0),
-            jnp.sum(gain2_grad, axis=0),
-            jnp.sum(gate_bias_part, axis=0),
-            small[0:9],
-            unpair(d_decay),
-            unpair(d_open),
-        ),
-        ("seq", "row"),
-    )
-    gain1_sum, gain2_sum, gate_bias_sum, rows, decay_sum, open_sum = sums
+    lanes = 2048
+    gains = jnp.stack([jnp.sum(gain1_grad, axis=0), jnp.sum(gain2_grad, axis=0)])
+    small = jnp.concatenate(
+        [
+            jnp.pad(small[0:10], ((0, 0), (0, lanes - chans))),
+            jnp.pad(gains, ((0, 0), (0, lanes - depth))),
+            jnp.zeros((4, lanes), F32),
+        ],
+        axis=0,
+    )
+    if fast:
+        mains = [(dmlp, 3), (d_gate, 1), (d_input, 1), (d_out, 1)]
+        tiled = small.reshape(2, 8, lanes // 128, 128).transpose(0, 2, 1, 3)
+        *shares, gate_sums, sums = scatter_call(
+            mains, d_gates.reshape(SLOTS, -1, bwidth), tiled.reshape(SLOTS, 8, 128), zcount
+        )
+        g_mgate, g_mup, g_down, g_gate, g_input, g_out = shares
+        gate_sums = gate_sums.reshape(d_gates.shape)
+        sums = sums.reshape(2, lanes // 128, 8, 128).transpose(0, 2, 1, 3).reshape(16, lanes)
+    else:
+        g_mgate, g_mup, g_down = scatter_slots(dmlp, 3, count)
+        dmix = jnp.concatenate([d_gate, d_input, d_out], axis=1)
+        g_gate, g_input, g_out = scatter_slots(dmix, 3, count)
+        gate_sums, sums = lax.psum((d_gates.astype(F32), small), ("seq", "row"))
+    gate_sums = gate_sums.astype(F32)
+    rows = sums[0:10, :chans]
     return (
         out[:lrows].reshape(long_tokens.shape),
         out[lrows:].reshape(short_tokens.shape),
         long_grad.reshape(long_tokens.shape),
         short_grad.reshape(short_tokens.shape),
-        gain1_sum,
+        sums[10, :depth],
         g_gate.T,
-        gate_bias_sum,
+        rows[9],
         g_input.T,
         rows[0],
         rows[1:5],
         rows[5],
-        decay_sum,
+        gate_sums[0],
         rows[6],
-        open_sum,
+        gate_sums[1],
         rows[7],
         rows[8],
         g_out,
-        gain2_sum,
+        sums[11, :depth],
         g_mgate.T,
         g_mup.T,
         g_down,

time: 1020 us -> 533 us (0.52)
  waiting for transfers between devices: 749 us -> 0.14 us
  Pallas kernels: 176 us -> 462 us
  between operations: 15.3 us -> 1.73 us
  other arithmetic: 20.5 us -> 8.17 us
    reduce_scatter x2 -> x0, waiting for transfers between devices: 349 us -> none  [scatter_slots(): lax.psum_scatter(flat_grads, ('seq', 'row'), scatter_dimension=0, tiled=T...]
    pallas_call x0 -> x2, Pallas kernels: none -> 286 us  [the longest x1 153 us: scatter_call(): pl.pallas_call(functools.partial(scatter_kernel, zcount, chunks, (2, 2, 2...]
    psum x2 -> x0, waiting for transfers between devices: 240 us -> none  [shards(): lax.psum((jnp.sum(gain1_grad, axis=0), jnp.sum(gain2_grad, axis=0), jnp.s...]
    all_gather x2 -> x0, waiting for transfers between devices: 159 us -> none  [to_slots(): lax.all_gather(jnp.concatenate(parts, axis=0), ('seq', 'row'), axis=0, ti...]
  transfers between devices with their start and end apart: 8 -> 2, of which waited for: 6 -> 1; matrix products, arithmetic and copies ran while one was open for 3% -> 3% of each run, Pallas kernels for 3% -> 25%
where the time goes in v2:
time: 533 us; the launch traced here: 530 us
  Pallas kernels  462 us (87%)
  local copies, waits for them, and re-layouts  36.5 us (7%)
  blocking collectives  17.7 us (3%)
  other arithmetic  8.17 us (2%)
    pallas_call x1, Pallas kernels, scatter_call(): pl.pallas_call(functools.partial(scatter_kernel, zcount, chunks, (2, 2, 2...  153 us
    pallas_call x1, Pallas kernels, gather_call(): pl.pallas_call(functools.partial(gather_kernel, zcount, chunks, (2, 2, 3,...  133 us
    pallas_call x1, Pallas kernels, shards(): pl.pallas_call(functools.partial(mlp_kernel, ltiles, tokens // TILE), gri...  74.3 us
    pallas_call x1, Pallas kernels, shards(): pl.pallas_call(functools.partial(last_kernel, ltiles, tiles), grid=(group...  49.8 us
    pallas_call x1, Pallas kernels, shards(): pl.pallas_call(functools.partial(front_kernel, ltiles, tiles), grid=(grou...  32 us
    pallas_call x1, Pallas kernels, shards(): pl.pallas_call(functools.partial(back_kernel, ltiles, tiles), grid=(group...  19.9 us
    all_gather x2, blocking collectives, entering(): got = lax.all_gather(ends, 'seq')  17.7 us
  transfers between devices with their start and end apart: 2, of which 1 were waited for; matrix products, arithmetic and copies ran while one was open for 3% of the time, Pallas kernels for 25%

profile of v2, /device:TPU:0, one launch (start us, length us, event | category | flops | bytes accessed | tf_op | source)
XLA Modules:
  0.0 530.3 jit_solution(9155562757294896470)
XLA Ops:
  0.7 1.4 slice_bitcast_fusion.8
  2.1 2.9 collective-permute-start
  5.1 1.3 slice_bitcast_fusion.4
  8.0 1.2 pad_maximum_fusion.1.cot_ref
  11.8 1.3 stack.30
  13.1 1.3 stack.31
  14.4 1.3 stack.32
  15.7 1.3 stack.33
  17.0 1.3 stack.34
  18.3 132.8 %gather.1 = (bf16[2,2,2,4,144,1024]{5,4,3,2,1,0:T(8,128)(2,1)}, bf16[2,2,2,4,288,1024]{5,4,3,2,1,0:T(8,128)(2,1)}) custom-call(bf16[144,1024]{1,0:T(8,128)(2,1)} %pad_maximum_fusion.3.refs_0_, bf16[288,1024]{1,0:T(8,128)(2,1)} %pad_maximum_fusion.2.refs_1_), custom_call_target="tpu_custom_call" | custom-call | tf_op jit(solution)/shard_map/gather/pallas_call | solution.py:601
  151.9 1.6 concatenate.48.pc_ref
  153.6 1.1 pad_maximum_fusion.x_ref
  154.7 32.0 %front.1 = (f32[656,1536]{1,0:T(8,128)}, f32[656,1536]{1,0:T(8,128)}, f32[656,1536]{1,0:T(8,128)}, f32[656,1536]{1,0:T(8,128)}, f32[656,1536]{1,0:T(8,128)}, /*i...) custom-call(f32[1,1]{1,0:T(1,128)} %bitcast.6.first_ref, ...), custom_call_target="tpu_custom_call" | custom-call | tf_op jit(solution)/shard_map/front/pallas_call | solution.py:905
  187.6 1.1 copy-done.7
  188.7 8.8 %all-gather.2 = f32[8,2,1536]{2,1,0:T(2,128)S(1)} all-gather(f32[1,2,1536]{2,1,0:T(2,128)S(1)} %slice_bitcast_fusion.10), channel_id=2, replica_groups=mesh['seq'=8,'row'=4] {'seq'}, dimensions={0}, use_global_device_ids=true | all-gather | bytes 110592 | tf_op jit(solution)/shard_map/all_gather | solution.py:802
  198.4 74.3 %mlp.1 = (bf16[640,1024]{1,0:T(8,128)(2,1)}, f32[640,1024]{1,0:T(8,128)}, bf16[640,1024]{1,0:T(8,128)(2,1)}, bf16[128,1536]{1,0:T(8,128)(2,1)}, f32[8,1024]{1,0:T(8,128)}, /*index=5*/bf16[32,288,1024]{2,1,0:T(8,128)(2,1)}) custom-call(bf16[656,1024]{1,0:T(8,128)(2,1)} %copy-done, bf16[640,1024]{1,0:T(8,128)(2,1)} %pad_maximum_fusion.1.cot_ref, ...), custom_call_target="tpu_custom_call" | custom-call | tf_op jit(solution)/shard_map/mlp/pallas_call | solution.py:931
  272.7 1.3 copy-done.8
  274.0 1.0 copy-done.11
  275.0 19.9 %back.1 = (bf16[32,48,1024]{2,1,0:T(8,128)(2,1)}, bf16[656,1536]{1,0:T(8,128)(2,1)}, f32[656,1536]{1,0:T(8,128)}, f32[144,1536]{1,0:T(8,128)S(1)}, f32[8,1536]{1,0:T(8,128)S(1)}, /*index=5*/f32[8,1536]{1,0:T(8,128)S(1)}) custom-call(bf16[640,1024]{1,0:T(8,128)(2,1)S(1)} %copy-done.8, bf16[32,144,1024]{2,1,0:T(8,128)(2,1)} %bitcast.81, ...), custom_call_target="tpu_custom_call" | custom-call | tf_op jit(solution)/shard_map/back/pallas_call | solution.py:965
  294.9 1.0 copy-done.9
  295.9 8.8 %all-gather.3 = f32[8,2,1536]{2,1,0:T(2,128)S(1)} all-gather(f32[1,2,1536]{2,1,0:T(2,128)S(1)} %slice_bitcast_fusion.9), channel_id=3, replica_groups=mesh['seq'=8,'row'=4] {'seq'}, dimensions={0}, use_global_device_ids=true | all-gather | bytes 110592 | tf_op jit(solution)/shard_map/all_gather | solution.py:802
  305.6 49.8 %last.1 = (f32[640,1024]{1,0:T(8,128)}, f32[16,1024]{1,0:T(8,128)}, f32[8,1024]{1,0:T(8,128)}, bf16[32,48,1024]{2,1,0:T(8,128)(2,1)}, bf16[32,48,1024]{2,1,0:T(8...) custom-call(f32[1,1]{1,0:T(1,128)} %bitcast.6.first_ref, bf16[656,1024]{1,0:T(8,128)(2,1)} %copy-done, ...), custom_call_target="tpu_custom_call" | custom-call | tf_op jit(solution)/shard_map/last/pallas_call | solution.py:985
  356.1 1.6 fusion.6
  357.8 153.0 %scatter.1 = (f32[96,1024]{1,0:T(8,128)}, f32[96,1024]{1,0:T(8,128)}, f32[96,1024]{1,0:T(8,128)}, f32[48,1024]{1,0:T(8,128)}, f32[48,1024]{1,0:T(8,128)}, /*inde...) custom-call(bf16[2,2,2,4,288,1024]{5,4,3,2,1,0:T(8,128)(2,1)} %bitcast.84, ...), custom_call_target="tpu_custom_call" | custom-call | tf_op jit(solution)/shard_map/scatter/pallas_call | solution.py:757
  510.8 1.4 slice.274
  512.2 1.4 fusion.11
  513.6 3.3 slice_bitcast_fusion
  516.9 1.1 slice_bitcast_fusion.2
  518.0 1.0 slice_bitcast_fusion.1
  519.8 2.1 fusion.10
  521.8 1.4 collective-permute-start.1
  523.3 1.7 slice_reduce_fusion
  (105 shorter events, 13.7 us)
Async XLA Ops:
  0.7 5.7 %copy-start.19 = (bf16[8,192,192]{2,1,0:T(8,128)(2,1)S(1)}, bf16[8,192,192]{2,1,0:T(8,128)(2,1)}, u32[]{:S(2)}) copy-start(bf16[8,192,192]{2,1,0:T(8,128)(2,1)} %param.36) | copy-start | bytes 1769476
  2.1 151.4 %collective-permute-start = (bf16[16,1024]{1,0:T(8,128)(2,1)}, bf16[16,1024]{1,0:T(8,128)(2,1)}, u32[]{:S(2)}, u32[]{:S(2)}) collective-permute-start(bf16[16,1024]{1,0:T(8,128)(2,1)} %slice_bitcast_fusion.8), channel_id=1, source_target_pairs={{0,4},{4,8},{8,12},{12,16},{16,20},{20,24},{24,28},{1,5},{5,9},{9,... | collective-permute-start | bytes 98312 | tf_op jit(solution)/shard_map/ppermute | solution.py:814
  5.1 2.1 copy-start.36
  5.1 2.8 copy-start.24
  5.1 2.9 copy-start.17
  7.9 1.3 copy-start.25
  7.9 1.3 copy-start.26
  8.0 2.1 copy-start.15
  10.6 144.1 %copy-start.1 = (bf16[4,384,384]{2,1,0:T(8,128)(2,1)}, bf16[4,384,384]{2,1,0:T(8,128)(2,1)S(1)}, u32[]{:S(2)}) copy-start(bf16[4,384,384]{2,1,0:T(8,128)(2,1)S(1)} %get-tuple-element.151.wd_ref) | copy-start | bytes 3538948
  10.6 144.1 %copy-start.2 = (bf16[4,384,384]{2,1,0:T(8,128)(2,1)}, bf16[4,384,384]{2,1,0:T(8,128)(2,1)S(1)}, u32[]{:S(2)}) copy-start(bf16[4,384,384]{2,1,0:T(8,128)(2,1)S(1)} %get-tuple-element.152.wo_ref) | copy-start | bytes 3538948
  10.6 141.3 %copy-start.35 = (f32[4,1536]{1,0:T(4,128)S(1)}, f32[4,1536]{1,0:T(4,128)}, u32[]{:S(2)}) copy-start(f32[4,1536]{1,0:T(4,128)} %param.34) | copy-start | bytes 73732
  10.6 143.0 %copy-start.18 = (bf16[1,512,1024]{2,1,0:T(8,128)(2,1)S(1)}, bf16[1,512,1024]{2,1,0:T(8,128)(2,1)}, u32[]{:S(2)}) copy-start(bf16[1,512,1024]{2,1,0:T(8,128)(2,1)} %param.25) | copy-start | bytes 3145732
  151.1 3.5 copy-start.13
  153.5 119.1 %copy-start.6 = (f32[16,1536]{1,0:T(8,128)}, f32[16,1536]{1,0:T(8,128)S(1)}, u32[]{:S(2)}) copy-start(f32[16,1536]{1,0:T(8,128)S(1)} %concatenate.48.pc_ref) | copy-start | bytes 294916
  154.6 32.0 %copy-start = (bf16[656,1024]{1,0:T(8,128)(2,1)}, bf16[656,1024]{1,0:T(8,128)(2,1)S(1)}, u32[]{:S(2)}) copy-start(bf16[656,1024]{1,0:T(8,128)(2,1)S(1)} %pad_maximum_fusion.x_ref) | copy-start | bytes 4030468
  198.4 74.3 %copy-start.4 = (f32[144,1536]{1,0:T(8,128)S(1)}, f32[144,1536]{1,0:T(8,128)}, u32[]{:S(2)}) copy-start(f32[144,1536]{1,0:T(8,128)} %copy-done.3) | copy-start | bytes 2654212
  198.4 74.3 %copy-start.5 = (bf16[512,1536]{1,0:T(8,128)(2,1)S(1)}, bf16[512,1536]{1,0:T(8,128)(2,1)}, u32[]{:S(2)}) copy-start(bf16[512,1536]{1,0:T(8,128)(2,1)} %get-tuple-element.76.mixs_ref) | copy-start | bytes 4718596
  198.4 74.3 %copy-start.10 = (f32[8,1536]{1,0:T(8,128)S(1)}, f32[8,1536]{1,0:T(8,128)}, u32[]{:S(2)}) copy-start(f32[8,1536]{1,0:T(8,128)} %broadcast_in_dim.41.sin_ref) | copy-start | bytes 147460
  272.7 1.3 copy-start.8
  295.8 9.7 %copy-start.12 = (f32[8,1536]{1,0:T(8,128)}, f32[8,1536]{1,0:T(8,128)S(1)}, u32[]{:S(2)}) copy-start(f32[8,1536]{1,0:T(8,128)S(1)} %get-tuple-element.90.bias_ref) | copy-start | bytes 147460
  305.6 50.5 %copy-start.34 = (f32[8,1024]{1,0:T(8,128)S(1)}, f32[8,1024]{1,0:T(8,128)}, u32[]{:S(2)}) copy-start(f32[8,1024]{1,0:T(8,128)} %get-tuple-element.100) | copy-start | bytes 98308
  513.6 4.4 copy-start.16
  518.0 1.8 copy-start.14
  519.8 2.1 copy-start.37
  519.8 6.2 %copy-start.30 = (f32[48,1024]{1,0:T(8,128)S(1)}, f32[48,1024]{1,0:T(8,128)}, u32[]{:S(2)}) copy-start(f32[48,1024]{1,0:T(8,128)} %get-tuple-element.102) | copy-start | bytes 589828
  519.8 6.9 %copy-start.29 = (f32[48,1024]{1,0:T(8,128)S(1)}, f32[48,1024]{1,0:T(8,128)}, u32[]{:S(2)}) copy-start(f32[48,1024]{1,0:T(8,128)} %get-tuple-element.103) | copy-start | bytes 589828
  519.8 7.6 %copy-start.28 = (f32[48,1024]{1,0:T(8,128)S(1)}, f32[48,1024]{1,0:T(8,128)}, u32[]{:S(2)}) copy-start(f32[48,1024]{1,0:T(8,128)} %get-tuple-element.190) | copy-start | bytes 589828
  521.8 6.2 %copy-start.23 = (f32[96,1024]{1,0:T(8,128)S(1)}, f32[96,1024]{1,0:T(8,128)}, u32[]{:S(2)}) copy-start(f32[96,1024]{1,0:T(8,128)} %get-tuple-element.106) | copy-start | bytes 1179652
  521.8 7.0 %copy-start.22 = (f32[96,1024]{1,0:T(8,128)S(1)}, f32[96,1024]{1,0:T(8,128)}, u32[]{:S(2)}) copy-start(f32[96,1024]{1,0:T(8,128)} %get-tuple-element.107) | copy-start | bytes 1179652
  521.8 7.7 %copy-start.21 = (f32[96,1024]{1,0:T(8,128)S(1)}, f32[96,1024]{1,0:T(8,128)}, u32[]{:S(2)}) copy-start(f32[96,1024]{1,0:T(8,128)} %get-tuple-element.194) | copy-start | bytes 1179652
  521.8 3.3 collective-permute-start.1
  526.0 4.3 copy-start.20
  (8 other events, 8.1 us)

commit v3 on v1

--- a/solution.py
+++ b/solution.py
@@ -10,6 +10,7 @@
 EPSILON = 1e-06
 F32 = jnp.float32
 BF16 = jnp.bfloat16
+GRID = (2, 2, 2, 4)
 SLOTS = 32
 TILE = 16
 HALO = 16
@@ -91,7 +92,7 @@
 
 
 def flat(block):
-    return block.reshape(block.shape[0] * block.shape[1], block.shape[2])
+    return block.reshape(-1, block.shape[-1])
 
 
 def gates(dp, ip, c8):
@@ -118,11 +119,429 @@
     return out, moved
 
 
-def front_kernel(
-    ltiles, tiles, first_ref, x_ref, gain_ref, wg_ref, wi_ref, wd_ref, wo_ref, pc_ref,
-    gp_ref, in_ref, dp_ref, ip_ref, st_ref, pr_ref, mix_ref, end_ref, nm_ref, cv_ref, cl_ref,
-):
-    @pl.when(pl.program_id(0) == 0)
+def place_of():
+    s = lax.axis_index("seq")
+    return s // 4, (s // 2) % 2, s % 2, lax.axis_index("row")
+
+
+def device_at(y, x, c, z):
+    return ((y * 2 + x) * 2 + c, z)
+
+
+class Peers:
+    def __init__(self, zcount):
+        y, x, c, z = self.place = place_of()
+        self.far = [(z + k) % zcount for k in range(1, zcount)]
+        self.along = [device_at(y, x, c, q) for q in self.far]
+        self.near = ((y + c) % 2, (x + 1 - c) % 2)
+        self.first = device_at(*self.near, c, z)
+        self.second = device_at((y + 1 - c) % 2, (x + c) % 2, c, z)
+        self.other = device_at(y, x, 1 - c, z)
+
+    def meet(self):
+        everyone = [*self.along, self.first, self.second, self.other]
+        barrier = pltpu.get_barrier_semaphore()
+        for peer in everyone:
+            pl.semaphore_signal(
+                barrier, inc=1, device_id=peer, device_id_type=pl.DeviceIdType.MESH
+            )
+        pl.semaphore_wait(barrier, len(everyone))
+
+
+def remote(source, target, send, recv, device):
+    return pltpu.make_async_remote_copy(
+        src_ref=source,
+        dst_ref=target,
+        send_sem=send,
+        recv_sem=recv,
+        device_id=device,
+        device_id_type=pl.DeviceIdType.MESH,
+    )
+
+
+class Spread:
+    def __init__(self, peers, own, full, send, recv):
+        self.peers, self.own, self.full, self.send, self.recv = peers, own, full, send, recv
+
+    def go(self, stage, act):
+        y, x, c, z = self.peers.place
+        p, full = self.peers, self.full
+        if stage == 0:
+            for k, device in enumerate(p.along):
+                act(remote(self.own, full(y, x, c, z), self.send(k), self.recv(k), device))
+            return
+        k = len(p.along) + stage - 1
+        if stage == 2:
+
+            @pl.when(c == 0)
+            def _():
+                part = full(y, slice(None), c, slice(None))
+                act(remote(part, part, self.send(k), self.recv(k), p.second))
+
+            @pl.when(c == 1)
+            def _():
+                part = full(slice(None), x, c, slice(None))
+                act(remote(part, part, self.send(k), self.recv(k), p.second))
+
+            return
+        if stage == 1:
+            part, device = full(y, x, c, slice(None)), p.first
+        else:
+            part, device = full(slice(None), slice(None), c, slice(None)), p.other
+        act(remote(part, part, self.send(k), self.recv(k), device))
+
+    def start(self, stage):
+        self.go(stage, lambda d: d.start())
+
+    def arrive(self, stage):
+        self.go(stage, lambda d: d.wait_recv())
+
+    def drain(self):
+        for stage in range(4):
+            self.go(stage, lambda d: d.wait_send())
+
+
+def wave_of(t, count, lags):
+    for stage in range(len(lags), -1, -1):
+        piece = t - sum(lags[:stage])
+        if 0 <= piece < count:
+            yield piece, stage
+
+
+class Gather:
+    def __init__(self, zcount, ins, outs, sems, chunks, lags):
+        self.csem, self.ssem, self.rsem = sems
+        self.peers = Peers(zcount)
+        self.lags = lags
+        y, x, c, z = self.peers.place
+        self.spreads, self.copies = [], []
+        for i, (which, start, size) in enumerate(chunks):
+            rows = pl.ds(start, size)
+            own = ins[which].at[rows]
+
+            def full(a, b, d, e, ref=outs[which], rows=rows):
+                return ref.at[a, b, d, e, rows]
+
+            def send(k, i=i):
+                return self.ssem.at[i, k]
+
+            def recv(k, i=i):
+                return self.rsem.at[i, k]
+
+            self.spreads.append(Spread(self.peers, own, full, send, recv))
+            self.copies.append(pltpu.make_async_copy(own, full(y, x, c, z), self.csem.at[i]))
+        self.waves = len(chunks) + sum(lags) + 1
+
+    def wave(self, t):
+        for i, stage in wave_of(t, len(self.spreads), self.lags):
+            if stage == 0:
+                self.copies[i].start()
+            elif stage == 1:
+                self.copies[i].wait()
+            if stage > 0:
+                self.spreads[i].arrive(stage - 1)
+            if stage < 4:
+                self.spreads[i].start(stage)
+
+    def drain(self):
+        for spread in self.spreads:
+            spread.drain()
+
+
+def in_turn(weave, step, plan):
+    def point(k):
+        for s, points in enumerate(plan):
+            if k < len(points) and points[k]:
+
+                @pl.when(step == s)
+                def _(todo=points[k]):
+                    for t in todo:
+                        weave.wave(t)
+
+    return point
+
+
+def spread_out(waves, ahead, steps, points):
+    todo = list(range(waves))
+    plan = []
+    for s in range(steps):
+        row = []
+        for k in range(points):
+            take = ahead if s == 0 and k == 0 else 1
+            if s == steps - 1 and k == points - 1:
+                take = len(todo)
+            row.append(todo[:take])
+            todo = todo[take:]
+        plan.append(row)
+    return plan
+
+
+def row_chunks(parts, size):
+    return [
+        (which, start, size)
+        for which, part in enumerate(parts)
+        for start in range(0, part.shape[0], size)
+    ]
+
+
+def gather_sems(count, zcount):
+    links = pltpu.SemaphoreType.DMA((count, zcount + 2))
+    return [pltpu.SemaphoreType.DMA((count,)), links, links]
+
+
+def gathered(part, zcount):
+    return jax.ShapeDtypeStruct((2, 2, 2, zcount) + part.shape, part.dtype)
+
+
+def gather_kernel(zcount, chunks, lags, number, *refs):
+    gather = Gather(zcount, refs[:number], refs[number : 2 * number], refs[2 * number :], chunks, lags)
+    gather.peers.meet()
+    for t in range(gather.waves):
+        gather.wave(t)
+    gather.drain()
+
+
+def gather_call(parts, zcount):
+    chunks = row_chunks(parts, 16)
+    hbm = pl.BlockSpec(memory_space=pl.ANY)
+    return pl.pallas_call(
+        functools.partial(gather_kernel, zcount, chunks, (2, 2, 3, 2), len(parts)),
+        out_shape=[gathered(p, zcount) for p in parts],
+        in_specs=[hbm] * len(parts),
+        out_specs=[hbm] * len(parts),
+        scratch_shapes=gather_sems(len(chunks), zcount),
+        compiler_params=pltpu.CompilerParams(collective_id=0, has_side_effects=True),
+        name="gather",
+    )(*parts)
+
+
+CORE, GATES, SUMS, HALVED = 0, 1, 2, 3
+
+
+class Scatter:
+    def __init__(self, zcount, ins, outs, buffers, sems, chunks, lags):
+        self.peers = Peers(zcount)
+        self.zcount, self.chunks, self.lags = zcount, chunks, lags
+        self.ins, self.outs, self.buffers = ins, outs, buffers
+        self.csem, self.ssem, self.rsem = sems[:3]
+        self.pieces = [Piece(self, i, sems[3:], *chunk) for i, chunk in enumerate(chunks)]
+        self.waves = len(chunks) + sum(lags) + 1
+
+    def wave(self, t):
+        for i, stage in wave_of(t, len(self.pieces), self.lags):
+            if stage <= 4 or self.pieces[i].spread is not None:
+                self.pieces[i].step(stage)
+
+    def drain(self):
+        for piece in self.pieces:
+            piece.drain()
+
+
+def add_into(into, i, part, j):
+    into[i] = (into[i].astype(F32) + part[j].astype(F32)).astype(into.dtype)
+
+
+class Piece:
+    def __init__(self, owner, i, sems, kind, slot, which, source, span, target, place):
+        self.o, self.i, self.kind, self.slot = owner, i, kind, slot
+        self.a, self.r0, self.r1, self.r2, self.r3 = owner.buffers[kind]
+        self.source, self.lead, self.rows = owner.ins[which], source, pl.ds(*span)
+        self.target, self.place = owner.outs[target], place
+        self.spread = None
+        if kind in (GATES, SUMS):
+            y, x, c, z = owner.peers.place
+
+            def full(*at_place):
+                return self.target.at[at_place]
+
+            def send(k):
+                return sems[0].at[i, k]
+
+            def recv(k):
+                return sems[1].at[i, k]
+
+            self.spread = Spread(owner.peers, full(y, x, c, z), full, send, recv)
+
+    def local(self):
+        c = self.o.peers.place[2]
+        if self.kind == HALVED:
+            mine = self.source.at[self.lead, :, :, :, self.rows]
+        else:
+            mine = self.source.at[:, :, c, :, self.rows]
+        return pltpu.make_async_copy(mine, self.a.at[self.slot], self.o.csem.at[self.i])
+
+    def send(self, stage, act):
+        s, peers = self.slot, self.o.peers
+        y, x, c, z = peers.place
+
+        def go(source, target, k, device):
+            act(remote(source, target, self.o.ssem.at[self.i, k], self.o.rsem.at[self.i, k], device))
+
+        if stage == 0:
+            if self.kind != HALVED:
+                theirs = self.source.at[:, :, 1 - c, :, self.rows]
+                go(theirs, self.r0.at[s], 0, peers.other)
+        elif stage == 1:
+
+            @pl.when(c == 0)
+            def _():
+                go(self.a.at[s, 1 - y], self.r1.at[s], 1, peers.second)
+
+            @pl.when(c == 1)
+            def _():
+                go(self.a.at[s, :, 1 - x], self.r1.at[s], 1, peers.second)
+
+        elif stage == 2:
+            go(self.a.at[(s, *peers.near)], self.r2.at[s], 2, peers.first)
+        else:
+            for k, device in enumerate(peers.along):
+                go(self.a.at[s, y, x, peers.far[k]], self.r3.at[s, k], 3 + k, device)
+
+    def step(self, stage):
+        s, zcount = self.slot, self.o.zcount
+        y, x, c, z = self.o.peers.place
+        if stage == 0:
+            self.local().start()
+        elif stage <= 4:
+            self.send(stage - 1, lambda d: d.wait_recv())
+        else:
+            self.spread.arrive(stage - 5)
+        if stage == 1:
+            self.local().wait()
+            if self.kind != HALVED:
+
+                @pl.loop(0, 4 * zcount)
+                def _(q):
+                    i = (s, q // (2 * zcount), (q // zcount) % 2, q % zcount)
+                    add_into(self.a, i, self.r0, i)
+
+        elif stage == 2:
+
+            @pl.loop(0, 2 * zcount)
+            def _(q):
+                h = q // zcount
+                i = (s, y * (1 - c) + h * c, h * (1 - c) + x * c, q % zcount)
+                add_into(self.a, i, self.r1, (s, h, q % zcount))
+
+        elif stage == 3:
+
+            @pl.loop(0, zcount)
+            def _(q):
+                add_into(self.a, (s, y, x, q), self.r2, (s, q))
+
+        elif stage == 4:
+            total = self.a[s, y, x, z].astype(F32)
+            for k in range(zcount - 1):
+                total = total + self.r3[s, k].astype(F32)
+            if self.spread is None:
+                self.target[self.place : self.place + total.shape[0]] = total
+            else:
+                self.target[y, x, c, z] = total.astype(self.target.dtype)
+        if stage < 4:
+            self.send(stage, lambda d: d.start())
+        elif stage < 8 and self.spread is not None:
+            self.spread.start(stage - 4)
+
+    def drain(self):
+        for stage in range(4):
+            self.send(stage, lambda d: d.wait_send())
+        if self.spread is not None:
+            self.spread.drain()
+
+
+def five(number, shape, dtype, zcount):
+    lead = [(2, 2, zcount), (2, 2, zcount), (2, zcount), (zcount,), (zcount - 1,)]
+    return [pltpu.VMEM((number, *d, *shape), dtype) for d in lead]
+
+
+def scatter_kernel(zcount, chunks, lags, nin, nout, *refs):
+    ins, outs, rest = refs[:nin], refs[nin : nin + nout], refs[nin + nout :]
+    halved = (rest[15], None, *rest[16:19])
+    buffers = [rest[0:5], rest[5:10], rest[10:15], halved]
+    scatter = Scatter(zcount, ins, outs, buffers, rest[19:], chunks, lags)
+    scatter.peers.meet()
+    for t in range(scatter.waves):
+        scatter.wave(t)
+    scatter.drain()
+
+
+def scatter_call(halved, mains, gate_grads, sums, zcount):
+    grid = (2, 2, 2, zcount)
+    rows, depth = mains[0].shape[1:]
+    nmain = len(mains)
+    ins = [m.reshape(grid + m.shape[1:]) for m in mains]
+    ins += [a.reshape(grid + a.shape[1:]) for a in (gate_grads, sums)]
+    outs = [shape_of((rows, depth), F32) for _ in mains]
+    outs += [shape_of(a.shape, a.dtype) for a in ins[nmain:]]
+    chunks = [
+        (SUMS, 0, nmain + 1, None, (0, sums.shape[1]), nmain + 1, 0),
+        (GATES, 0, nmain, None, (0, gate_grads.shape[1]), nmain, 0),
+    ]
+    halves = halved.shape[0]
+    number = 0
+    ins.append(halved)
+    for k in range(3):
+        outs.append(shape_of((halves * rows, depth), F32))
+        for h in range(halves):
+            chunks.append(
+                (HALVED, number, nmain + 2, h, (k * rows, rows), nmain + 2 + k, h * rows)
+            )
+            number += 1
+    for i in range(nmain):
+        chunks.append((CORE, i, i, None, (0, rows), i, 0))
+    n = len(chunks)
+    links = pltpu.SemaphoreType.DMA((n, zcount + 2))
+    lone = five(number, (rows, depth), BF16, zcount)
+    return pl.pallas_call(
+        functools.partial(
+            scatter_kernel, zcount, chunks, (2, 2, 2, 2, 1, 1, 1, 1), len(ins), len(outs)
+        ),
+        out_shape=outs,
+        in_specs=[pl.BlockSpec(memory_space=pl.ANY)] * len(ins),
+        out_specs=[pl.BlockSpec(memory_space=pltpu.VMEM)] * len(outs),
+        scratch_shapes=[
+            *five(nmain, (rows, depth), BF16, zcount),
+            *five(1, gate_grads.shape[1:], BF16, zcount),
+            *five(1, sums.shape[1:], F32, zcount),
+            lone[0], *lone[2:],
+            pltpu.SemaphoreType.DMA((n,)),
+            links, links, links, links,
+        ],
+        compiler_params=pltpu.CompilerParams(
+            collective_id=1, has_side_effects=True, vmem_limit_bytes=62 * MIB
+        ),
+        name="scatter",
+    )(*ins)
+
+
+def no_point(k):
+    pass
+
+
+def front_kernel(ltiles, tiles, links, *refs):
+    (
+        first_ref, x_ref, gain_ref, wg_ref, wi_ref, wd_ref, wo_ref, pc_ref
+    ) = refs[:8]
+    refs = refs[8:]
+    point, gather = no_point, None
+    step = pl.program_id(0)
+    if links is not None:
+        zcount, chunks, lags, plan, number = links
+        gather = Gather(
+            zcount, refs[:number], refs[number + 9 : 2 * number + 9], refs[2 * number + 11 :], chunks, lags
+        )
+        refs = refs[number : number + 9] + refs[2 * number + 9 : 2 * number + 11]
+        point = in_turn(gather, step, plan)
+    gp_ref, in_ref, dp_ref, ip_ref, st_ref, pr_ref, mix_ref, end_ref, nm_ref, cv_ref, cl_ref = refs
+
+    @pl.when(step == 0)
+    def _():
+        if gather is not None:
+            gather.peers.meet()
+
+    point(0)
+
+    @pl.when(step == 0)
     def _():
         @pl.loop(0, tiles)
         def _(j):
@@ -133,6 +552,7 @@
     nm = nm_ref[...]
     gp_ref[...] = dot_nt(nm, flat(wg_ref[...])) + pc_ref[GB : GB + 1, :]
     in_ref[...] = dot_nt(nm, flat(wi_ref[...])) + pc_ref[IB : IB + 1, :]
+    point(1)
     in_ref[0:HALO, :] = in_ref[0:HALO, :] * first_ref[0, 0]
     cl_ref[0:HALO, :] = jnp.zeros((HALO, cl_ref.shape[1]), BF16)
 
@@ -143,6 +563,7 @@
         cv_ref[at(j), :] = out
         cl_ref[at(j), :] = out.astype(BF16)
 
+    point(2)
     low = cl_ref[...]
     dp_ref[...] = dot_nn(low, wd_ref[0]) + pc_ref[DB : DB + 1, :]
     ip_ref[...] = dot_nn(low, wo_ref[0]) + pc_ref[OB : OB + 1, :]
@@ -177,17 +598,97 @@
         return s[TILE - 1 : TILE]
 
     lax.fori_loop(0, tiles - 1 - ltiles, short_step, jnp.zeros((1, width), F32))
-
-
-def mlp_kernel(
-    ltiles, tiles, x_ref, cot_ref, st_ref, pr_ref, gp_ref, sin_ref, mixs_ref, wo_ref, gain_ref,
-    w_ref, out_ref, dres_ref, rlow_ref, mixl_ref, gain_grad_ref, dw_ref,
-    n2_ref, acc_o, acc_n, g_ref, u_ref, d_ref, h_ref, dg_ref, du_ref,
-):
+    point(3)
+    if gather is not None:
+
+        @pl.when(step == pl.num_programs(0) - 1)
+        def _():
+            gather.drain()
+
+
+def mlp_kernel(ltiles, tiles, links, *refs):
+    (
+        x_ref, cot_ref, st_ref, pr_ref, gp_ref, sin_ref, mixs_ref, wo_ref, gain_ref, w1_ref, w2_ref
+    ) = refs[:11]
+    refs = refs[11:]
+    point, gather = no_point, None
     step = pl.program_id(0)
+    last = pl.num_programs(0) - 1
+    out_ref, dres_ref, rlow_ref, mixl_ref, gain_grad_ref, dw_hbm = refs[:6]
+    refs = refs[6:]
+    if links is not None:
+        zcount, chunks, lags, plan = links
+        own_ref, w2_ref = w2_ref, refs[0]
+        gather = Gather(zcount, [own_ref], [w2_ref], refs[-3:], chunks, lags)
+        got_ref, sems, credit = refs[-6], refs[-5], refs[-4]
+        refs = refs[1:-6]
+        point = in_turn(gather, step, plan)
+    (
+        n2_ref, acc_o, acc_n, g_ref, u_ref, d_ref, h_ref, dg_ref, du_ref, wbuf, dwbuf, wsem, dsem
+    ) = refs
     lrows = ltiles * TILE
     half = g_ref.shape[1] // 2
-    share = w_ref.shape[1] // 3
+    share = wbuf.shape[-2] // 3
+    steps = 2 * GRID[0]
+
+    def load(s):
+        source = w1_ref if s < steps // 2 else w2_ref
+        return pltpu.make_async_copy(
+            source.at[s % (steps // 2)], wbuf.at[s % 2], wsem.at[s % 2]
+        )
+
+    def each(todo, first=0):
+        for s in range(first, steps):
+
+            @pl.when(step == s)
+            def _(s=s):
+                todo(s)
+
+    if gather is not None:
+        y, x, c, z = gather.peers.place
+
+    def store(s):
+        h, q = s // (steps // 2), s % (steps // 2)
+        mine = dwbuf if gather is None else dwbuf.at[:, c]
+        return pltpu.make_async_copy(mine, dw_hbm.at[h, q], dsem)
+
+    def swap():
+        return remote(
+            dwbuf.at[:, 1 - c], got_ref, sems.at[0], sems.at[1], gather.peers.other
+        )
+
+    def settle(s):
+        if gather is not None:
+            swap().wait_recv()
+
+            @pl.loop(0, got_ref.shape[0] * got_ref.shape[1])
+            def _(k):
+                i, j = k // got_ref.shape[1], k % got_ref.shape[1]
+                both = dwbuf[i, c, j].astype(F32) + got_ref[i, j].astype(F32)
+                dwbuf[i, c, j] = both.astype(BF16)
+
+            if s < steps - 1:
+                pl.semaphore_signal(
+                    credit,
+                    inc=1,
+                    device_id=gather.peers.other,
+                    device_id_type=pl.DeviceIdType.MESH,
+                )
+        store(s).start()
+
+    def clear(s):
+        store(s).wait()
+        if gather is not None:
+            swap().wait_send()
+
+    @pl.when(step == 0)
+    def _():
+        load(0).start()
+        load(1).start()
+        if gather is not None:
+            gather.peers.meet()
+
+    point(0)
 
     @pl.when(step == 0)
     def _():
@@ -212,13 +713,25 @@
 
         acc_n[...] = jnp.zeros_like(acc_n)
 
+    point(1)
+
+    @pl.when(step == steps // 2)
+    def _():
+        load(steps // 2).start()
+        load(steps // 2 + 1).start()
+
+    each(lambda s: load(s).wait())
+    slot = lax.rem(step, 2)
     n2 = n2_ref[...]
-    wg = flat(w_ref[:, 0:share, :])
-    wu = flat(w_ref[:, share : 2 * share, :])
-    wd = flat(w_ref[:, 2 * share :, :])
+    wg = flat(wbuf[slot, ..., 0:share, :])
+    wu = flat(wbuf[slot, ..., share : 2 * share, :])
+    wd = flat(wbuf[slot, ..., 2 * share :, :])
     g_ref[...] = dot_nt(n2, wg)
     u_ref[...] = dot_nt(n2, wu)
+    point(2)
     d_ref[...] = dot_nt(cot_ref[...], wd)
+    each(lambda s: settle(s - 1), 1)
+    point(3)
 
     @pl.loop(0, tiles)
     def _(i):
@@ -231,14 +744,27 @@
             dg_ref[at(i), cols] = (d * u * slope).astype(BF16)
             du_ref[at(i), cols] = (d * ge).astype(BF16)
 
+    point(4)
     acc_o[...] += dot_nn(h_ref[...], wd)
     acc_n[...] += dot_nn(dg_ref[...], wg) + dot_nn(du_ref[...], wu)
-    shape = (dw_ref.shape[0], share, dw_ref.shape[2])
-    dw_ref[:, 0:share, :] = dot_tn(dg_ref[...], n2).astype(BF16).reshape(shape)
-    dw_ref[:, share : 2 * share, :] = dot_tn(du_ref[...], n2).astype(BF16).reshape(shape)
-    dw_ref[:, 2 * share :, :] = dot_tn(h_ref[...], cot_ref[...]).astype(BF16).reshape(shape)
-
-    @pl.when(step == pl.num_programs(0) - 1)
+    point(5)
+    each(lambda s: clear(s - 1), 1)
+    lead = dwbuf.shape[:-2]
+    rest = (share, dwbuf.shape[-1])
+    for k, (left, right) in enumerate(((dg_ref, n2_ref), (du_ref, n2_ref), (h_ref, cot_ref))):
+        grad = dot_tn(left[...], right[...]).astype(BF16)
+        dwbuf[..., k * share : (k + 1) * share, :] = grad.reshape(lead + rest)
+        if k < 2:
+            point(6 + k)
+
+    if gather is not None:
+        @pl.when(step > 0)
+        def _():
+            pl.semaphore_wait(credit, 1)
+
+        swap().start()
+
+    @pl.when(step == last)
     def _():
         def one(i, total):
             r = dres_ref[at(i), :]
@@ -253,6 +779,10 @@
             return total + fold(dn * (r * s))
 
         gain_grad_ref[...] = lax.fori_loop(0, tiles, one, jnp.zeros(gain_grad_ref.shape, F32))
+        settle(steps - 1)
+        clear(steps - 1)
+        if gather is not None:
+            gather.drain()
 
 
 def back_kernel(
@@ -315,7 +845,7 @@
 def last_kernel(
     ltiles, tiles, first_ref, x_ref, gain_ref, nm_ref, dres_ref, wg_ref, wi_ref, wd_ref, wo_ref,
     pc_ref, in_ref, dp_ref, ip_ref, st_ref, pr_ref, sin_ref, tot_ref, rch_ref, cin_ref, gl_ref,
-    dx_ref, halo_ref, gain_grad_ref, dwg_ref, dwi_ref, gd_ref, go_ref, small_ref,
+    bias_ref, dx_ref, halo_ref, gain_grad_ref, dwg_ref, dwi_ref, gg_ref, small_ref,
     acc, dc_ref, cl_ref, dl_ref, ol_ref, il_ref,
 ):
     width = in_ref.shape[1]
@@ -373,8 +903,11 @@
     _, sum_d, sum_o, sum_p = carry
 
     low, dlow, olow = cl_ref[...], dl_ref[...], ol_ref[...]
-    gd_ref[0] = dot_tn(low, dlow)
-    go_ref[0] = dot_tn(low, olow)
+    half = width // 2
+    for which, grads in ((0, dlow), (1, olow)):
+        product = dot_tn(low, grads).astype(BF16)
+        gg_ref[which, 0] = product[:half, :half]
+        gg_ref[which, 1] = product[half:, half:]
     dc_ref[...] += dot_nt(dlow, wd_ref[0]) + dot_nt(olow, wo_ref[0])
 
     def conv_step(j, carry):
@@ -396,7 +929,7 @@
         )
 
     sum_c, sum_i, sums = lax.fori_loop(0, tiles, conv_step, (zero8, zero8, (zero8,) * 4))
-    parts = [sum_i, *sums, sum_c, sum_d, sum_o, sum_p * pc_ref[S8 : S8 + 1, :]]
+    parts = [sum_i, *sums, sum_c, sum_d, sum_o, sum_p * pc_ref[S8 : S8 + 1, :], bias_ref[...]]
     rows = [jnp.sum(p, axis=0, keepdims=True) for p in parts]
     small_ref[...] = jnp.concatenate(rows + [jnp.zeros((16 - len(rows), width), F32)], axis=0)
 
@@ -450,9 +983,9 @@
     return pl.BlockSpec((rows, width), lambda g: (0, g))
 
 
-def params(limit):
+def params(limit, **more):
     return pltpu.CompilerParams(
-        dimension_semantics=("arbitrary",), vmem_limit_bytes=int(limit * MIB)
+        dimension_semantics=("arbitrary",), vmem_limit_bytes=int(limit * MIB), **more
     )
 
 
@@ -463,12 +996,6 @@
     top = jnp.concatenate([pairs[:, 0], zero], axis=2)
     low = jnp.concatenate([zero, pairs[:, 1]], axis=2)
     return jnp.concatenate([top, low], axis=1)
-
-
-def unpair(grads):
-    width = grads.shape[1] // 2
-    both = jnp.stack([grads[:, :width, :width], grads[:, width:, width:]], axis=1)
-    return both.reshape(-1, width, width)
 
 
 def to_slots(parts, count):
@@ -548,8 +1075,36 @@
 
     long_x = long_tokens.reshape(lrows, depth)
     halo_x = hop(long_x[lrows - HALO :], "seq", 1)
-    mixw = to_slots([gate_weight.T, input_weight.T, out_weight], count)
-    mlpw = to_slots([mlp_gate_weight.T, mlp_up_weight.T, mlp_down_weight], count)
+    pair_own = [gate_weight.T, input_weight.T]
+    mlp_own = [mlp_gate_weight.T, mlp_up_weight.T, mlp_down_weight]
+    zcount = lax.axis_size("row")
+    fast = lax.axis_size("seq") == 8 and count == SLOTS
+    hbm = pl.BlockSpec(memory_space=pl.ANY)
+    if fast:
+        (pairw,) = gather_call([jnp.concatenate(pair_own, axis=0)], zcount)
+        hshare = mlp_own[0].shape[0] // 2
+        mlp_first, mlp_second = [
+            jnp.concatenate([w[h * hshare : (h + 1) * hshare] for w in mlp_own]) for h in range(2)
+        ]
+        front_own = [out_weight, mlp_first]
+        front_chunks = row_chunks(front_own, 16)
+        lags = (2, 2, 3, 2)
+        plan = spread_out(len(front_chunks) + sum(lags) + 1, 2, 4, 4)
+        front_links = (zcount, front_chunks, lags, plan, len(front_own))
+        front_extra = dict(
+            specs=[hbm] * 2,
+            shapes=[gathered(w, zcount) for w in front_own],
+            scratch=gather_sems(len(front_chunks), zcount),
+            params=dict(collective_id=2, has_side_effects=True),
+        )
+    else:
+        pairw = to_slots(pair_own, count)
+        outw = to_slots([out_weight], count)
+        mlpw = to_slots(mlp_own, count).reshape(GRID + (3, 2, -1, depth))
+        w_first, w_second = [mlpw[..., h, :, :].reshape(GRID + (-1, depth)) for h in range(2)]
+        front_own, front_links = [], None
+        front_extra = dict(specs=[], shapes=[], scratch=[], params={})
+    pairw = pairw.reshape(SLOTS, -1, depth)
     x = jnp.concatenate([halo_x, long_x, short_tokens.reshape(srows, depth)], axis=0)
     place = lax.axis_index("seq")
     first = jnp.where(place > 0, 1.0, 0.0).astype(F32).reshape(1, 1)
@@ -591,63 +1146,83 @@
 
     wide = shape_of((total, chans), F32)
     narrow = shape_of((HALO + lrows, chans), F32)
-    gp, inner, dp, ip, states, reach, mix_s, ends, normed = pl.pallas_call(
-        functools.partial(front_kernel, ltiles, tiles),
+    gp, inner, dp, ip, states, reach, mix_s, ends, normed, *wide_w = pl.pallas_call(
+        functools.partial(front_kernel, ltiles, tiles, front_links),
         grid=(groups,),
         in_specs=[
             scalar, whole((total, depth)), whole((1, depth)), mix_part(0), mix_part(1),
-            pair_spec, pair_spec, pc_spec,
+            pair_spec, pair_spec, pc_spec, *front_extra["specs"],
         ],
         out_specs=[
             col, col, col, col, col, col_long, columns(srows, width), col8,
-            kept((total, depth)),
+            kept((total, depth)), *front_extra["specs"],
         ],
         out_shape=[
             wide, wide, wide, wide, wide, narrow, shape_of((srows, chans), BF16),
-            shape_of((8, chans), F32), shape_of((total, depth), BF16),
-        ],
-        scratch_shapes=[pltpu.VMEM((total, width), F32), pltpu.VMEM((total, width), BF16)],
-        compiler_params=params(48),
+            shape_of((8, chans), F32), shape_of((total, depth), BF16), *front_extra["shapes"],
+        ],
+        scratch_shapes=[
+            pltpu.VMEM((total, width), F32), pltpu.VMEM((total, width), BF16),
+            *front_extra["scratch"],
+        ],
+        compiler_params=params(48, **front_extra["params"]),
         name="front",
-    )(first, x, gain1, mixw, mixw, pair_d, pair_o, chan)
+    )(first, x, gain1, pairw, pairw, pair_d, pair_o, chan, *front_own)
+    if fast:
+        outw, w_first = wide_w
+        outw = outw.reshape(SLOTS, -1, depth)
 
     s_in = entering(ends[0:2], False)
 
     steps = 4
     hid = units // steps
-    slots = SLOTS // steps
-    share = 3 * ushare
-    out, d_res, rlow, mix_l, gain2_grad, dmlp = pl.pallas_call(
-        functools.partial(mlp_kernel, ltiles, tokens // TILE),
+    block = GRID[1:] + (3 * ushare // 2, depth)
+    wbuf = pltpu.VMEM((2,) + block, BF16)
+    dwbuf = pltpu.VMEM(block, BF16)
+    one_dma = pltpu.SemaphoreType.DMA
+    if fast:
+        chunks = row_chunks([mlp_second], 16)
+        waves = len(chunks) + sum(lags) + 1
+        plan = spread_out(waves, 3, 3, 8)
+        mlp_links = (zcount, chunks, lags, plan)
+        w_last, more_specs, more_shapes = mlp_second, [hbm], [gathered(mlp_second, zcount)]
+        half_block = (block[0],) + block[2:]
+        more_scratch = [
+            pltpu.VMEM(half_block, BF16), one_dma((2,)), pltpu.SemaphoreType.REGULAR,
+            *gather_sems(len(chunks), zcount),
+        ]
+        dw_shape = (2, 2) + half_block
+        more_params = dict(collective_id=3, has_side_effects=True)
+    else:
+        mlp_links, w_last, more_specs, more_shapes, more_scratch = None, w_second, [], [], []
+        dw_shape, more_params = (2, 2) + block, {}
+    out, d_res, rlow, mix_l, gain2_grad, dmlp, *_ = pl.pallas_call(
+        functools.partial(mlp_kernel, ltiles, tokens // TILE, mlp_links),
         grid=(steps,),
         in_specs=[
             whole((total, depth)), whole((tokens, depth)), whole((HALO + lrows, chans)),
             whole((HALO + lrows, chans)), whole((HALO + lrows, chans)), whole((8, chans)),
-            whole((srows, chans)),
-            pl.BlockSpec((SLOTS, cshare, depth), lambda g: (0, 2, 0), pipeline_mode=pl.Buffered(1)),
-            whole((1, depth)),
-            pl.BlockSpec((slots, share, depth), lambda g: (g, 0, 0)),
+            whole((srows, chans)), whole((SLOTS, cshare, depth)), whole((1, depth)), hbm, hbm,
         ],
         out_specs=[
             whole((tokens, depth)), whole((tokens, depth)), whole((tokens, depth)),
-            whole((lrows, chans)), whole((8, depth)),
-            pl.BlockSpec((slots, share, depth), lambda g: (g, 0, 0)),
+            whole((lrows, chans)), whole((8, depth)), hbm, *more_specs,
         ],
         out_shape=[
             shape_of((tokens, depth), BF16), shape_of((tokens, depth), F32),
             shape_of((tokens, depth), BF16), shape_of((lrows, chans), BF16),
-            shape_of((8, depth), F32), shape_of((SLOTS, share, depth), BF16),
+            shape_of((8, depth), F32), shape_of(dw_shape, BF16), *more_shapes,
         ],
         scratch_shapes=[
             pltpu.VMEM((tokens, depth), BF16), pltpu.VMEM((tokens, depth), F32),
             pltpu.VMEM((tokens, depth), F32), pltpu.VMEM((tokens, hid), F32),
             pltpu.VMEM((tokens, hid), F32), pltpu.VMEM((tokens, hid), F32),
             pltpu.VMEM((tokens, hid), BF16), pltpu.VMEM((tokens, hid), BF16),
-            pltpu.VMEM((tokens, hid), BF16),
-        ],
-        compiler_params=params(60),
+            pltpu.VMEM((tokens, hid), BF16), wbuf, dwbuf, one_dma((2,)), one_dma, *more_scratch,
+        ],
+        compiler_params=params(62, **more_params),
         name="mlp",
-    )(x, cot, states, reach, gp, s_in, mix_s, mixw, gain2, mlpw)
+    )(x, cot, states, reach, gp, s_in, mix_s, outw, gain2, w_first, w_last)
 
     slot_spec = pl.BlockSpec((per, cshare, depth), lambda g: (g, 0, 0))
     slot_shape = shape_of((SLOTS, cshare, depth), BF16)
@@ -655,7 +1230,7 @@
         functools.partial(back_kernel, ltiles, tiles),
         grid=(groups,),
         in_specs=[
-            whole((tokens, depth)), mix_part(2), columns(lrows, width), columns(srows, width),
+            whole((tokens, depth)), mix_part(0), columns(lrows, width), columns(srows, width),
             col, col, col_long, col8, col, pc_spec,
         ],
         out_specs=[slot_spec, col, col, col_long, col8, col8],
@@ -666,26 +1241,27 @@
         scratch_shapes=[pltpu.VMEM((tokens, width), F32)],
         compiler_params=params(48),
         name="back",
-    )(rlow, mixw, mix_l, mix_s, gp, states, reach, s_in, dp, chan)
+    )(rlow, outw, mix_l, mix_s, gp, states, reach, s_in, dp, chan)
 
     c_in = entering(back_ends[0:2], True)
 
-    grad_pair = shape_of((groups, width, width), F32)
-    d_x, d_halo, gain1_grad, d_gate, d_input, d_decay, d_open, small = pl.pallas_call(
+    blocks, bwidth = decay_gate_weight.shape[0:2]
+    d_x, d_halo, gain1_grad, d_gate, d_input, d_gates, small = pl.pallas_call(
         functools.partial(last_kernel, ltiles, tiles),
         grid=(groups,),
         in_specs=[
             scalar, whole((total, depth)), whole((1, depth)), whole((total, depth)),
             whole((tokens, depth)), mix_part(0), mix_part(1), pair_spec, pair_spec, pc_spec,
-            col, col, col, col, col_long, col8, col, col_long, col8, col,
+            col, col, col, col, col_long, col8, col, col_long, col8, col, col8,
         ],
         out_specs=[
             whole((tokens, depth)), whole((HALO, depth)), whole((8, depth)), slot_spec, slot_spec,
-            pair_spec, pair_spec, pc_spec,
+            pl.BlockSpec((2, 2, bwidth, bwidth), lambda g: (0, g, 0, 0)), pc_spec,
         ],
         out_shape=[
             shape_of((tokens, depth), F32), shape_of((HALO, depth), F32), shape_of((8, depth), F32),
-            slot_shape, slot_shape, grad_pair, grad_pair, shape_of((16, chans), F32),
+            slot_shape, slot_shape, shape_of((2, blocks, bwidth, bwidth), BF16),
+            shape_of((16, chans), F32),
         ],
         scratch_shapes=[
             pltpu.VMEM((total, depth), F32), pltpu.VMEM((total, width), F32),
@@ -695,48 +1271,61 @@
         compiler_params=params(60),
         name="last",
     )(
-        first, x, gain1, normed, d_res, mixw, mixw, pair_d, pair_o, chan,
+        first, x, gain1, normed, d_res, pairw, pairw, pair_d, pair_o, chan,
         inner, dp, ip, states, reach, s_in, total_grad, back_reach, c_in, gate_low,
+        gate_bias_part,
     )
 
     late = hop(d_halo, "seq", -1)
     long_grad = d_x[:lrows].at[lrows - HALO :].add(late)
     short_grad = d_x[lrows:]
 
-    g_mgate, g_mup, g_down = scatter_slots(dmlp, 3, count)
-    dmix = jnp.concatenate([d_gate, d_input, d_out], axis=1)
-    g_gate, g_input, g_out = scatter_slots(dmix, 3, count)
-    sums = lax.psum(
-        (
-            jnp.sum(gain1_grad, axis=0),
-            jnp.sum(gain2_grad, axis=0),
-            jnp.sum(gate_bias_part, axis=0),
-            small[0:9],
-            unpair(d_decay),
-            unpair(d_open),
-        ),
-        ("seq", "row"),
+    lanes = 2048
+    gains = jnp.stack([jnp.sum(gain1_grad, axis=0), jnp.sum(gain2_grad, axis=0)])
+    small = jnp.concatenate(
+        [
+            jnp.pad(small[0:10], ((0, 0), (0, lanes - chans))),
+            jnp.pad(gains, ((0, 0), (0, lanes - depth))),
+            jnp.zeros((4, lanes), F32),
+        ],
+        axis=0,
     )
-    gain1_sum, gain2_sum, gate_bias_sum, rows, decay_sum, open_sum = sums
+    if fast:
+        mains = [d_gate, d_input, d_out]
+        tiled = small.reshape(2, 8, lanes // 128, 128).transpose(0, 2, 1, 3)
+        shares = scatter_call(
+            dmlp, mains, d_gates.reshape(SLOTS, -1, bwidth), tiled.reshape(SLOTS, 8, 128), zcount
+        )
+        g_gate, g_input, g_out, gate_sums, sums, g_mgate, g_mup, g_down = shares
+        gate_sums = gate_sums.reshape(d_gates.shape)
+        sums = sums.reshape(2, lanes // 128, 8, 128).transpose(0, 2, 1, 3).reshape(16, lanes)
+    else:
+        dmlp = dmlp.reshape(2, SLOTS, 3, -1, depth).transpose(1, 2, 0, 3, 4)
+        g_mgate, g_mup, g_down = scatter_slots(dmlp.reshape(SLOTS, -1, depth), 3, count)
+        dmix = jnp.concatenate([d_gate, d_input, d_out], axis=1)
+        g_gate, g_input, g_out = scatter_slots(dmix, 3, count)
+        gate_sums, sums = lax.psum((d_gates.astype(F32), small), ("seq", "row"))
+    gate_sums = gate_sums.astype(F32)
+    rows = sums[0:10, :chans]
     return (
         out[:lrows].reshape(long_tokens.shape),
         out[lrows:].reshape(short_tokens.shape),
         long_grad.reshape(long_tokens.shape),
         short_grad.reshape(short_tokens.shape),
-        gain1_sum,
+        sums[10, :depth],
         g_gate.T,
-        gate_bias_sum,
+        rows[9],
         g_input.T,
         rows[0],
         rows[1:5],
         rows[5],
-        decay_sum,
+        gate_sums[0],
         rows[6],
-        open_sum,
+        gate_sums[1],
         rows[7],
         rows[8],
         g_out,
-        gain2_sum,
+        sums[11, :depth],
         g_mgate.T,
         g_mup.T,
         g_down,

time: 1020 us -> 515 us (0.50)
  waiting for transfers between devices: 749 us -> 0.13 us
  Pallas kernels: 176 us -> 439 us
  between operations: 15.3 us -> 1.74 us
  other arithmetic: 20.5 us -> 9.53 us
    reduce_scatter x2 -> x0, waiting for transfers between devices: 349 us -> none  [scatter_slots(): lax.psum_scatter(flat_grads, ('seq', 'row'), scatter_dimension=0, tiled=T...]
    pallas_call x2 -> x4, Pallas kernels: 106 us -> 370 us  [the longest x1 152 us: scatter_call(): pl.pallas_call(functools.partial(scatter_kernel, zcount, chunks, (2, 2, 2...]
    psum x2 -> x0, waiting for transfers between devices: 240 us -> none  [shards(): lax.psum((jnp.sum(gain1_grad, axis=0), jnp.sum(gain2_grad, axis=0), jnp.s...]
    all_gather x2 -> x0, waiting for transfers between devices: 159 us -> none  [to_slots(): lax.all_gather(jnp.concatenate(parts, axis=0), ('seq', 'row'), axis=0, ti...]
  transfers between devices with their start and end apart: 8 -> 2, of which waited for: 6 -> 1; matrix products, arithmetic and copies ran while one was open for 3% -> 3% of each run, Pallas kernels for 3% -> 8%
where the time goes in v3:
time: 515 us; the launch traced here: 512 us
  Pallas kernels  439 us (85%)
  local copies, waits for them, and re-layouts  38.4 us (7%)
  blocking collectives  18.2 us (4%)
  other arithmetic  9.53 us (2%)
    pallas_call x1, Pallas kernels, scatter_call(): pl.pallas_call(functools.partial(scatter_kernel, zcount, chunks, (2, 2, 2...  152 us
    pallas_call x1, Pallas kernels, shards(): pl.pallas_call(functools.partial(mlp_kernel, ltiles, tokens // TILE, mlp_...  104 us
    pallas_call x1, Pallas kernels, shards(): pl.pallas_call(functools.partial(front_kernel, ltiles, tiles, front_links...  71.3 us
    pallas_call x1, Pallas kernels, shards(): pl.pallas_call(functools.partial(last_kernel, ltiles, tiles), grid=(group...  49.8 us
    pallas_call x1, Pallas kernels, gather_call(): pl.pallas_call(functools.partial(gather_kernel, zcount, chunks, (2, 2, 3,...  42 us
    pallas_call x1, Pallas kernels, shards(): pl.pallas_call(functools.partial(back_kernel, ltiles, tiles), grid=(group...  19.9 us
    all_gather x2, blocking collectives, entering(): got = lax.all_gather(ends, 'seq')  18.2 us
    unnamed x88, local copies, waits for them, and re-layouts  12.2 us
  transfers between devices with their start and end apart: 2, of which 1 were waited for; matrix products, arithmetic and copies ran while one was open for 3% of the time, Pallas kernels for 8%

profile of v3, /device:TPU:0, one launch (start us, length us, event | category | flops | bytes accessed | tf_op | source)
XLA Modules:
  0.0 511.9 jit_solution(9926273080158857275)
XLA Ops:
  0.7 1.4 slice_bitcast_fusion.8
  2.1 2.9 collective-permute-start
  5.1 1.7 fusion.11
  6.7 1.6 fusion.12
  8.4 1.7 fusion.13
  10.1 1.2 slice_bitcast_fusion.4
  12.9 1.2 pad_maximum_fusion.1.refs_1_
  15.2 0.9 pad_maximum_fusion.2
  20.3 42.0 %gather.1 = bf16[2,2,2,4,96,1024]{5,4,3,2,1,0:T(8,128)(2,1)} custom-call(bf16[96,1024]{1,0:T(8,128)(2,1)} %pad_maximum_fusion.4.refs_0_), custom_call_target="tpu_custom_call" | custom-call | tf_op jit(solution)/shard_map/gather/pallas_call | solution.py:307
  62.6 2.4 pad_maximum_fusion.refs_1_.refs_0_.x_ref
  65.0 71.3 %front.1 = (f32[656,1536]{1,0:T(8,128)}, f32[656,1536]{1,0:T(8,128)}, f32[656,1536]{1,0:T(8,128)}, f32[656,1536]{1,0:T(8,128)}, f32[656,1536]{1,0:T(8,128)}, /*i...) custom-call(f32[1,1]{1,0:T(1,128)} %bitcast.6.refs_0_.first_ref, ...), custom_call_target="tpu_custom_call" | custom-call | tf_op jit(solution)/shard_map/front/pallas_call | solution.py:1149
  136.4 0.9 copy-done.2
  137.3 1.1 copy-done.6
  138.3 9.1 %all-gather.2 = f32[8,2,1536]{2,1,0:T(2,128)S(1)} all-gather(f32[1,2,1536]{2,1,0:T(2,128)S(1)} %slice_bitcast_fusion.10), channel_id=2, replica_groups=mesh['seq'=8,'row'=4] {'seq'}, dimensions={0}, use_global_device_ids=true | all-gather | bytes 110592 | tf_op jit(solution)/shard_map/all_gather | solution.py:1025
  148.3 104.4 %mlp.1 = (bf16[640,1024]{1,0:T(8,128)(2,1)}, f32[640,1024]{1,0:T(8,128)}, bf16[640,1024]{1,0:T(8,128)(2,1)}, bf16[128,1536]{1,0:T(8,128)(2,1)}, f32[8,1024]{1,0:...) custom-call(bf16[656,1024]{1,0:T(8,128)(2,1)} %pad_maximum_fusion.refs_1_.refs_0_.x_ref, ...), custom_call_target="tpu_custom_call" | custom-call | tf_op jit(solution)/shard_map/mlp/pallas_call | solution.py:1199
  252.7 1.4 copy-done.4
  254.1 1.3 copy-done.7
  255.4 1.0 copy-done.10
  256.4 19.9 %back.1 = (bf16[32,48,1024]{2,1,0:T(8,128)(2,1)}, bf16[656,1536]{1,0:T(8,128)(2,1)}, f32[656,1536]{1,0:T(8,128)}, f32[144,1536]{1,0:T(8,128)S(1)}, f32[8,1536]{1,0:T(8,128)S(1)}, /*index=5*/f32[8,1536]{1,0:T(8,128)S(1)}) custom-call(bf16[640,1024]{1,0:T(8,128)(2,1)S(1)} %copy-done.7, bf16[32,48,1024]{2,1,0:T(8,128)(2,1)} %bitcast.82, ...), custom_call_target="tpu_custom_call" | custom-call | tf_op jit(solution)/shard_map/back/pallas_call | solution.py:1229
  276.3 0.9 copy-done.8
  277.8 9.1 %all-gather.3 = f32[8,2,1536]{2,1,0:T(2,128)S(1)} all-gather(f32[1,2,1536]{2,1,0:T(2,128)S(1)} %slice_bitcast_fusion.9), channel_id=3, replica_groups=mesh['seq'=8,'row'=4] {'seq'}, dimensions={0}, use_global_device_ids=true | all-gather | bytes 110592 | tf_op jit(solution)/shard_map/all_gather | solution.py:1025
  287.8 49.8 %last.1 = (f32[640,1024]{1,0:T(8,128)}, f32[16,1024]{1,0:T(8,128)}, f32[8,1024]{1,0:T(8,128)}, bf16[32,48,1024]{2,1,0:T(8,128)(2,1)}, bf16[32,48,1024]{2,1,0:T(8...) custom-call(f32[1,1]{1,0:T(1,128)} %bitcast.6.refs_0_.first_ref, ...), custom_call_target="tpu_custom_call" | custom-call | tf_op jit(solution)/shard_map/last/pallas_call | solution.py:1249
  338.4 1.6 fusion.6
  340.0 152.2 %scatter.1 = (f32[48,1024]{1,0:T(8,128)}, f32[48,1024]{1,0:T(8,128)}, f32[48,1024]{1,0:T(8,128)}, bf16[2,2,2,4,96,192]{5,4,3,2,1,0:T(8,128)(2,1)}, f32[2,2,2,4,8...) custom-call(bf16[2,2,2,4,48,1024]{5,4,3,2,1,0:T(8,128)(2,1)} %bitcast.84, ...), custom_call_target="tpu_custom_call" | custom-call | tf_op jit(solution)/shard_map/scatter/pallas_call | solution.py:495
  492.3 1.4 slice.302
  493.7 1.4 fusion.14
  495.1 3.3 slice_bitcast_fusion
  498.4 1.2 slice_bitcast_fusion.2
  499.6 1.0 slice_bitcast_fusion.1
  501.4 2.1 fusion.10
  503.4 1.4 collective-permute-start.1
  504.9 1.7 slice_reduce_fusion
  (112 shorter events, 15.6 us)
Async XLA Ops:
  0.7 10.6 %copy-start.18 = (bf16[8,192,192]{2,1,0:T(8,128)(2,1)S(1)}, bf16[8,192,192]{2,1,0:T(8,128)(2,1)}, u32[]{:S(2)}) copy-start(bf16[8,192,192]{2,1,0:T(8,128)(2,1)} %param.36) | copy-start | bytes 1769476
  2.1 60.4 %collective-permute-start = (bf16[16,1024]{1,0:T(8,128)(2,1)}, bf16[16,1024]{1,0:T(8,128)(2,1)}, u32[]{:S(2)}, u32[]{:S(2)}) collective-permute-start(bf16[16,1024]{1,0:T(8,128)(2,1)} %slice_bitcast_fusion.8), channel_id=1, source_target_pairs={{0,4},{4,8},{8,12},{12,16},{16,20},{20,24},{24,28},{1,5},{5,9},{9,... | collective-permute-start | bytes 98312 | tf_op jit(solution)/shard_map/ppermute | solution.py:1037
  5.1 7.0 %copy-start.38 = (f32[1536]{0:T(1024)S(1)}, f32[1536]{0:T(1024)}, u32[]{:S(2)}) copy-start(f32[1536]{0:T(1024)} %param.40) | copy-start | bytes 18436
  5.1 7.7 %copy-start.30 = (bf16[1,128,1024]{2,1,0:T(8,128)(2,1)S(1)}, bf16[1,128,1024]{2,1,0:T(8,128)(2,1)}, u32[]{:S(2)}) copy-start(bf16[1,128,1024]{2,1,0:T(8,128)(2,1)} %param.27) | copy-start | bytes 786436
  8.4 4.5 copy-start.17
  12.7 1.3 copy-start.15
  14.1 1.1 copy-start.28
  14.1 2.0 copy-start.34
  14.1 2.0 copy-start.35
  14.6 50.4 %copy-start = (bf16[4,384,384]{2,1,0:T(8,128)(2,1)}, bf16[4,384,384]{2,1,0:T(8,128)(2,1)S(1)}, u32[]{:S(2)}) copy-start(bf16[4,384,384]{2,1,0:T(8,128)(2,1)S(1)} %get-tuple-element.159.refs_5_.wd_ref) | copy-start | bytes 3538948
  14.6 50.4 %copy-start.1 = (bf16[4,384,384]{2,1,0:T(8,128)(2,1)}, bf16[4,384,384]{2,1,0:T(8,128)(2,1)S(1)}, u32[]{:S(2)}) copy-start(bf16[4,384,384]{2,1,0:T(8,128)(2,1)S(1)} %get-tuple-element.160.refs_6_.wo_ref) | copy-start | bytes 3538948
  20.3 42.1 %copy-start.37 = (f32[4,1536]{1,0:T(4,128)S(1)}, f32[4,1536]{1,0:T(4,128)}, u32[]{:S(2)}) copy-start(f32[4,1536]{1,0:T(4,128)} %param.34) | copy-start | bytes 73732
  20.3 42.3 %copy-start.29 = (bf16[1,128,1024]{2,1,0:T(8,128)(2,1)S(1)}, bf16[1,128,1024]{2,1,0:T(8,128)(2,1)}, u32[]{:S(2)}) copy-start(bf16[1,128,1024]{2,1,0:T(8,128)(2,1)} %param.24) | copy-start | bytes 786436
  62.3 2.7 copy-start.11
  62.3 2.7 copy-start.13
  62.5 190.2 %copy-start.5 = (f32[16,1536]{1,0:T(8,128)}, f32[16,1536]{1,0:T(8,128)S(1)}, u32[]{:S(2)}) copy-start(f32[16,1536]{1,0:T(8,128)S(1)} %concatenate.50.refs_7_.pc_ref) | copy-start | bytes 294916
  148.3 104.4 %copy-start.3 = (f32[144,1536]{1,0:T(8,128)S(1)}, f32[144,1536]{1,0:T(8,128)}, u32[]{:S(2)}) copy-start(f32[144,1536]{1,0:T(8,128)} %copy-done.2) | copy-start | bytes 2654212
  148.3 104.4 %copy-start.9 = (f32[8,1536]{1,0:T(8,128)S(1)}, f32[8,1536]{1,0:T(8,128)}, u32[]{:S(2)}) copy-start(f32[8,1536]{1,0:T(8,128)} %broadcast_in_dim.41.refs_5_.sin_ref) | copy-start | bytes 147460
  252.7 1.4 copy-start.4
  254.1 1.3 copy-start.7
  287.8 50.5 %copy-start.36 = (f32[8,1024]{1,0:T(8,128)S(1)}, f32[8,1024]{1,0:T(8,128)}, u32[]{:S(2)}) copy-start(f32[8,1024]{1,0:T(8,128)} %get-tuple-element.99) | copy-start | bytes 98308
  495.1 4.5 copy-start.16
  498.4 3.0 copy-start.14
  501.4 2.1 copy-start.39
  501.4 6.2 %copy-start.33 = (f32[48,1024]{1,0:T(8,128)S(1)}, f32[48,1024]{1,0:T(8,128)}, u32[]{:S(2)}) copy-start(f32[48,1024]{1,0:T(8,128)} %get-tuple-element.102) | copy-start | bytes 589828
  501.4 6.9 %copy-start.32 = (f32[48,1024]{1,0:T(8,128)S(1)}, f32[48,1024]{1,0:T(8,128)}, u32[]{:S(2)}) copy-start(f32[48,1024]{1,0:T(8,128)} %get-tuple-element.103) | copy-start | bytes 589828
  501.4 7.6 %copy-start.31 = (f32[48,1024]{1,0:T(8,128)S(1)}, f32[48,1024]{1,0:T(8,128)}, u32[]{:S(2)}) copy-start(f32[48,1024]{1,0:T(8,128)} %get-tuple-element.198) | copy-start | bytes 589828
  501.4 8.3 %copy-start.22 = (f32[96,1024]{1,0:T(8,128)S(1)}, f32[96,1024]{1,0:T(8,128)}, u32[]{:S(2)}) copy-start(f32[96,1024]{1,0:T(8,128)} %get-tuple-element.106) | copy-start | bytes 1179652
  503.4 7.0 %copy-start.21 = (f32[96,1024]{1,0:T(8,128)S(1)}, f32[96,1024]{1,0:T(8,128)}, u32[]{:S(2)}) copy-start(f32[96,1024]{1,0:T(8,128)} %get-tuple-element.107) | copy-start | bytes 1179652
  503.4 7.7 %copy-start.20 = (f32[96,1024]{1,0:T(8,128)S(1)}, f32[96,1024]{1,0:T(8,128)}, u32[]{:S(2)}) copy-start(f32[96,1024]{1,0:T(8,128)} %get-tuple-element.202) | copy-start | bytes 1179652
  503.4 3.3 collective-permute-start.1
  507.6 4.3 copy-start.19
  (10 other events, 9.4 us)

commit v4 on v3

--- a/solution.py
+++ b/solution.py
@@ -15,6 +15,7 @@
 TILE = 16
 HALO = 16
 MIB = 1024 * 1024
+TAIL_SLOTS = 11
 GELU_A = 0.7978845608028654
 GELU_B = 0.044715
 
@@ -248,9 +249,9 @@
             spread.drain()
 
 
-def in_turn(weave, step, plan):
+def in_turn(weave, step, plan, first=0):
     def point(k):
-        for s, points in enumerate(plan):
+        for s, points in enumerate(plan, first):
             if k < len(points) and points[k]:
 
                 @pl.when(step == s)
@@ -276,6 +277,17 @@
     return plan
 
 
+def paced(waves, ahead, marks):
+    last = marks[-1][-1]
+    plan = [[[] for _ in row] for row in marks]
+    spots = [(t, s, k) for s, row in enumerate(marks) for k, t in enumerate(row)]
+    for w in range(waves):
+        due = last * max(0, w - ahead) / max(1, waves - ahead)
+        _, s, k = next(spot for spot in spots if spot[0] >= due)
+        plan[s][k].append(w)
+    return plan
+
+
 def row_chunks(parts, size):
     return [
         (which, start, size)
@@ -347,7 +359,7 @@
         self.a, self.r0, self.r1, self.r2, self.r3 = owner.buffers[kind]
         self.source, self.lead, self.rows = owner.ins[which], source, pl.ds(*span)
         self.target, self.place = owner.outs[target], place
-        self.spread = None
+        self.spread, self.drained = None, False
         if kind in (GATES, SUMS):
             y, x, c, z = owner.peers.place
 
@@ -401,6 +413,9 @@
         s, zcount = self.slot, self.o.zcount
         y, x, c, z = self.o.peers.place
         if stage == 0:
+            for earlier in self.o.pieces[: self.i]:
+                if (earlier.kind, earlier.slot) == (self.kind, s):
+                    earlier.drain()
             self.local().start()
         elif stage <= 4:
             self.send(stage - 1, lambda d: d.wait_recv())
@@ -443,6 +458,9 @@
             self.spread.start(stage - 4)
 
     def drain(self):
+        if self.drained:
+            return
+        self.drained = True
         for stage in range(4):
             self.send(stage, lambda d: d.wait_send())
         if self.spread is not None:
@@ -456,16 +474,15 @@
 
 def scatter_kernel(zcount, chunks, lags, nin, nout, *refs):
     ins, outs, rest = refs[:nin], refs[nin : nin + nout], refs[nin + nout :]
-    halved = (rest[15], None, *rest[16:19])
-    buffers = [rest[0:5], rest[5:10], rest[10:15], halved]
-    scatter = Scatter(zcount, ins, outs, buffers, rest[19:], chunks, lags)
+    buffers = [rest[0:5], rest[5:10], rest[10:15]]
+    scatter = Scatter(zcount, ins, outs, buffers, rest[15:], chunks, lags)
     scatter.peers.meet()
     for t in range(scatter.waves):
         scatter.wave(t)
     scatter.drain()
 
 
-def scatter_call(halved, mains, gate_grads, sums, zcount):
+def scatter_call(mains, gate_grads, sums, zcount):
     grid = (2, 2, 2, zcount)
     rows, depth = mains[0].shape[1:]
     nmain = len(mains)
@@ -477,21 +494,14 @@
         (SUMS, 0, nmain + 1, None, (0, sums.shape[1]), nmain + 1, 0),
         (GATES, 0, nmain, None, (0, gate_grads.shape[1]), nmain, 0),
     ]
-    halves = halved.shape[0]
+    size = 16
     number = 0
-    ins.append(halved)
-    for k in range(3):
-        outs.append(shape_of((halves * rows, depth), F32))
-        for h in range(halves):
-            chunks.append(
-                (HALVED, number, nmain + 2, h, (k * rows, rows), nmain + 2 + k, h * rows)
-            )
+    for i in range(nmain):
+        for start in range(0, rows, size):
+            chunks.append((CORE, number, i, None, (start, size), i, start))
             number += 1
-    for i in range(nmain):
-        chunks.append((CORE, i, i, None, (0, rows), i, 0))
     n = len(chunks)
     links = pltpu.SemaphoreType.DMA((n, zcount + 2))
-    lone = five(number, (rows, depth), BF16, zcount)
     return pl.pallas_call(
         functools.partial(
             scatter_kernel, zcount, chunks, (2, 2, 2, 2, 1, 1, 1, 1), len(ins), len(outs)
@@ -500,10 +510,9 @@
         in_specs=[pl.BlockSpec(memory_space=pl.ANY)] * len(ins),
         out_specs=[pl.BlockSpec(memory_space=pltpu.VMEM)] * len(outs),
         scratch_shapes=[
-            *five(nmain, (rows, depth), BF16, zcount),
+            *five(number, (size, depth), BF16, zcount),
             *five(1, gate_grads.shape[1:], BF16, zcount),
             *five(1, sums.shape[1:], F32, zcount),
-            lone[0], *lone[2:],
             pltpu.SemaphoreType.DMA((n,)),
             links, links, links, links,
         ],
@@ -785,16 +794,18 @@
             gather.drain()
 
 
-def back_kernel(
-    ltiles, tiles, rlow_ref, wo_ref, mixl_ref, mixs_ref, gp_ref, st_ref, pr_ref, sin_ref, dp_ref,
-    pc_ref, dwo_ref, gl_ref, tot_ref, rch_ref, end_ref, bias_ref, dm_ref,
+def back_part(
+    ltiles, tiles, point, rlow_ref, wo_ref, mixl_ref, mixs_ref, gp_ref, st_ref, pr_ref, sin_ref,
+    dp_ref, pc_ref, dwo_ref, gl_ref, tot_ref, rch_ref, end_ref, bias_ref, dm_ref,
 ):
+    point(0)
     lrows = ltiles * TILE
     width = gp_ref.shape[1]
     rlow = rlow_ref[...]
     dm_ref[...] = dot_nt(rlow, flat(wo_ref[...]))
     grad = dot_tn(mixl_ref[...], rlow_ref[0:lrows, :]) + dot_tn(mixs_ref[...], rlow_ref[lrows:, :])
     dwo_ref[...] = grad.astype(BF16).reshape(dwo_ref.shape)
+    point(1)
     gl_ref[0:HALO, :] = jnp.zeros((HALO, width), BF16)
     last = row_iota((TILE, width)) == TILE - 1
 
@@ -823,6 +834,7 @@
         short_step,
         (jnp.zeros((1, width), F32), jnp.zeros((8, width), F32)),
     )
+    point(2)
     s_in = sin_ref[0:1, :]
 
     def long_step(i, carry):
@@ -842,14 +854,27 @@
     bias_ref[...] = bias
 
 
-def last_kernel(
-    ltiles, tiles, first_ref, x_ref, gain_ref, nm_ref, dres_ref, wg_ref, wi_ref, wd_ref, wo_ref,
-    pc_ref, in_ref, dp_ref, ip_ref, st_ref, pr_ref, sin_ref, tot_ref, rch_ref, cin_ref, gl_ref,
-    bias_ref, dx_ref, halo_ref, gain_grad_ref, dwg_ref, dwi_ref, gg_ref, small_ref,
-    acc, dc_ref, cl_ref, dl_ref, ol_ref, il_ref,
+def last_part(
+    ltiles, tiles, groups, point, exchange, residual, first_ref, x_ref, gain_ref, nm_ref,
+    wg_ref, wi_ref, wd_ref, wo_ref, pc_ref, in_ref, dp_ref, ip_ref, st_ref, pr_ref, sin_ref,
+    tot_ref, rch_ref, gl_ref, bias_ref, dx_ref, halo_ref, gain_grad_ref, dwg_ref, dwi_ref,
+    gg_ref, small_ref, acc, dc_ref, cl_ref, dl_ref, ol_ref, il_ref,
 ):
     width = in_ref.shape[1]
-    step = pl.program_id(0)
+    step = pl.program_id(0) - groups
+    point(0)
+    for g in range(groups):
+
+        @pl.when(step == g)
+        def _(g=g):
+            dc_ref[0:1, :] = exchange.entering(g, True)
+
+    c_in = dc_ref[0:1, :]
+
+    @pl.when(step == groups - 1)
+    def _():
+        residual.start()
+
     zero8 = jnp.zeros((8, width), F32)
     cl_ref[0:HALO, :] = jnp.zeros((HALO, width), BF16)
     dl_ref[0:HALO, :] = jnp.zeros((HALO, width), BF16)
@@ -884,7 +909,6 @@
         )
 
     s_in = sin_ref[0:1, :]
-    c_in = cin_ref[0:1, :]
 
     def long_step(i, carry):
         j = 1 + i
@@ -901,6 +925,7 @@
         0, tiles - 1 - ltiles, short_step, (jnp.zeros((1, width), F32),) + carry[1:]
     )
     _, sum_d, sum_o, sum_p = carry
+    point(1)
 
     low, dlow, olow = cl_ref[...], dl_ref[...], ol_ref[...]
     half = width // 2
@@ -909,6 +934,8 @@
         gg_ref[which, 0] = product[:half, :half]
         gg_ref[which, 1] = product[half:, half:]
     dc_ref[...] += dot_nt(dlow, wd_ref[0]) + dot_nt(olow, wo_ref[0])
+
+    point(2)
 
     def conv_step(j, carry):
         sum_c, sum_i, sums = carry
@@ -933,9 +960,11 @@
     rows = [jnp.sum(p, axis=0, keepdims=True) for p in parts]
     small_ref[...] = jnp.concatenate(rows + [jnp.zeros((16 - len(rows), width), F32)], axis=0)
 
+    point(3)
     nm = nm_ref[...]
     dwi_ref[...] = dot_tn(il_ref[...], nm).astype(BF16).reshape(dwi_ref.shape)
     dwg_ref[...] = dot_tn(gl_ref[...], nm).astype(BF16).reshape(dwg_ref.shape)
+    point(4)
     part = dot_nn(gl_ref[...], flat(wg_ref[...])) + dot_nn(il_ref[...], flat(wi_ref[...]))
 
     @pl.when(step == 0)
@@ -946,8 +975,10 @@
     def _():
         acc[...] += part
 
-    @pl.when(step == pl.num_programs(0) - 1)
+    @pl.when(step == groups - 1)
     def _():
+        residual.wait()
+
         def norm_back(j):
             v = x_ref[at(j), :].astype(F32)
             dn = acc[at(j), :]
@@ -961,10 +992,132 @@
 
         def one(i, total):
             d, part = norm_back(1 + i)
-            dx_ref[at(i), :] = dres_ref[at(i), :] + d
+            dx_ref[at(i), :] = dx_ref[at(i), :] + d
             return total + part
 
         gain_grad_ref[...] = lax.fori_loop(0, tiles - 1, one, total)
+
+    point(5)
+
+
+class Exchange:
+    def __init__(self, mine, theirs, ssem, rsem):
+        self.mine, self.theirs, self.ssem, self.rsem = mine, theirs, ssem, rsem
+        self.count = lax.axis_size("seq")
+        self.place = lax.axis_index("seq")
+
+    def peer(self, k):
+        return (lax.rem(self.place + k, self.count), lax.axis_index("row"))
+
+    def go(self, g, act):
+        for k in range(1, self.count):
+            act(
+                remote(
+                    self.mine.at[g],
+                    self.theirs.at[g, self.place],
+                    self.ssem.at[g, k - 1],
+                    self.rsem.at[g, k - 1],
+                    self.peer(k),
+                )
+            )
+
+    def start(self, g):
+        self.go(g, lambda d: d.start())
+
+    def entering(self, g, reverse):
+        self.go(g, lambda d: d.wait_recv())
+        state = jnp.zeros((1, self.mine.shape[-1]), F32)
+        for hop in range(self.count - 1):
+            source = self.count - 1 - hop if reverse else hop
+            ahead = source > self.place if reverse else source < self.place
+            reach = self.theirs[g, source, 0:1, :]
+            drive = self.theirs[g, source, 1:2, :]
+            state = jnp.where(ahead, reach * state + drive, state)
+        return state
+
+    def drain(self, groups):
+        for g in range(groups):
+            self.go(g, lambda d: d.wait_send())
+
+
+def exchange_scratch(groups, width, count):
+    links = pltpu.SemaphoreType.DMA((groups, count - 1))
+    return [
+        pltpu.VMEM((groups, 8, width), F32),
+        pltpu.VMEM((groups, count, 8, width), F32),
+        links, links,
+    ]
+
+
+def meet_all(exchange, zcount):
+    place, row = exchange.place, lax.axis_index("row")
+    everyone = [exchange.peer(k) for k in range(1, exchange.count)]
+    everyone += [(place, lax.rem(row + k, zcount)) for k in range(1, zcount)]
+    barrier = pltpu.get_barrier_semaphore()
+    for peer in everyone:
+        pl.semaphore_signal(barrier, inc=1, device_id=peer, device_id_type=pl.DeviceIdType.MESH)
+    pl.semaphore_wait(barrier, len(everyone))
+
+
+def tail_kernel(ltiles, tiles, groups, links, *refs):
+    (
+        first_ref, x_ref, gain_ref, nm_ref, dres_hbm, rlow_ref, w_ref, wg_ref, wi_ref, wd_ref,
+        wo_ref, pc_ref, mixl_ref, mixs_ref, gp_ref, in_ref, dp_ref, ip_ref, st_ref, pr_ref, sin_ref,
+    ) = refs[:21]
+    refs = refs[21:]
+    step = pl.program_id(0)
+    group = lax.rem(step, groups)
+    back_point, last_point, scatter = no_point, no_point, None
+    if links is not None:
+        zcount, chunks, lags, plan = links
+        halved = (refs[-9], None, *refs[-8:-5])
+        scatter = Scatter(
+            zcount, [refs[0]], refs[9:12], [None, None, None, halved], refs[-5:], chunks, lags
+        )
+        refs = refs[1:9] + refs[12:-9]
+        back_point = in_turn(scatter, step, plan[:groups])
+        last_point = in_turn(scatter, step, plan[groups:], groups)
+    dx_ref, halo_ref, gain_grad_ref, dwo_ref, dwg_ref, dwi_ref, gg_ref, small_ref = refs[:8]
+    (
+        acc, dc_ref, cl_ref, dl_ref, ol_ref, il_ref, gls, tots, rchs, bias_ref, dsem, *swap
+    ) = refs[8:]
+    exchange = Exchange(*swap)
+    gl_ref, tot_ref, rch_ref = gls.at[group], tots.at[group], rchs.at[group]
+    residual = pltpu.make_async_copy(dres_hbm, dx_ref, dsem)
+    width = gp_ref.shape[1]
+
+    @pl.when(step == 0)
+    def _():
+        meet_all(exchange, 1 if scatter is None else zcount)
+
+    @pl.when(step < groups)
+    def _():
+        back_part(
+            ltiles, tiles, back_point, rlow_ref, w_ref, mixl_ref, mixs_ref, gp_ref, st_ref, pr_ref,
+            sin_ref, dp_ref, pc_ref, dwo_ref, gl_ref, tot_ref, rch_ref, exchange.mine.at[group],
+            bias_ref.at[group], acc.at[0 : rlow_ref.shape[0], 0:width],
+        )
+        for g in range(groups):
+
+            @pl.when(step == g)
+            def _(g=g):
+                exchange.theirs[g, exchange.place] = jnp.zeros(exchange.theirs.shape[2:], F32)
+                exchange.start(g)
+
+    @pl.when(step >= groups)
+    def _():
+        last_part(
+            ltiles, tiles, groups, last_point, exchange, residual, first_ref, x_ref, gain_ref, nm_ref,
+            wg_ref, wi_ref, wd_ref, wo_ref, pc_ref, in_ref, dp_ref, ip_ref, st_ref, pr_ref, sin_ref,
+            tot_ref, rch_ref, gl_ref, bias_ref.at[group], dx_ref, halo_ref, gain_grad_ref, dwg_ref,
+            dwi_ref, gg_ref, small_ref, acc, dc_ref, cl_ref, dl_ref, ol_ref, il_ref,
+        )
+
+    @pl.when(step == pl.num_programs(0) - 1)
+    def _():
+        exchange.drain(groups)
+        if scatter is not None:
+            scatter.drain()
 
 
 def shape_of(shape, dtype):
@@ -1224,60 +1377,88 @@
         name="mlp",
     )(x, cot, states, reach, gp, s_in, mix_s, outw, gain2, w_first, w_last)
 
-    slot_spec = pl.BlockSpec((per, cshare, depth), lambda g: (g, 0, 0))
     slot_shape = shape_of((SLOTS, cshare, depth), BF16)
-    d_out, gate_low, total_grad, back_reach, back_ends, gate_bias_part = pl.pallas_call(
-        functools.partial(back_kernel, ltiles, tiles),
-        grid=(groups,),
+    blocks, bwidth = decay_gate_weight.shape[0:2]
+
+    def early(g):
+        return jnp.minimum(g, groups - 1)
+
+    def late(g):
+        return jnp.maximum(g - groups, 0)
+
+    def both_times(g):
+        return lax.rem(g, groups)
+
+    def slot_at(when, which=0):
+        return pl.BlockSpec((per, cshare, depth), lambda g: (when(g), which, 0))
+
+    def pair_at(when):
+        return pl.BlockSpec((1, width, width), lambda g: (when(g), 0, 0))
+
+    def cols_at(nrows, when):
+        return pl.BlockSpec((nrows, width), lambda g: (0, when(g)))
+
+    tail_links, tail_in, tail_specs, tail_shapes, tail_scratch, tail_params = None, [], [], [], [], {}
+    if fast:
+        size = 16
+        tail_chunks = []
+        for h in range(2):
+            for start in range(0, 3 * ushare // 2, size):
+                k, offset = divmod(start, ushare // 2)
+                tail_chunks.append(
+                    (HALVED, len(tail_chunks) % TAIL_SLOTS, 0, h, (start, size), k, h * (ushare // 2) + offset)
+                )
+        tail_lags = (1, 2, 2, 2)
+        marks = [[5.0 * g + t for t in (0.0, 1.5, 4.0)] for g in range(groups)]
+        marks += [
+            [5.0 * groups + 12.5 * g + t for t in (0.0, 5.0, 6.0, 9.0, 10.5, 12.5)] for g in range(groups)
+        ]
+        plan = paced(len(tail_chunks) + sum(tail_lags) + 1, 3, marks)
+        tail_links = (zcount, tail_chunks, tail_lags, plan)
+        tail_in, tail_specs = [dmlp], [hbm]
+        tail_shapes = [shape_of((ushare, depth), F32)] * 3
+        lone = five(TAIL_SLOTS, (size, depth), BF16, zcount)
+        links = one_dma((len(tail_chunks), zcount + 2))
+        tail_scratch = [lone[0], *lone[2:], one_dma((len(tail_chunks),)), links, links, links, links]
+    d_x, d_halo, gain1_grad, d_out, d_gate, d_input, d_gates, small, *mlp_grads = pl.pallas_call(
+        functools.partial(tail_kernel, ltiles, tiles, groups, tail_links),
+        grid=(2 * groups,),
         in_specs=[
-            whole((tokens, depth)), mix_part(0), columns(lrows, width), columns(srows, width),
-            col, col, col_long, col8, col, pc_spec,
-        ],
-        out_specs=[slot_spec, col, col, col_long, col8, col8],
-        out_shape=[
-            slot_shape, shape_of((total, chans), BF16), wide, narrow,
-            shape_of((8, chans), F32), shape_of((8, chans), F32),
-        ],
-        scratch_shapes=[pltpu.VMEM((tokens, width), F32)],
-        compiler_params=params(48),
-        name="back",
-    )(rlow, outw, mix_l, mix_s, gp, states, reach, s_in, dp, chan)
-
-    c_in = entering(back_ends[0:2], True)
-
-    blocks, bwidth = decay_gate_weight.shape[0:2]
-    d_x, d_halo, gain1_grad, d_gate, d_input, d_gates, small = pl.pallas_call(
-        functools.partial(last_kernel, ltiles, tiles),
-        grid=(groups,),
-        in_specs=[
-            scalar, whole((total, depth)), whole((1, depth)), whole((total, depth)),
-            whole((tokens, depth)), mix_part(0), mix_part(1), pair_spec, pair_spec, pc_spec,
-            col, col, col, col, col_long, col8, col, col_long, col8, col, col8,
+            scalar, whole((total, depth)), whole((1, depth)), whole((total, depth)), hbm,
+            whole((tokens, depth)), slot_at(early), slot_at(late, 0), slot_at(late, 1),
+            pair_at(late), pair_at(late), cols_at(16, both_times), cols_at(lrows, early),
+            cols_at(srows, early), cols_at(total, early), cols_at(total, late),
+            cols_at(total, both_times), cols_at(total, late), cols_at(total, both_times),
+            cols_at(HALO + lrows, both_times), cols_at(8, both_times), *tail_specs,
         ],
         out_specs=[
-            whole((tokens, depth)), whole((HALO, depth)), whole((8, depth)), slot_spec, slot_spec,
-            pl.BlockSpec((2, 2, bwidth, bwidth), lambda g: (0, g, 0, 0)), pc_spec,
+            whole((tokens, depth)), whole((HALO, depth)), whole((8, depth)), slot_at(early),
+            slot_at(late), slot_at(late),
+            pl.BlockSpec((2, 2, bwidth, bwidth), lambda g: (0, late(g), 0, 0)), cols_at(16, late),
+            *[whole(t.shape) for t in tail_shapes],
         ],
         out_shape=[
             shape_of((tokens, depth), F32), shape_of((HALO, depth), F32), shape_of((8, depth), F32),
-            slot_shape, slot_shape, shape_of((2, blocks, bwidth, bwidth), BF16),
-            shape_of((16, chans), F32),
+            slot_shape, slot_shape, slot_shape, shape_of((2, blocks, bwidth, bwidth), BF16),
+            shape_of((16, chans), F32), *tail_shapes,
         ],
         scratch_shapes=[
             pltpu.VMEM((total, depth), F32), pltpu.VMEM((total, width), F32),
             pltpu.VMEM((total, width), BF16), pltpu.VMEM((total, width), BF16),
             pltpu.VMEM((total, width), BF16), pltpu.VMEM((total, width), BF16),
+            pltpu.VMEM((groups, total, width), BF16), pltpu.VMEM((groups, total, width), F32),
+            pltpu.VMEM((groups, HALO + lrows, width), F32), pltpu.VMEM((groups, 8, width), F32),
+            one_dma, *exchange_scratch(groups, width, lax.axis_size("seq")), *tail_scratch,
         ],
-        compiler_params=params(60),
-        name="last",
+        compiler_params=params(63, collective_id=4, has_side_effects=True),
+        name="tail",
     )(
-        first, x, gain1, normed, d_res, pairw, pairw, pair_d, pair_o, chan,
-        inner, dp, ip, states, reach, s_in, total_grad, back_reach, c_in, gate_low,
-        gate_bias_part,
+        first, x, gain1, normed, d_res, rlow, outw, pairw, pairw, pair_d, pair_o, chan, mix_l, mix_s,
+        gp, inner, dp, ip, states, reach, s_in, *tail_in,
     )
 
-    late = hop(d_halo, "seq", -1)
-    long_grad = d_x[:lrows].at[lrows - HALO :].add(late)
+    ahead = hop(d_halo, "seq", -1)
+    long_grad = d_x[:lrows].at[lrows - HALO :].add(ahead)
     short_grad = d_x[lrows:]
 
     lanes = 2048
@@ -1294,9 +1475,10 @@
         mains = [d_gate, d_input, d_out]
         tiled = small.reshape(2, 8, lanes // 128, 128).transpose(0, 2, 1, 3)
         shares = scatter_call(
-            dmlp, mains, d_gates.reshape(SLOTS, -1, bwidth), tiled.reshape(SLOTS, 8, 128), zcount
+            mains, d_gates.reshape(SLOTS, -1, bwidth), tiled.reshape(SLOTS, 8, 128), zcount
         )
-        g_gate, g_input, g_out, gate_sums, sums, g_mgate, g_mup, g_down = shares
+        g_gate, g_input, g_out, gate_sums, sums = shares
+        g_mgate, g_mup, g_down = mlp_grads
         gate_sums = gate_sums.reshape(d_gates.shape)
         sums = sums.reshape(2, lanes // 128, 8, 128).transpose(0, 2, 1, 3).reshape(16, lanes)
     else:

time: 515 us -> 463 us (0.90)
  Pallas kernels: 439 us -> 404 us
  blocking collectives: 18.2 us -> 9.11 us
  local copies, waits for them, and re-layouts: 38.4 us -> 32.6 us
    pallas_call x1, Pallas kernels: 152 us -> 68.5 us  [scatter_call(): pl.pallas_call(functools.partial(scatter_kernel, zcount, chunks, (2, 2, 2...]
    pallas_call x2 -> x1, Pallas kernels: 69.6 us -> 118 us  [shards(): pl.pallas_call(functools.partial(tail_kernel, ltiles, tiles, groups, tail...]
    all_gather x2 -> x1, blocking collectives: 18.2 us -> 9.11 us  [entering(): got = lax.all_gather(ends, 'seq')]
    unnamed x88 -> x73, local copies, waits for them, and re-layouts: 12.2 us -> 6.97 us
  transfers between devices with their start and end apart: 2 -> 2, of which waited for: 1 -> 1; matrix products, arithmetic and copies ran while one was open for 3% -> 3% of each run, Pallas kernels for 8% -> 9%
where the time goes in v4:
time: 463 us; the launch traced here: 461 us
  Pallas kernels  404 us (87%)
  local copies, waits for them, and re-layouts  32.6 us (7%)
  other arithmetic  9.27 us (2%)
  blocking collectives  9.11 us (2%)
    pallas_call x1, Pallas kernels, shards(): pl.pallas_call(functools.partial(tail_kernel, ltiles, tiles, groups, tail...  118 us
    pallas_call x1, Pallas kernels, shards(): pl.pallas_call(functools.partial(mlp_kernel, ltiles, tokens // TILE, mlp_...  104 us
    pallas_call x1, Pallas kernels, shards(): pl.pallas_call(functools.partial(front_kernel, ltiles, tiles, front_links...  71.3 us
    pallas_call x1, Pallas kernels, scatter_call(): pl.pallas_call(functools.partial(scatter_kernel, zcount, chunks, (2, 2, 2...  68.5 us
    pallas_call x1, Pallas kernels, gather_call(): pl.pallas_call(functools.partial(gather_kernel, zcount, chunks, (2, 2, 3,...  42 us
  transfers between devices with their start and end apart: 2, of which 1 were waited for; matrix products, arithmetic and copies ran while one was open for 3% of the time, Pallas kernels for 9%

profile of v4, /device:TPU:0, one launch (start us, length us, event | category | flops | bytes accessed | tf_op | source)
XLA Modules:
  0.0 461.1 jit_solution(3478904014400413406)
XLA Ops:
  0.7 1.4 slice_bitcast_fusion.8
  2.1 2.9 collective-permute-start
  5.1 1.7 fusion.10
  6.7 1.6 fusion.11
  8.4 1.7 fusion.12
  10.1 1.2 slice_bitcast_fusion.4
  11.3 0.8 slice_bitcast_fusion.6
  12.9 1.2 pad_maximum_fusion.1.refs_1_
  15.2 0.9 pad_maximum_fusion.2
  20.3 42.0 %gather.1 = bf16[2,2,2,4,96,1024]{5,4,3,2,1,0:T(8,128)(2,1)} custom-call(bf16[96,1024]{1,0:T(8,128)(2,1)} %pad_maximum_fusion.4.refs_0_), custom_call_target="tpu_custom_call" | custom-call | tf_op jit(solution)/shard_map/gather/pallas_call | solution.py:319
  62.6 2.4 pad_maximum_fusion.refs_1_.refs_0_
  65.0 71.3 %front.1 = (f32[656,1536]{1,0:T(8,128)}, f32[656,1536]{1,0:T(8,128)}, f32[656,1536]{1,0:T(8,128)}, f32[656,1536]{1,0:T(8,128)}, f32[656,1536]{1,0:T(8,128)}, /*i...) custom-call(f32[1,1]{1,0:T(1,128)} %bitcast.6.refs_0_, ...), custom_call_target="tpu_custom_call" | custom-call | tf_op jit(solution)/shard_map/front/pallas_call | solution.py:1302
  136.4 0.9 copy-done.2
  137.3 1.1 copy-done.3
  138.3 9.1 %all-gather.1 = f32[8,2,1536]{2,1,0:T(2,128)S(1)} all-gather(f32[1,2,1536]{2,1,0:T(2,128)S(1)} %slice_bitcast_fusion.9), channel_id=2, replica_groups=mesh['seq'=8,'row'=4] {'seq'}, dimensions={0}, use_global_device_ids=true | all-gather | bytes 110592 | tf_op jit(solution)/shard_map/all_gather | solution.py:1178
  148.3 104.1 %mlp.1 = (bf16[640,1024]{1,0:T(8,128)(2,1)}, f32[640,1024]{1,0:T(8,128)}, bf16[640,1024]{1,0:T(8,128)(2,1)}, bf16[128,1536]{1,0:T(8,128)(2,1)}, f32[8,1024]{1,0:...) custom-call(bf16[656,1024]{1,0:T(8,128)(2,1)} %pad_maximum_fusion.refs_1_.refs_0_, ...), custom_call_target="tpu_custom_call" | custom-call | tf_op jit(solution)/shard_map/mlp/pallas_call | solution.py:1352
  252.5 118.0 %tail.1 = (f32[640,1024]{1,0:T(8,128)}, f32[16,1024]{1,0:T(8,128)}, f32[8,1024]{1,0:T(8,128)}, bf16[32,48,1024]{2,1,0:T(8,128)(2,1)}, bf16[32,48,1024]{2,1,0:T(8...) custom-call(f32[1,1]{1,0:T(1,128)} %bitcast.6.refs_0_, ...), custom_call_target="tpu_custom_call" | custom-call | tf_op jit(solution)/shard_map/tail/pallas_call | solution.py:1423
  370.5 0.8 reduce_sum.18
  371.3 1.6 fusion.6
  372.9 68.5 %scatter.1 = (f32[48,1024]{1,0:T(8,128)}, f32[48,1024]{1,0:T(8,128)}, f32[48,1024]{1,0:T(8,128)}, bf16[2,2,2,4,96,192]{5,4,3,2,1,0:T(8,128)(2,1)}, f32[2,2,2,4,8,128]{5,4,3,2,1,0:T(8,128)}) custom-call(bf16[2,2,2,4,48,1024]{5,4,3,2,1,0:T(8,128)(2,1)} %bitcast.82, bf16[2,2,2,4,48,1024]{5,4,3,2,1,0:T(8,128)(2,1)} %bitcast.83, ...), custom_call_target="tpu_custom_call" | custom-call | tf_op jit(solution)/shard_map/scatter/pallas_call | solution.py:505
  441.5 1.4 slice.228
  442.9 1.4 fusion.13
  444.3 3.3 slice_bitcast_fusion
  447.6 1.2 slice_bitcast_fusion.2
  448.8 1.0 slice_bitcast_fusion.1
  450.6 2.1 fusion.9
  452.6 1.4 collective-permute-start.1
  454.1 1.8 slice_reduce_fusion
  455.9 0.8 bitcast_dynamic-update-slice_fusion
  458.9 0.7 copy.66
  459.6 0.7 copy.67
  460.4 0.7 copy.68
  (92 shorter events, 9.4 us)
Async XLA Ops:
  0.7 10.6 %copy-start.11 = (bf16[8,192,192]{2,1,0:T(8,128)(2,1)S(1)}, bf16[8,192,192]{2,1,0:T(8,128)(2,1)}, u32[]{:S(2)}) copy-start(bf16[8,192,192]{2,1,0:T(8,128)(2,1)} %param.36) | copy-start | bytes 1769476
  2.1 60.4 %collective-permute-start = (bf16[16,1024]{1,0:T(8,128)(2,1)}, bf16[16,1024]{1,0:T(8,128)(2,1)}, u32[]{:S(2)}, u32[]{:S(2)}) collective-permute-start(bf16[16,1024]{1,0:T(8,128)(2,1)} %slice_bitcast_fusion.8), channel_id=1, source_target_pairs={{0,4},{4,8},{8,12},{12,16},{16,20},{20,24},{24,28},{1,5},{5,9},{9,... | collective-permute-start | bytes 98312 | tf_op jit(solution)/shard_map/ppermute | solution.py:1190
  5.1 7.0 %copy-start.31 = (f32[1536]{0:T(1024)S(1)}, f32[1536]{0:T(1024)}, u32[]{:S(2)}) copy-start(f32[1536]{0:T(1024)} %param.40) | copy-start | bytes 18436
  5.1 7.7 %copy-start.23 = (bf16[1,128,1024]{2,1,0:T(8,128)(2,1)S(1)}, bf16[1,128,1024]{2,1,0:T(8,128)(2,1)}, u32[]{:S(2)}) copy-start(bf16[1,128,1024]{2,1,0:T(8,128)(2,1)} %param.27) | copy-start | bytes 786436
  8.4 4.5 copy-start.10
  12.7 1.3 copy-start.8
  14.0 1.0 copy-start.18
  14.0 1.0 copy-start.19
  14.0 1.1 copy-start.20
  14.1 1.1 copy-start.21
  14.1 2.0 copy-start.27
  14.1 2.0 copy-start.28
  14.6 50.4 %copy-start = (bf16[4,384,384]{2,1,0:T(8,128)(2,1)}, bf16[4,384,384]{2,1,0:T(8,128)(2,1)S(1)}, u32[]{:S(2)}) copy-start(bf16[4,384,384]{2,1,0:T(8,128)(2,1)S(1)} %get-tuple-element.136.refs_5_.refs_9_) | copy-start | bytes 3538948
  14.6 50.4 %copy-start.1 = (bf16[4,384,384]{2,1,0:T(8,128)(2,1)}, bf16[4,384,384]{2,1,0:T(8,128)(2,1)S(1)}, u32[]{:S(2)}) copy-start(bf16[4,384,384]{2,1,0:T(8,128)(2,1)S(1)} %get-tuple-element.137.refs_6_.refs_10_) | copy-start | bytes 3538948
  20.3 42.1 %copy-start.30 = (f32[4,1536]{1,0:T(4,128)S(1)}, f32[4,1536]{1,0:T(4,128)}, u32[]{:S(2)}) copy-start(f32[4,1536]{1,0:T(4,128)} %param.34) | copy-start | bytes 73732
  20.3 42.3 %copy-start.22 = (bf16[1,128,1024]{2,1,0:T(8,128)(2,1)S(1)}, bf16[1,128,1024]{2,1,0:T(8,128)(2,1)}, u32[]{:S(2)}) copy-start(bf16[1,128,1024]{2,1,0:T(8,128)(2,1)} %param.24) | copy-start | bytes 786436
  62.3 2.7 copy-start.5
  62.3 2.7 copy-start.6
  62.5 73.8 %copy-start.4 = (f32[16,1536]{1,0:T(8,128)}, f32[16,1536]{1,0:T(8,128)S(1)}, u32[]{:S(2)}) copy-start(f32[16,1536]{1,0:T(8,128)S(1)} %concatenate.50.refs_7_.refs_11_) | copy-start | bytes 294916
  137.3 1.1 copy-start.3
  252.5 118.8 %copy-start.29 = (f32[8,1024]{1,0:T(8,128)S(1)}, f32[8,1024]{1,0:T(8,128)}, u32[]{:S(2)}) copy-start(f32[8,1024]{1,0:T(8,128)} %get-tuple-element.90) | copy-start | bytes 98308
  444.3 4.5 copy-start.9
  447.6 3.0 copy-start.7
  450.6 2.1 copy-start.32
  450.6 6.2 %copy-start.26 = (f32[48,1024]{1,0:T(8,128)S(1)}, f32[48,1024]{1,0:T(8,128)}, u32[]{:S(2)}) copy-start(f32[48,1024]{1,0:T(8,128)} %get-tuple-element.92) | copy-start | bytes 589828
  450.6 6.9 %copy-start.25 = (f32[48,1024]{1,0:T(8,128)S(1)}, f32[48,1024]{1,0:T(8,128)}, u32[]{:S(2)}) copy-start(f32[48,1024]{1,0:T(8,128)} %get-tuple-element.93) | copy-start | bytes 589828
  450.6 7.6 %copy-start.24 = (f32[48,1024]{1,0:T(8,128)S(1)}, f32[48,1024]{1,0:T(8,128)}, u32[]{:S(2)}) copy-start(f32[48,1024]{1,0:T(8,128)} %get-tuple-element.175) | copy-start | bytes 589828
  450.6 8.3 %copy-start.15 = (f32[96,1024]{1,0:T(8,128)S(1)}, f32[96,1024]{1,0:T(8,128)}, u32[]{:S(2)}) copy-start(f32[96,1024]{1,0:T(8,128)} %get-tuple-element.96) | copy-start | bytes 1179652
  452.6 7.0 %copy-start.14 = (f32[96,1024]{1,0:T(8,128)S(1)}, f32[96,1024]{1,0:T(8,128)}, u32[]{:S(2)}) copy-start(f32[96,1024]{1,0:T(8,128)} %get-tuple-element.97) | copy-start | bytes 1179652
  452.6 7.7 %copy-start.13 = (f32[96,1024]{1,0:T(8,128)S(1)}, f32[96,1024]{1,0:T(8,128)}, u32[]{:S(2)}) copy-start(f32[96,1024]{1,0:T(8,128)} %get-tuple-element.179) | copy-start | bytes 1179652
  452.6 3.3 collective-permute-start.1
  456.8 4.3 copy-start.12
  (3 other events, 2.7 us)

commit v5 on v4

--- a/solution.py
+++ b/solution.py
@@ -15,7 +15,8 @@
 TILE = 16
 HALO = 16
 MIB = 1024 * 1024
-TAIL_SLOTS = 11
+TAIL_SLOTS = 10
+CORE_SLOTS = 5
 GELU_A = 0.7978845608028654
 GELU_B = 0.044715
 
@@ -349,6 +350,10 @@
             piece.drain()
 
 
+def slot_of_core(i, slots):
+    return i % slots
+
+
 def add_into(into, i, part, j):
     into[i] = (into[i].astype(F32) + part[j].astype(F32)).astype(into.dtype)
 
@@ -357,6 +362,7 @@
     def __init__(self, owner, i, sems, kind, slot, which, source, span, target, place):
         self.o, self.i, self.kind, self.slot = owner, i, kind, slot
         self.a, self.r0, self.r1, self.r2, self.r3 = owner.buffers[kind]
+        self.from_core = 0 if self.r0 is None else slot_of_core(i, self.r0.shape[0])
         self.source, self.lead, self.rows = owner.ins[which], source, pl.ds(*span)
         self.target, self.place = owner.outs[target], place
         self.spread, self.drained = None, False
@@ -392,7 +398,7 @@
         if stage == 0:
             if self.kind != HALVED:
                 theirs = self.source.at[:, :, 1 - c, :, self.rows]
-                go(theirs, self.r0.at[s], 0, peers.other)
+                go(theirs, self.r0.at[self.from_core], 0, peers.other)
         elif stage == 1:
 
             @pl.when(c == 0)
@@ -414,7 +420,7 @@
         y, x, c, z = self.o.peers.place
         if stage == 0:
             for earlier in self.o.pieces[: self.i]:
-                if (earlier.kind, earlier.slot) == (self.kind, s):
+                if earlier.a is self.a and earlier.slot == s:
                     earlier.drain()
             self.local().start()
         elif stage <= 4:
@@ -427,8 +433,8 @@
 
                 @pl.loop(0, 4 * zcount)
                 def _(q):
-                    i = (s, q // (2 * zcount), (q // zcount) % 2, q % zcount)
-                    add_into(self.a, i, self.r0, i)
+                    i = (q // (2 * zcount), (q // zcount) % 2, q % zcount)
+                    add_into(self.a, (s, *i), self.r0, (self.from_core, *i))
 
         elif stage == 2:
 
@@ -470,57 +476,6 @@
 def five(number, shape, dtype, zcount):
     lead = [(2, 2, zcount), (2, 2, zcount), (2, zcount), (zcount,), (zcount - 1,)]
     return [pltpu.VMEM((number, *d, *shape), dtype) for d in lead]
-
-
-def scatter_kernel(zcount, chunks, lags, nin, nout, *refs):
-    ins, outs, rest = refs[:nin], refs[nin : nin + nout], refs[nin + nout :]
-    buffers = [rest[0:5], rest[5:10], rest[10:15]]
-    scatter = Scatter(zcount, ins, outs, buffers, rest[15:], chunks, lags)
-    scatter.peers.meet()
-    for t in range(scatter.waves):
-        scatter.wave(t)
-    scatter.drain()
-
-
-def scatter_call(mains, gate_grads, sums, zcount):
-    grid = (2, 2, 2, zcount)
-    rows, depth = mains[0].shape[1:]
-    nmain = len(mains)
-    ins = [m.reshape(grid + m.shape[1:]) for m in mains]
-    ins += [a.reshape(grid + a.shape[1:]) for a in (gate_grads, sums)]
-    outs = [shape_of((rows, depth), F32) for _ in mains]
-    outs += [shape_of(a.shape, a.dtype) for a in ins[nmain:]]
-    chunks = [
-        (SUMS, 0, nmain + 1, None, (0, sums.shape[1]), nmain + 1, 0),
-        (GATES, 0, nmain, None, (0, gate_grads.shape[1]), nmain, 0),
-    ]
-    size = 16
-    number = 0
-    for i in range(nmain):
-        for start in range(0, rows, size):
-            chunks.append((CORE, number, i, None, (start, size), i, start))
-            number += 1
-    n = len(chunks)
-    links = pltpu.SemaphoreType.DMA((n, zcount + 2))
-    return pl.pallas_call(
-        functools.partial(
-            scatter_kernel, zcount, chunks, (2, 2, 2, 2, 1, 1, 1, 1), len(ins), len(outs)
-        ),
-        out_shape=outs,
-        in_specs=[pl.BlockSpec(memory_space=pl.ANY)] * len(ins),
-        out_specs=[pl.BlockSpec(memory_space=pltpu.VMEM)] * len(outs),
-        scratch_shapes=[
-            *five(number, (size, depth), BF16, zcount),
-            *five(1, gate_grads.shape[1:], BF16, zcount),
-            *five(1, sums.shape[1:], F32, zcount),
-            pltpu.SemaphoreType.DMA((n,)),
-            links, links, links, links,
-        ],
-        compiler_params=pltpu.CompilerParams(
-            collective_id=1, has_side_effects=True, vmem_limit_bytes=62 * MIB
-        ),
-        name="scatter",
-    )(*ins)
 
 
 def no_point(k):
@@ -796,13 +751,14 @@
 
 def back_part(
     ltiles, tiles, point, rlow_ref, wo_ref, mixl_ref, mixs_ref, gp_ref, st_ref, pr_ref, sin_ref,
-    dp_ref, pc_ref, dwo_ref, gl_ref, tot_ref, rch_ref, end_ref, bias_ref, dm_ref,
+    dp_ref, pc_ref, dwo_ref, gl_ref, tot_ref, rch_ref, end_ref, bias_ref, dm_ref, free,
 ):
     point(0)
     lrows = ltiles * TILE
     width = gp_ref.shape[1]
     rlow = rlow_ref[...]
     dm_ref[...] = dot_nt(rlow, flat(wo_ref[...]))
+    free()
     grad = dot_tn(mixl_ref[...], rlow_ref[0:lrows, :]) + dot_tn(mixs_ref[...], rlow_ref[lrows:, :])
     dwo_ref[...] = grad.astype(BF16).reshape(dwo_ref.shape)
     point(1)
@@ -858,7 +814,7 @@
     ltiles, tiles, groups, point, exchange, residual, first_ref, x_ref, gain_ref, nm_ref,
     wg_ref, wi_ref, wd_ref, wo_ref, pc_ref, in_ref, dp_ref, ip_ref, st_ref, pr_ref, sin_ref,
     tot_ref, rch_ref, gl_ref, bias_ref, dx_ref, halo_ref, gain_grad_ref, dwg_ref, dwi_ref,
-    gg_ref, small_ref, acc, dc_ref, cl_ref, dl_ref, ol_ref, il_ref,
+    gg_ref, small_ref, acc, dc_ref, cl_ref, dl_ref, ol_ref, il_ref, gain2_ref, free, keep,
 ):
     width = in_ref.shape[1]
     step = pl.program_id(0) - groups
@@ -931,8 +887,10 @@
     half = width // 2
     for which, grads in ((0, dlow), (1, olow)):
         product = dot_tn(low, grads).astype(BF16)
-        gg_ref[which, 0] = product[:half, :half]
-        gg_ref[which, 1] = product[half:, half:]
+        shape = (2, half // 2, half)
+        place = (which, step // 2, lax.rem(step, 2))
+        gg_ref[(*place, slice(0, 2))] = product[:half, :half].reshape(shape)
+        gg_ref[(*place, slice(2, 4))] = product[half:, half:].reshape(shape)
     dc_ref[...] += dot_nt(dlow, wd_ref[0]) + dot_nt(olow, wo_ref[0])
 
     point(2)
@@ -958,12 +916,19 @@
     sum_c, sum_i, sums = lax.fori_loop(0, tiles, conv_step, (zero8, zero8, (zero8,) * 4))
     parts = [sum_i, *sums, sum_c, sum_d, sum_o, sum_p * pc_ref[S8 : S8 + 1, :], bias_ref[...]]
     rows = [jnp.sum(p, axis=0, keepdims=True) for p in parts]
-    small_ref[...] = jnp.concatenate(rows + [jnp.zeros((16 - len(rows), width), F32)], axis=0)
+    block = jnp.concatenate(rows + [jnp.zeros((16 - len(rows), width), F32)], axis=0)
+    for i in range(width // 128):
+        at_block = step * (width // 128) + i
+        x, c, z = at_block // 8, lax.rem(at_block // 4, 2), lax.rem(at_block, 4)
+        for h in range(2):
+            small_ref[h, x, c, z] = block[8 * h : 8 * h + 8, 128 * i : 128 * i + 128]
 
     point(3)
+    free()
     nm = nm_ref[...]
     dwi_ref[...] = dot_tn(il_ref[...], nm).astype(BF16).reshape(dwi_ref.shape)
     dwg_ref[...] = dot_tn(gl_ref[...], nm).astype(BF16).reshape(dwg_ref.shape)
+    keep()
     point(4)
     part = dot_nn(gl_ref[...], flat(wg_ref[...])) + dot_nn(il_ref[...], flat(wi_ref[...]))
 
@@ -996,6 +961,14 @@
             return total + part
 
         gain_grad_ref[...] = lax.fori_loop(0, tiles - 1, one, total)
+        zero = jnp.zeros((8, 128), F32)
+        for h in range(2):
+            for z in range(4):
+                small_ref[h, 1, 1, z] = zero
+        for z, ref in enumerate((gain_grad_ref, gain2_ref)):
+            total = jnp.sum(ref[...], axis=0, keepdims=True)
+            for i in range(8):
+                small_ref[0, 1, 1, z, i : i + 1, :] = total[:, 128 * i : 128 * i + 128]
 
     point(5)
 
@@ -1064,23 +1037,50 @@
         first_ref, x_ref, gain_ref, nm_ref, dres_hbm, rlow_ref, w_ref, wg_ref, wi_ref, wd_ref,
         wo_ref, pc_ref, mixl_ref, mixs_ref, gp_ref, in_ref, dp_ref, ip_ref, st_ref, pr_ref, sin_ref,
     ) = refs[:21]
-    refs = refs[21:]
+    gain2_ref = refs[21]
+    refs = refs[22:]
     step = pl.program_id(0)
     group = lax.rem(step, groups)
     back_point, last_point, scatter = no_point, no_point, None
+    nscratch = 19
     if links is not None:
         zcount, chunks, lags, plan = links
-        halved = (refs[-9], None, *refs[-8:-5])
+        halved_ref, refs = refs[0], refs[1:]
+        outs, shares = refs[:8], refs[8:14]
+        scratch, pool = refs[14 : 14 + nscratch], refs[14 + nscratch :]
+    else:
+        outs, scratch = refs[:8], refs[8:]
+    dx_ref, halo_ref, gain_grad_ref, dwo_hbm, dwg_hbm, dwi_hbm, gates_hbm, sums_hbm = outs
+    (
+        acc, dc_ref, cl_ref, dl_ref, ol_ref, il_ref, gls, tots, rchs, bias_ref, wst, gsrc, ssrc,
+        dsem, wsem, *swap
+    ) = scratch
+    gates_full, sums_full = gsrc, ssrc
+    if links is not None:
+        *pool, gates_full, sums_full = pool
+        main, gate_pool, sum_pool = pool[0:5], pool[5:10], pool[10:15]
         scatter = Scatter(
-            zcount, [refs[0]], refs[9:12], [None, None, None, halved], refs[-5:], chunks, lags
+            zcount,
+            [halved_ref, dwo_hbm, dwg_hbm, dwi_hbm, gsrc, ssrc],
+            [*shares, gates_full, sums_full],
+            [main, gate_pool, sum_pool, main],
+            pool[15:],
+            chunks,
+            lags,
         )
-        refs = refs[1:9] + refs[12:-9]
         back_point = in_turn(scatter, step, plan[:groups])
         last_point = in_turn(scatter, step, plan[groups:], groups)
-    dx_ref, halo_ref, gain_grad_ref, dwo_ref, dwg_ref, dwi_ref, gg_ref, small_ref = refs[:8]
-    (
-        acc, dc_ref, cl_ref, dl_ref, ol_ref, il_ref, gls, tots, rchs, bias_ref, dsem, *swap
-    ) = refs[8:]
+
+    def stash(g, k, target):
+        return pltpu.make_async_copy(wst.at[k], target.at[g // 2, g % 2], wsem.at[k])
+
+    def stashed(first, what):
+        for g in range(groups):
+
+            @pl.when(step == first + g)
+            def _(g=g):
+                what(g)
+
     exchange = Exchange(*swap)
     gl_ref, tot_ref, rch_ref = gls.at[group], tots.at[group], rchs.at[group]
     residual = pltpu.make_async_copy(dres_hbm, dx_ref, dsem)
@@ -1094,9 +1094,11 @@
     def _():
         back_part(
             ltiles, tiles, back_point, rlow_ref, w_ref, mixl_ref, mixs_ref, gp_ref, st_ref, pr_ref,
-            sin_ref, dp_ref, pc_ref, dwo_ref, gl_ref, tot_ref, rch_ref, exchange.mine.at[group],
+            sin_ref, dp_ref, pc_ref, wst.at[0], gl_ref, tot_ref, rch_ref, exchange.mine.at[group],
             bias_ref.at[group], acc.at[0 : rlow_ref.shape[0], 0:width],
+            lambda: stashed(0, lambda g: stash(g - 1, 0, dwo_hbm).wait() if g > 0 else None),
         )
+        stashed(0, lambda g: stash(g, 0, dwo_hbm).start())
         for g in range(groups):
 
             @pl.when(step == g)
@@ -1106,11 +1108,28 @@
 
     @pl.when(step >= groups)
     def _():
+        @pl.when(step == groups)
+        def _():
+            stash(groups - 1, 0, dwo_hbm).wait()
+
+        def before(g):
+            if g > 0:
+                stash(g - 1, 1, dwg_hbm).wait()
+                stash(g - 1, 2, dwi_hbm).wait()
+
+        def after(g):
+            stash(g, 1, dwg_hbm).start()
+            stash(g, 2, dwi_hbm).start()
+            if g == groups - 1:
+                stash(g, 1, dwg_hbm).wait()
+                stash(g, 2, dwi_hbm).wait()
+
         last_part(
             ltiles, tiles, groups, last_point, exchange, residual, first_ref, x_ref, gain_ref, nm_ref,
             wg_ref, wi_ref, wd_ref, wo_ref, pc_ref, in_ref, dp_ref, ip_ref, st_ref, pr_ref, sin_ref,
-            tot_ref, rch_ref, gl_ref, bias_ref.at[group], dx_ref, halo_ref, gain_grad_ref, dwg_ref,
-            dwi_ref, gg_ref, small_ref, acc, dc_ref, cl_ref, dl_ref, ol_ref, il_ref,
+            tot_ref, rch_ref, gl_ref, bias_ref.at[group], dx_ref, halo_ref, gain_grad_ref,
+            wst.at[1], wst.at[2], gsrc, ssrc, acc, dc_ref, cl_ref, dl_ref, ol_ref, il_ref, gain2_ref,
+            lambda: stashed(groups, before), lambda: stashed(groups, after),
         )
 
     @pl.when(step == pl.num_programs(0) - 1)
@@ -1118,6 +1137,14 @@
         exchange.drain(groups)
         if scatter is not None:
             scatter.drain()
+        final = [
+            pltpu.make_async_copy(gates_full, gates_hbm, wsem.at[0]),
+            pltpu.make_async_copy(sums_full, sums_hbm, wsem.at[1]),
+        ]
+        for copy in final:
+            copy.start()
+        for copy in final:
+            copy.wait()
 
 
 def shape_of(shape, dtype):
@@ -1398,29 +1425,52 @@
     def cols_at(nrows, when):
         return pl.BlockSpec((nrows, width), lambda g: (0, when(g)))
 
-    tail_links, tail_in, tail_specs, tail_shapes, tail_scratch, tail_params = None, [], [], [], [], {}
+    gate_shape, sum_shape = GRID + (bwidth // 2, bwidth), GRID + (8, 128)
+    grads_shape = shape_of(GRID + (cshare, depth), BF16)
+    tail_links, tail_in, tail_specs, tail_shapes, tail_scratch = None, [], [], [], []
     if fast:
-        size = 16
+        size, hshare = 16, ushare // 2
         tail_chunks = []
+        number = 0
         for h in range(2):
-            for start in range(0, 3 * ushare // 2, size):
-                k, offset = divmod(start, ushare // 2)
+            for start in range(0, 3 * hshare, size):
+                k, offset = divmod(start, hshare)
                 tail_chunks.append(
-                    (HALVED, len(tail_chunks) % TAIL_SLOTS, 0, h, (start, size), k, h * (ushare // 2) + offset)
+                    (HALVED, number % TAIL_SLOTS, 0, h, (start, size), k, h * hshare + offset)
                 )
-        tail_lags = (1, 2, 2, 2)
+                number += 1
+        for which in (1, 2, 3):
+            if which == 2:
+                tail_chunks.append((SUMS, 0, 5, None, (0, 8), 7, 0))
+                tail_chunks.append((GATES, 0, 4, None, (0, bwidth // 2), 6, 0))
+                during = len(tail_chunks) - 2
+            for start in range(0, cshare, size):
+                tail_chunks.append(
+                    (CORE, number % TAIL_SLOTS, which, None, (start, size), 2 + which, start)
+                )
+                number += 1
+        tail_lags = (1, 2, 2, 2, 1, 1, 1, 1)
         marks = [[5.0 * g + t for t in (0.0, 1.5, 4.0)] for g in range(groups)]
         marks += [
             [5.0 * groups + 12.5 * g + t for t in (0.0, 5.0, 6.0, 9.0, 10.5, 12.5)] for g in range(groups)
         ]
-        plan = paced(len(tail_chunks) + sum(tail_lags) + 1, 3, marks)
+        plan = paced(during, 3, marks)
+        plan[-1][-1] += range(during, len(tail_chunks) + sum(tail_lags) + 1)
         tail_links = (zcount, tail_chunks, tail_lags, plan)
-        tail_in, tail_specs = [dmlp], [hbm]
-        tail_shapes = [shape_of((ushare, depth), F32)] * 3
+        tail_in, tail_specs = [dmlp], [whole((ushare, depth))] * 3 + [whole((cshare, depth))] * 3
+        tail_shapes = [shape_of((ushare, depth), F32)] * 3 + [shape_of((cshare, depth), F32)] * 3
         lone = five(TAIL_SLOTS, (size, depth), BF16, zcount)
-        links = one_dma((len(tail_chunks), zcount + 2))
-        tail_scratch = [lone[0], *lone[2:], one_dma((len(tail_chunks),)), links, links, links, links]
-    d_x, d_halo, gain1_grad, d_out, d_gate, d_input, d_gates, small, *mlp_grads = pl.pallas_call(
+        lone[1] = five(CORE_SLOTS, (size, depth), BF16, zcount)[1]
+        n = len(tail_chunks)
+        links = one_dma((n, zcount + 2))
+        tail_scratch = [
+            *lone,
+            *five(1, gate_shape[4:], BF16, zcount),
+            *five(1, sum_shape[4:], F32, zcount),
+            one_dma((n,)), links, links, links, links,
+            pltpu.VMEM(gate_shape, BF16), pltpu.VMEM(sum_shape, F32),
+        ]
+    d_x, d_halo, _, d_out, d_gate, d_input, gate_sums, sums, *shares = pl.pallas_call(
         functools.partial(tail_kernel, ltiles, tiles, groups, tail_links),
         grid=(2 * groups,),
         in_specs=[
@@ -1429,18 +1479,17 @@
             pair_at(late), pair_at(late), cols_at(16, both_times), cols_at(lrows, early),
             cols_at(srows, early), cols_at(total, early), cols_at(total, late),
             cols_at(total, both_times), cols_at(total, late), cols_at(total, both_times),
-            cols_at(HALO + lrows, both_times), cols_at(8, both_times), *tail_specs,
+            cols_at(HALO + lrows, both_times), cols_at(8, both_times), whole((8, depth)),
+            *[hbm for _ in tail_in],
         ],
         out_specs=[
-            whole((tokens, depth)), whole((HALO, depth)), whole((8, depth)), slot_at(early),
-            slot_at(late), slot_at(late),
-            pl.BlockSpec((2, 2, bwidth, bwidth), lambda g: (0, late(g), 0, 0)), cols_at(16, late),
-            *[whole(t.shape) for t in tail_shapes],
+            whole((tokens, depth)), whole((HALO, depth)), whole((8, depth)), hbm, hbm, hbm, hbm, hbm,
+            *tail_specs,
         ],
         out_shape=[
             shape_of((tokens, depth), F32), shape_of((HALO, depth), F32), shape_of((8, depth), F32),
-            slot_shape, slot_shape, slot_shape, shape_of((2, blocks, bwidth, bwidth), BF16),
-            shape_of((16, chans), F32), *tail_shapes,
+            grads_shape, grads_shape, grads_shape, shape_of(gate_shape, BF16),
+            shape_of(sum_shape, F32), *tail_shapes,
         ],
         scratch_shapes=[
             pltpu.VMEM((total, depth), F32), pltpu.VMEM((total, width), F32),
@@ -1448,53 +1497,39 @@
             pltpu.VMEM((total, width), BF16), pltpu.VMEM((total, width), BF16),
             pltpu.VMEM((groups, total, width), BF16), pltpu.VMEM((groups, total, width), F32),
             pltpu.VMEM((groups, HALO + lrows, width), F32), pltpu.VMEM((groups, 8, width), F32),
-            one_dma, *exchange_scratch(groups, width, lax.axis_size("seq")), *tail_scratch,
+            pltpu.VMEM((3,) + GRID[2:] + (cshare, depth), BF16), pltpu.VMEM(gate_shape, BF16),
+            pltpu.VMEM(sum_shape, F32), one_dma, one_dma((3,)),
+            *exchange_scratch(groups, width, lax.axis_size("seq")), *tail_scratch,
         ],
         compiler_params=params(63, collective_id=4, has_side_effects=True),
         name="tail",
     )(
         first, x, gain1, normed, d_res, rlow, outw, pairw, pairw, pair_d, pair_o, chan, mix_l, mix_s,
-        gp, inner, dp, ip, states, reach, s_in, *tail_in,
+        gp, inner, dp, ip, states, reach, s_in, gain2_grad, *tail_in,
     )
 
     ahead = hop(d_halo, "seq", -1)
     long_grad = d_x[:lrows].at[lrows - HALO :].add(ahead)
     short_grad = d_x[lrows:]
 
-    lanes = 2048
-    gains = jnp.stack([jnp.sum(gain1_grad, axis=0), jnp.sum(gain2_grad, axis=0)])
-    small = jnp.concatenate(
-        [
-            jnp.pad(small[0:10], ((0, 0), (0, lanes - chans))),
-            jnp.pad(gains, ((0, 0), (0, lanes - depth))),
-            jnp.zeros((4, lanes), F32),
-        ],
-        axis=0,
-    )
     if fast:
-        mains = [d_gate, d_input, d_out]
-        tiled = small.reshape(2, 8, lanes // 128, 128).transpose(0, 2, 1, 3)
-        shares = scatter_call(
-            mains, d_gates.reshape(SLOTS, -1, bwidth), tiled.reshape(SLOTS, 8, 128), zcount
-        )
-        g_gate, g_input, g_out, gate_sums, sums = shares
-        g_mgate, g_mup, g_down = mlp_grads
-        gate_sums = gate_sums.reshape(d_gates.shape)
-        sums = sums.reshape(2, lanes // 128, 8, 128).transpose(0, 2, 1, 3).reshape(16, lanes)
+        g_mgate, g_mup, g_down, g_out, g_gate, g_input = shares
     else:
         dmlp = dmlp.reshape(2, SLOTS, 3, -1, depth).transpose(1, 2, 0, 3, 4)
         g_mgate, g_mup, g_down = scatter_slots(dmlp.reshape(SLOTS, -1, depth), 3, count)
-        dmix = jnp.concatenate([d_gate, d_input, d_out], axis=1)
+        dmix = jnp.concatenate([d_gate, d_input, d_out], axis=4).reshape(SLOTS, -1, depth)
         g_gate, g_input, g_out = scatter_slots(dmix, 3, count)
-        gate_sums, sums = lax.psum((d_gates.astype(F32), small), ("seq", "row"))
-    gate_sums = gate_sums.astype(F32)
-    rows = sums[0:10, :chans]
+        gate_sums, sums = lax.psum((gate_sums.astype(F32), sums), ("seq", "row"))
+    gate_sums = gate_sums.reshape(2, blocks, bwidth, bwidth).astype(F32)
+    sums = sums.reshape(2, 16, 8, 128)
+    gain_sums = sums[0, 12:14].reshape(2, depth)
+    rows = sums.transpose(0, 2, 1, 3).reshape(16, 2048)[0:10, :chans]
     return (
         out[:lrows].reshape(long_tokens.shape),
         out[lrows:].reshape(short_tokens.shape),
         long_grad.reshape(long_tokens.shape),
         short_grad.reshape(short_tokens.shape),
-        sums[10, :depth],
+        gain_sums[0],
         g_gate.T,
         rows[9],
         g_input.T,
@@ -1507,7 +1542,7 @@
         rows[7],
         rows[8],
         g_out,
-        sums[11, :depth],
+        gain_sums[1],
         g_mgate.T,
         g_mup.T,
         g_down,

time: 463 us -> 442 us (0.955)
  Pallas kernels: 404 us -> 384 us
    pallas_call x1 -> x0, Pallas kernels: 68.5 us -> none  [scatter_call(): pl.pallas_call(functools.partial(scatter_kernel, zcount, chunks, (2, 2, 2...]
    pallas_call x1, Pallas kernels: 118 us -> 167 us  [shards(): pl.pallas_call(functools.partial(tail_kernel, ltiles, tiles, groups, tail...]
  transfers between devices with their start and end apart: 2 -> 2, of which waited for: 1 -> 0; matrix products, arithmetic and copies ran while one was open for 3% -> 4% of each run, Pallas kernels for 9% -> 10%
where the time goes in v5:
time: 442 us; the launch traced here: 439 us
  Pallas kernels  384 us (87%)
  local copies, waits for them, and re-layouts  31.9 us (7%)
  blocking collectives  9.46 us (2%)
  other arithmetic  7.54 us (2%)
    pallas_call x1, Pallas kernels, shards(): pl.pallas_call(functools.partial(tail_kernel, ltiles, tiles, groups, tail...  167 us
    pallas_call x1, Pallas kernels, shards(): pl.pallas_call(functools.partial(mlp_kernel, ltiles, tokens // TILE, mlp_...  104 us
    pallas_call x1, Pallas kernels, shards(): pl.pallas_call(functools.partial(front_kernel, ltiles, tiles, front_links...  71 us
    pallas_call x1, Pallas kernels, gather_call(): pl.pallas_call(functools.partial(gather_kernel, zcount, chunks, (2, 2, 3,...  42 us
    all_gather x1, blocking collectives, entering(): got = lax.all_gather(ends, 'seq')  9.46 us
  transfers between devices with their start and end apart: 2, of which 0 were waited for; matrix products, arithmetic and copies ran while one was open for 4% of the time, Pallas kernels for 10%

profile of v5, /device:TPU:0, one launch (start us, length us, event | category | flops | bytes accessed | tf_op | source)
XLA Modules:
  0.0 438.6 jit_solution(7923614552098101019)
XLA Ops:
  0.7 1.4 slice_bitcast_fusion.8
  2.1 2.9 collective-permute-start
  5.7 0.7 divide_multiply_fusion
  6.4 1.7 fusion.9
  8.1 1.6 fusion.10
  9.7 1.7 fusion.11
  11.5 1.2 slice_bitcast_fusion.6
  12.6 0.8 slice_bitcast_fusion.4
  13.6 1.2 pad_maximum_fusion.1.refs_1_
  15.8 0.9 pad_maximum_fusion.2
  17.5 0.7 stack.21
  18.2 0.7 stack.22
  18.9 0.7 stack.23
  21.0 42.0 %gather.1 = bf16[2,2,2,4,96,1024]{5,4,3,2,1,0:T(8,128)(2,1)} custom-call(bf16[96,1024]{1,0:T(8,128)(2,1)} %pad_maximum_fusion.4.refs_0_), custom_call_target="tpu_custom_call" | custom-call | tf_op jit(solution)/shard_map/gather/pallas_call | solution.py:320
  63.2 2.4 pad_maximum_fusion.refs_1_.refs_0_
  65.6 71.0 %front.1 = (f32[656,1536]{1,0:T(8,128)}, f32[656,1536]{1,0:T(8,128)}, f32[656,1536]{1,0:T(8,128)}, f32[656,1536]{1,0:T(8,128)}, f32[656,1536]{1,0:T(8,128)}, /*i...) custom-call(f32[1,1]{1,0:T(1,128)} %bitcast.6.refs_0_, ...), custom_call_target="tpu_custom_call" | custom-call | tf_op jit(solution)/shard_map/front/pallas_call | solution.py:1329
  136.6 0.9 copy-done.2
  137.5 1.1 copy-done.3
  138.6 9.5 %all-gather.1 = f32[8,2,1536]{2,1,0:T(2,128)S(1)} all-gather(f32[1,2,1536]{2,1,0:T(2,128)S(1)} %slice_bitcast_fusion.9), channel_id=2, replica_groups=mesh['seq'=8,'row'=4] {'seq'}, dimensions={0}, use_global_device_ids=true | all-gather | bytes 110592 | tf_op jit(solution)/shard_map/all_gather | solution.py:1205
  148.9 103.6 %mlp.1 = (bf16[640,1024]{1,0:T(8,128)(2,1)}, f32[640,1024]{1,0:T(8,128)}, bf16[640,1024]{1,0:T(8,128)(2,1)}, bf16[128,1536]{1,0:T(8,128)(2,1)}, f32[8,1024]{1,0:...) custom-call(bf16[656,1024]{1,0:T(8,128)(2,1)} %pad_maximum_fusion.refs_1_.refs_0_, ...), custom_call_target="tpu_custom_call" | custom-call | tf_op jit(solution)/shard_map/mlp/pallas_call | solution.py:1379
  252.4 1.7 slice_bitcast_fusion.7
  254.1 2.3 slice_bitcast_fusion.1
  256.4 167.4 %tail.1 = (f32[640,1024]{1,0:T(8,128)}, f32[16,1024]{1,0:T(8,128)}, f32[8,1024]{1,0:T(8,128)}, bf16[2,2,2,4,48,1024]{5,4,3,2,1,0:T(8,128)(2,1)}, bf16[2,2,2,4,48...) custom-call(f32[1,1]{1,0:T(1,128)} %bitcast.6.refs_0_, ...), custom_call_target="tpu_custom_call" | custom-call | tf_op jit(solution)/shard_map/tail/pallas_call | solution.py:1473
  423.7 1.1 slice_bitcast_fusion.2
  424.9 3.3 slice_bitcast_fusion
  429.4 1.3 collective-permute-start.1
  430.7 2.1 fusion.8
  433.5 0.9 bitcast_dynamic-update-slice_fusion
  434.3 0.7 copy.63
  436.4 0.7 copy.66
  437.2 0.7 copy.67
  437.9 0.7 copy.68
  (81 shorter events, 7.6 us)
Async XLA Ops:
  0.7 12.0 %copy-start.10 = (bf16[8,192,192]{2,1,0:T(8,128)(2,1)S(1)}, bf16[8,192,192]{2,1,0:T(8,128)(2,1)}, u32[]{:S(2)}) copy-start(bf16[8,192,192]{2,1,0:T(8,128)(2,1)} %param.38) | copy-start | bytes 1769476
  2.1 61.0 %collective-permute-start = (bf16[16,1024]{1,0:T(8,128)(2,1)}, bf16[16,1024]{1,0:T(8,128)(2,1)}, u32[]{:S(2)}, u32[]{:S(2)}) collective-permute-start(bf16[16,1024]{1,0:T(8,128)(2,1)} %slice_bitcast_fusion.8), channel_id=1, source_target_pairs={{0,4},{4,8},{8,12},{12,16},{16,20},{20,24},{24,28},{1,5},{5,9},{9,... | collective-permute-start | bytes 98312 | tf_op jit(solution)/shard_map/ppermute | solution.py:1217
  6.4 7.0 %copy-start.22 = (bf16[1,128,1024]{2,1,0:T(8,128)(2,1)S(1)}, bf16[1,128,1024]{2,1,0:T(8,128)(2,1)}, u32[]{:S(2)}) copy-start(bf16[1,128,1024]{2,1,0:T(8,128)(2,1)} %param.27) | copy-start | bytes 786436
  9.7 3.8 copy-start.9
  13.4 1.3 copy-start.8
  14.7 0.9 copy-start.16
  14.7 1.0 copy-start.17
  14.7 1.0 copy-start.18
  14.7 1.1 copy-start.19
  14.7 1.1 copy-start.20
  14.8 2.0 copy-start.26
  14.8 2.0 copy-start.27
  15.3 50.3 %copy-start = (bf16[4,384,384]{2,1,0:T(8,128)(2,1)}, bf16[4,384,384]{2,1,0:T(8,128)(2,1)S(1)}, u32[]{:S(2)}) copy-start(bf16[4,384,384]{2,1,0:T(8,128)(2,1)S(1)} %get-tuple-element.124.refs_5_.refs_9_) | copy-start | bytes 3538948
  15.3 50.3 %copy-start.1 = (bf16[4,384,384]{2,1,0:T(8,128)(2,1)}, bf16[4,384,384]{2,1,0:T(8,128)(2,1)S(1)}, u32[]{:S(2)}) copy-start(bf16[4,384,384]{2,1,0:T(8,128)(2,1)S(1)} %get-tuple-element.125.refs_6_.refs_10_) | copy-start | bytes 3538948
  21.0 42.0 %copy-start.29 = (f32[4,1536]{1,0:T(4,128)S(1)}, f32[4,1536]{1,0:T(4,128)}, u32[]{:S(2)}) copy-start(f32[4,1536]{1,0:T(4,128)} %param.34) | copy-start | bytes 73732
  21.0 42.2 %copy-start.21 = (bf16[1,128,1024]{2,1,0:T(8,128)(2,1)S(1)}, bf16[1,128,1024]{2,1,0:T(8,128)(2,1)}, u32[]{:S(2)}) copy-start(bf16[1,128,1024]{2,1,0:T(8,128)(2,1)} %param.24) | copy-start | bytes 786436
  63.0 2.6 copy-start.5
  63.0 2.6 copy-start.6
  63.1 73.4 %copy-start.4 = (f32[16,1536]{1,0:T(8,128)}, f32[16,1536]{1,0:T(8,128)S(1)}, u32[]{:S(2)}) copy-start(f32[16,1536]{1,0:T(8,128)S(1)} %concatenate.47.refs_7_.refs_11_) | copy-start | bytes 294916
  136.6 0.9 copy-start.2
  137.5 1.1 copy-start.3
  424.8 3.3 copy-start.28
  424.8 4.5 %copy-start.30 = (f32[16,1024]{1,0:T(8,128)S(1)}, f32[16,1024]{1,0:T(8,128)}, u32[]{:S(2)}) copy-start(f32[16,1024]{1,0:T(8,128)} %get-tuple-element.78) | copy-start | bytes 196612
  424.8 5.8 %copy-start.7 = (bf16[2,2,2,4,96,192]{5,4,3,2,1,0:T(8,128)(2,1)S(1)}, bf16[2,2,2,4,96,192]{5,4,3,2,1,0:T(8,128)(2,1)}, u32[]{:S(2)}) copy-start(bf16[2,2,2,4,96,192]{5,4,3,2,1,0:T(8,128)(2,1)} %get-tuple-element.82) | copy-start | bytes 3538948
  429.4 4.1 collective-permute-start.1
  430.7 3.6 copy-start.25
  430.7 4.4 copy-start.24
  430.7 5.0 %copy-start.23 = (f32[48,1024]{1,0:T(8,128)S(1)}, f32[48,1024]{1,0:T(8,128)}, u32[]{:S(2)}) copy-start(f32[48,1024]{1,0:T(8,128)} %get-tuple-element.163) | copy-start | bytes 589828
  430.7 5.7 %copy-start.14 = (f32[96,1024]{1,0:T(8,128)S(1)}, f32[96,1024]{1,0:T(8,128)}, u32[]{:S(2)}) copy-start(f32[96,1024]{1,0:T(8,128)} %get-tuple-element.84) | copy-start | bytes 1179652
  432.8 4.4 %copy-start.13 = (f32[96,1024]{1,0:T(8,128)S(1)}, f32[96,1024]{1,0:T(8,128)}, u32[]{:S(2)}) copy-start(f32[96,1024]{1,0:T(8,128)} %get-tuple-element.85) | copy-start | bytes 1179652
  432.8 5.1 %copy-start.12 = (f32[96,1024]{1,0:T(8,128)S(1)}, f32[96,1024]{1,0:T(8,128)}, u32[]{:S(2)}) copy-start(f32[96,1024]{1,0:T(8,128)} %get-tuple-element.167) | copy-start | bytes 1179652
  434.3 4.3 copy-start.11
  (1 other events, 0.9 us)

commit v6 on v5

--- a/solution.py
+++ b/solution.py
@@ -217,11 +217,11 @@
         self.lags = lags
         y, x, c, z = self.peers.place
         self.spreads, self.copies = [], []
-        for i, (which, start, size) in enumerate(chunks):
-            rows = pl.ds(start, size)
-            own = ins[which].at[rows]
-
-            def full(a, b, d, e, ref=outs[which], rows=rows):
+        for i, (which, start, size, target, offset) in enumerate(chunks):
+            own = ins[which].at[pl.ds(start, size)]
+            rows = pl.ds(offset, size)
+
+            def full(a, b, d, e, ref=outs[target], rows=rows):
                 return ref.at[a, b, d, e, rows]
 
             def send(k, i=i):
@@ -291,41 +291,15 @@
 
 def row_chunks(parts, size):
     return [
-        (which, start, size)
-        for which, part in enumerate(parts)
-        for start in range(0, part.shape[0], size)
+        (which, start + i, size, target, offset + i)
+        for which, start, count, target, offset in parts
+        for i in range(0, count, size)
     ]
 
 
 def gather_sems(count, zcount):
     links = pltpu.SemaphoreType.DMA((count, zcount + 2))
     return [pltpu.SemaphoreType.DMA((count,)), links, links]
-
-
-def gathered(part, zcount):
-    return jax.ShapeDtypeStruct((2, 2, 2, zcount) + part.shape, part.dtype)
-
-
-def gather_kernel(zcount, chunks, lags, number, *refs):
-    gather = Gather(zcount, refs[:number], refs[number : 2 * number], refs[2 * number :], chunks, lags)
-    gather.peers.meet()
-    for t in range(gather.waves):
-        gather.wave(t)
-    gather.drain()
-
-
-def gather_call(parts, zcount):
-    chunks = row_chunks(parts, 16)
-    hbm = pl.BlockSpec(memory_space=pl.ANY)
-    return pl.pallas_call(
-        functools.partial(gather_kernel, zcount, chunks, (2, 2, 3, 2), len(parts)),
-        out_shape=[gathered(p, zcount) for p in parts],
-        in_specs=[hbm] * len(parts),
-        out_specs=[hbm] * len(parts),
-        scratch_shapes=gather_sems(len(chunks), zcount),
-        compiler_params=pltpu.CompilerParams(collective_id=0, has_side_effects=True),
-        name="gather",
-    )(*parts)
 
 
 CORE, GATES, SUMS, HALVED = 0, 1, 2, 3
@@ -482,42 +456,206 @@
     pass
 
 
-def front_kernel(ltiles, tiles, links, *refs):
+class Exchange:
+    def __init__(self, mine, theirs, ssem, rsem):
+        self.mine, self.theirs, self.ssem, self.rsem = mine, theirs, ssem, rsem
+        self.count = lax.axis_size("seq")
+        self.place = lax.axis_index("seq")
+
+    def peer(self, k):
+        return (lax.rem(self.place + k, self.count), lax.axis_index("row"))
+
+    def go(self, g, act):
+        for k in range(1, self.count):
+            act(
+                remote(
+                    self.mine.at[g],
+                    self.theirs.at[g, self.place],
+                    self.ssem.at[g, k - 1],
+                    self.rsem.at[g, k - 1],
+                    self.peer(k),
+                )
+            )
+
+    def start(self, g):
+        self.go(g, lambda d: d.start())
+
+    def entering(self, g, reverse):
+        self.go(g, lambda d: d.wait_recv())
+        state = jnp.zeros((1, self.mine.shape[-1]), F32)
+        for hop in range(self.count - 1):
+            source = self.count - 1 - hop if reverse else hop
+            ahead = source > self.place if reverse else source < self.place
+            reach = self.theirs[g, source, 0:1, :]
+            drive = self.theirs[g, source, 1:2, :]
+            state = jnp.where(ahead, reach * state + drive, state)
+        return state
+
+    def drain(self, groups):
+        for g in range(groups):
+            self.go(g, lambda d: d.wait_send())
+
+
+def exchange_scratch(groups, width, count):
+    links = pltpu.SemaphoreType.DMA((groups, count - 1))
+    return [
+        pltpu.VMEM((groups, 8, width), F32),
+        pltpu.VMEM((groups, count, 8, width), F32),
+        links, links,
+    ]
+
+
+def meet_all(exchange, zcount):
+    place, row = exchange.place, lax.axis_index("row")
+    everyone = [exchange.peer(k) for k in range(1, exchange.count)]
+    everyone += [(place, lax.rem(row + k, zcount)) for k in range(1, zcount)]
+    barrier = pltpu.get_barrier_semaphore()
+    for peer in everyone:
+        pl.semaphore_signal(barrier, inc=1, device_id=peer, device_id_type=pl.DeviceIdType.MESH)
+    pl.semaphore_wait(barrier, len(everyone))
+
+
+def pair_up(pair, blocks):
+    half = blocks.shape[1]
+    pair[...] = jnp.zeros_like(pair)
+    pair[0:half, 0:half] = blocks[0]
+    pair[half:, half:] = blocks[1]
+
+
+def front_kernel(ltiles, tiles, groups, links, *refs):
     (
-        first_ref, x_ref, gain_ref, wg_ref, wi_ref, wd_ref, wo_ref, pc_ref
-    ) = refs[:8]
-    refs = refs[8:]
+        long_ref, short_ref, lcot_ref, scot_ref, length_ref, gain_ref, *channel_refs
+    ) = refs[:14]
+    wd_ref, wo_ref = refs[14:16]
+    refs = refs[16:]
+    step = pl.program_id(0)
     point, gather = no_point, None
-    step = pl.program_id(0)
-    if links is not None:
-        zcount, chunks, lags, plan, number = links
-        gather = Gather(
-            zcount, refs[:number], refs[number + 9 : 2 * number + 9], refs[2 * number + 11 :], chunks, lags
-        )
-        refs = refs[number : number + 9] + refs[2 * number + 9 : 2 * number + 11]
+    zcount = 1
+    if links is None:
+        pairw, refs = refs[0], refs[1:]
+    else:
+        zcount, chunks, lags, ready, plan = links
+        owns, made = refs[:6], refs[18:21]
+        pairw = made[0]
+        gather = Gather(zcount, owns, made, refs[-3:], chunks, lags)
+        refs = refs[6:18] + refs[21:-3]
         point = in_turn(gather, step, plan)
-    gp_ref, in_ref, dp_ref, ip_ref, st_ref, pr_ref, mix_ref, end_ref, nm_ref, cv_ref, cl_ref = refs
+    gp, inn, dp, ip, st, pr, mix, sin_ref, nm_ref, x_ref, cot_ref, pc_ref = refs[:12]
+    cv_ref, cl_ref, wbuf, pairs, halo, isem, wsem, hsem, *swap = refs[12:]
+    exchange = Exchange(*swap)
+    lrows = ltiles * TILE
+    place = exchange.place
+
+    def load(g):
+        return pltpu.make_async_copy(pairw.at[g // 2, g % 2], wbuf.at[g % 2], wsem.at[g % 2])
 
     @pl.when(step == 0)
     def _():
-        if gather is not None:
-            gather.peers.meet()
-
-    point(0)
-
-    @pl.when(step == 0)
-    def _():
-        @pl.loop(0, tiles)
-        def _(j):
+        srows = short_ref.shape[0]
+        copies = [
+            pltpu.make_async_copy(source, target, isem.at[k])
+            for k, (source, target) in enumerate(
+                [
+                    (long_ref, x_ref.at[pl.ds(HALO, lrows)]),
+                    (short_ref, x_ref.at[pl.ds(HALO + lrows, srows)]),
+                    (lcot_ref, cot_ref.at[pl.ds(0, lrows)]),
+                    (scot_ref, cot_ref.at[pl.ds(lrows, srows)]),
+                ]
+            )
+        ]
+        for copy in copies:
+            copy.start()
+        meet_all(exchange, zcount)
+        ahead = remote(
+            long_ref.at[pl.ds(lrows - HALO, HALO)], halo, hsem.at[0], hsem.at[1], exchange.peer(1)
+        )
+        ahead.start()
+        todo = [] if gather is None else list(range(ready))
+
+        def some(count):
+            for t in todo[:count]:
+                gather.wave(t)
+            del todo[:count]
+
+        some(4)
+        for copy in copies:
+            copy.wait()
+
+        @pl.loop(0, ltiles)
+        def _(i):
+            rows = row_iota((TILE, 1)) + (place * lrows + i * TILE)
+            keep = jnp.where(rows < length_ref[0], 1.0, 0.0)
+            cot_ref[at(i), :] = (cot_ref[at(i), :].astype(F32) * keep).astype(BF16)
+
+        some(1)
+        ahead.wait_recv()
+        x_ref[0:HALO, :] = halo[...]
+
+        def norm(j):
             v = x_ref[at(j), :].astype(F32)
             s = lax.rsqrt(jnp.mean(v * v, axis=1, keepdims=True) + EPSILON)
             nm_ref[at(j), :] = (v * s * gain_ref[...]).astype(BF16)
 
+        pl.loop(0, tiles // 2)(norm)
+        some(1)
+        pl.loop(tiles // 2, tiles)(norm)
+        some(len(todo))
+        ahead.wait_send()
+        load(0).start()
+        load(1).start()
+
+    @pl.when(step > 0)
+    def _():
+        for g in range(groups):
+
+            @pl.when(step == g + 1)
+            def _(g=g):
+                load(g).wait()
+
+        for k, ref in zip((GB, IB, CW, CB, DB, OB, C8, S8), channel_refs):
+            pc_ref[k : k + ref.shape[0], :] = ref[...]
+        pc_ref[S8 + 1 :, :] = jnp.zeros((15 - S8, pc_ref.shape[1]), F32)
+        pair_up(pairs.at[0], wd_ref)
+        pair_up(pairs.at[1], wo_ref)
+        slot = lax.rem(step - 1, 2)
+        share = wbuf.shape[-2] // 2
+        front_part(
+            ltiles, tiles, point, place, nm_ref, wbuf.at[slot, :, :, 0:share],
+            wbuf.at[slot, :, :, share : 2 * share], pairs, pc_ref, gp, inn, dp, ip, st, pr, mix,
+            exchange.mine.at[step - 1], cv_ref, cl_ref,
+        )
+        for g in range(groups):
+
+            @pl.when(step == g + 1)
+            def _(g=g):
+                if g + 2 < groups:
+                    load(g + 2).start()
+                exchange.theirs[g, place] = jnp.zeros(exchange.theirs.shape[2:], F32)
+                exchange.start(g)
+
+        point(3)
+
+    @pl.when(step == groups)
+    def _():
+        width = gp.shape[1]
+        for g in range(groups):
+            state = exchange.entering(g, False)
+            sin_ref[:, g * width : (g + 1) * width] = jnp.broadcast_to(state, (8, width))
+        exchange.drain(groups)
+        if gather is not None:
+            gather.drain()
+
+
+def front_part(
+    ltiles, tiles, point, place, nm_ref, wg_ref, wi_ref, pairs, pc_ref, gp_ref, in_ref, dp_ref,
+    ip_ref, st_ref, pr_ref, mix_ref, end_ref, cv_ref, cl_ref,
+):
+    point(0)
     nm = nm_ref[...]
     gp_ref[...] = dot_nt(nm, flat(wg_ref[...])) + pc_ref[GB : GB + 1, :]
     in_ref[...] = dot_nt(nm, flat(wi_ref[...])) + pc_ref[IB : IB + 1, :]
     point(1)
-    in_ref[0:HALO, :] = in_ref[0:HALO, :] * first_ref[0, 0]
+    in_ref[0:HALO, :] = in_ref[0:HALO, :] * jnp.where(place > 0, 1.0, 0.0)
     cl_ref[0:HALO, :] = jnp.zeros((HALO, cl_ref.shape[1]), BF16)
 
     @pl.loop(1, tiles)
@@ -529,8 +667,8 @@
 
     point(2)
     low = cl_ref[...]
-    dp_ref[...] = dot_nn(low, wd_ref[0]) + pc_ref[DB : DB + 1, :]
-    ip_ref[...] = dot_nn(low, wo_ref[0]) + pc_ref[OB : OB + 1, :]
+    dp_ref[...] = dot_nn(low, pairs[0]) + pc_ref[DB : DB + 1, :]
+    ip_ref[...] = dot_nn(low, pairs[1]) + pc_ref[OB : OB + 1, :]
 
     def scanned(j):
         _, opening, a, square = gates(dp_ref[at(j), :], ip_ref[at(j), :], pc_ref[C8 : C8 + 1, :])
@@ -562,12 +700,6 @@
         return s[TILE - 1 : TILE]
 
     lax.fori_loop(0, tiles - 1 - ltiles, short_step, jnp.zeros((1, width), F32))
-    point(3)
-    if gather is not None:
-
-        @pl.when(step == pl.num_programs(0) - 1)
-        def _():
-            gather.drain()
 
 
 def mlp_kernel(ltiles, tiles, links, *refs):
@@ -578,12 +710,15 @@
     point, gather = no_point, None
     step = pl.program_id(0)
     last = pl.num_programs(0) - 1
-    out_ref, dres_ref, rlow_ref, mixl_ref, gain_grad_ref, dw_hbm = refs[:6]
-    refs = refs[6:]
     if links is not None:
         zcount, chunks, lags, plan = links
-        own_ref, w2_ref = w2_ref, refs[0]
-        gather = Gather(zcount, [own_ref], [w2_ref], refs[-3:], chunks, lags)
+        owns = [w2_ref, *refs[:2]]
+        refs = refs[2:]
+    outl_ref, outs_ref, dres_ref, rlow_ref, mixl_ref, gain_grad_ref, dw_hbm = refs[:7]
+    refs = refs[7:]
+    if links is not None:
+        w2_ref = refs[0]
+        gather = Gather(zcount, owns, [w2_ref], refs[-3:], chunks, lags)
         got_ref, sems, credit = refs[-6], refs[-5], refs[-4]
         refs = refs[1:-6]
         point = in_turn(gather, step, plan)
@@ -732,7 +867,6 @@
     def _():
         def one(i, total):
             r = dres_ref[at(i), :]
-            out_ref[at(i), :] = acc_o[at(i), :].astype(BF16)
             dn = acc_n[at(i), :]
             s = lax.rsqrt(jnp.mean(r * r, axis=1, keepdims=True) + EPSILON)
             e = dn * gain_ref[...]
@@ -743,6 +877,8 @@
             return total + fold(dn * (r * s))
 
         gain_grad_ref[...] = lax.fori_loop(0, tiles, one, jnp.zeros(gain_grad_ref.shape, F32))
+        outl_ref[...] = acc_o[0:lrows, :].astype(BF16)
+        outs_ref[...] = acc_o[lrows:, :].astype(BF16)
         settle(steps - 1)
         clear(steps - 1)
         if gather is not None:
@@ -811,9 +947,9 @@
 
 
 def last_part(
-    ltiles, tiles, groups, point, exchange, residual, first_ref, x_ref, gain_ref, nm_ref,
-    wg_ref, wi_ref, wd_ref, wo_ref, pc_ref, in_ref, dp_ref, ip_ref, st_ref, pr_ref, sin_ref,
-    tot_ref, rch_ref, gl_ref, bias_ref, dx_ref, halo_ref, gain_grad_ref, dwg_ref, dwi_ref,
+    ltiles, tiles, groups, point, exchange, residual, x_ref, gain_ref, nm_ref, wg_ref, wi_ref,
+    wd_ref, wo_ref, pc_ref, in_ref, dp_ref, ip_ref, st_ref, pr_ref, sin_ref, tot_ref, rch_ref,
+    gl_ref, bias_ref, dxl_ref, dxs_ref, halo_ref, behind, pairs, gain_grad_ref, dwg_ref, dwi_ref,
     gg_ref, small_ref, acc, dc_ref, cl_ref, dl_ref, ol_ref, il_ref, gain2_ref, free, keep,
 ):
     width = in_ref.shape[1]
@@ -829,8 +965,12 @@
 
     @pl.when(step == groups - 1)
     def _():
-        residual.start()
-
+        for copy in residual:
+            copy.start()
+
+    first = jnp.where(exchange.place > 0, 1.0, 0.0)
+    pair_up(pairs.at[0], wd_ref)
+    pair_up(pairs.at[1], wo_ref)
     zero8 = jnp.zeros((8, width), F32)
     cl_ref[0:HALO, :] = jnp.zeros((HALO, width), BF16)
     dl_ref[0:HALO, :] = jnp.zeros((HALO, width), BF16)
@@ -891,7 +1031,7 @@
         place = (which, step // 2, lax.rem(step, 2))
         gg_ref[(*place, slice(0, 2))] = product[:half, :half].reshape(shape)
         gg_ref[(*place, slice(2, 4))] = product[half:, half:].reshape(shape)
-    dc_ref[...] += dot_nt(dlow, wd_ref[0]) + dot_nt(olow, wo_ref[0])
+    dc_ref[...] += dot_nt(dlow, pairs[0]) + dot_nt(olow, pairs[1])
 
     point(2)
 
@@ -905,7 +1045,7 @@
         d_in = pc_ref[CW : CW + 1, :] * cur
         for k in range(1, 4):
             d_in = d_in + pc_ref[CW + k : CW + k + 1, :] * shift_up(cur, later, k)
-        d_in = d_in * jnp.where(j == 0, first_ref[0, 0], 1.0)
+        d_in = d_in * jnp.where(j == 0, first, 1.0)
         il_ref[at(j), :] = d_in.astype(BF16)
         return (
             sum_c + fold(cur),
@@ -942,7 +1082,8 @@
 
     @pl.when(step == groups - 1)
     def _():
-        residual.wait()
+        for copy in residual:
+            copy.wait()
 
         def norm_back(j):
             v = x_ref[at(j), :].astype(F32)
@@ -954,13 +1095,18 @@
 
         halo, total = norm_back(0)
         halo_ref[...] = halo
-
-        def one(i, total):
-            d, part = norm_back(1 + i)
-            dx_ref[at(i), :] = dx_ref[at(i), :] + d
-            return total + part
-
-        gain_grad_ref[...] = lax.fori_loop(0, tiles - 1, one, total)
+        behind.start()
+        done = 1
+        for ref in (dxl_ref, dxs_ref):
+
+            def one(i, total, ref=ref, done=done):
+                d, part = norm_back(done + i)
+                ref[at(i), :] = ref[at(i), :] + d
+                return total + part
+
+            total = lax.fori_loop(0, ref.shape[0] // TILE, one, total)
+            done += ref.shape[0] // TILE
+        gain_grad_ref[...] = total
         zero = jnp.zeros((8, 128), F32)
         for h in range(2):
             for z in range(4):
@@ -973,76 +1119,16 @@
     point(5)
 
 
-class Exchange:
-    def __init__(self, mine, theirs, ssem, rsem):
-        self.mine, self.theirs, self.ssem, self.rsem = mine, theirs, ssem, rsem
-        self.count = lax.axis_size("seq")
-        self.place = lax.axis_index("seq")
-
-    def peer(self, k):
-        return (lax.rem(self.place + k, self.count), lax.axis_index("row"))
-
-    def go(self, g, act):
-        for k in range(1, self.count):
-            act(
-                remote(
-                    self.mine.at[g],
-                    self.theirs.at[g, self.place],
-                    self.ssem.at[g, k - 1],
-                    self.rsem.at[g, k - 1],
-                    self.peer(k),
-                )
-            )
-
-    def start(self, g):
-        self.go(g, lambda d: d.start())
-
-    def entering(self, g, reverse):
-        self.go(g, lambda d: d.wait_recv())
-        state = jnp.zeros((1, self.mine.shape[-1]), F32)
-        for hop in range(self.count - 1):
-            source = self.count - 1 - hop if reverse else hop
-            ahead = source > self.place if reverse else source < self.place
-            reach = self.theirs[g, source, 0:1, :]
-            drive = self.theirs[g, source, 1:2, :]
-            state = jnp.where(ahead, reach * state + drive, state)
-        return state
-
-    def drain(self, groups):
-        for g in range(groups):
-            self.go(g, lambda d: d.wait_send())
-
-
-def exchange_scratch(groups, width, count):
-    links = pltpu.SemaphoreType.DMA((groups, count - 1))
-    return [
-        pltpu.VMEM((groups, 8, width), F32),
-        pltpu.VMEM((groups, count, 8, width), F32),
-        links, links,
-    ]
-
-
-def meet_all(exchange, zcount):
-    place, row = exchange.place, lax.axis_index("row")
-    everyone = [exchange.peer(k) for k in range(1, exchange.count)]
-    everyone += [(place, lax.rem(row + k, zcount)) for k in range(1, zcount)]
-    barrier = pltpu.get_barrier_semaphore()
-    for peer in everyone:
-        pl.semaphore_signal(barrier, inc=1, device_id=peer, device_id_type=pl.DeviceIdType.MESH)
-    pl.semaphore_wait(barrier, len(everyone))
-
-
 def tail_kernel(ltiles, tiles, groups, links, *refs):
     (
-        first_ref, x_ref, gain_ref, nm_ref, dres_hbm, rlow_ref, w_ref, wg_ref, wi_ref, wd_ref,
-        wo_ref, pc_ref, mixl_ref, mixs_ref, gp_ref, in_ref, dp_ref, ip_ref, st_ref, pr_ref, sin_ref,
+        x_ref, gain_ref, nm_ref, dres_hbm, rlow_ref, w_ref, wg_ref, wi_ref, wd_ref, wo_ref, pc_ref,
+        mixl_ref, mixs_ref, gp_ref, in_ref, dp_ref, ip_ref, st_ref, pr_ref, sin_ref, gain2_ref,
     ) = refs[:21]
-    gain2_ref = refs[21]
-    refs = refs[22:]
+    refs = refs[21:]
     step = pl.program_id(0)
     group = lax.rem(step, groups)
     back_point, last_point, scatter = no_point, no_point, None
-    nscratch = 19
+    nscratch = 23
     if links is not None:
         zcount, chunks, lags, plan = links
         halved_ref, refs = refs[0], refs[1:]
@@ -1050,10 +1136,10 @@
         scratch, pool = refs[14 : 14 + nscratch], refs[14 + nscratch :]
     else:
         outs, scratch = refs[:8], refs[8:]
-    dx_ref, halo_ref, gain_grad_ref, dwo_hbm, dwg_hbm, dwi_hbm, gates_hbm, sums_hbm = outs
+    dxl_ref, dxs_ref, gain_grad_ref, dwo_hbm, dwg_hbm, dwi_hbm, gates_hbm, sums_hbm = outs
     (
         acc, dc_ref, cl_ref, dl_ref, ol_ref, il_ref, gls, tots, rchs, bias_ref, wst, gsrc, ssrc,
-        dsem, wsem, *swap
+        pairs, halo_out, halo_in, hsem, dsem, wsem, *swap
     ) = scratch
     gates_full, sums_full = gsrc, ssrc
     if links is not None:
@@ -1083,7 +1169,16 @@
 
     exchange = Exchange(*swap)
     gl_ref, tot_ref, rch_ref = gls.at[group], tots.at[group], rchs.at[group]
-    residual = pltpu.make_async_copy(dres_hbm, dx_ref, dsem)
+    lrows = ltiles * TILE
+    residual = [
+        pltpu.make_async_copy(dres_hbm.at[pl.ds(0, lrows)], dxl_ref, dsem.at[0]),
+        pltpu.make_async_copy(
+            dres_hbm.at[pl.ds(lrows, dxs_ref.shape[0])], dxs_ref, dsem.at[1]
+        ),
+    ]
+    behind = remote(
+        halo_out, halo_in, hsem.at[0], hsem.at[1], exchange.peer(exchange.count - 1)
+    )
     width = gp_ref.shape[1]
 
     @pl.when(step == 0)
@@ -1125,16 +1220,19 @@
                 stash(g, 2, dwi_hbm).wait()
 
         last_part(
-            ltiles, tiles, groups, last_point, exchange, residual, first_ref, x_ref, gain_ref, nm_ref,
+            ltiles, tiles, groups, last_point, exchange, residual, x_ref, gain_ref, nm_ref,
             wg_ref, wi_ref, wd_ref, wo_ref, pc_ref, in_ref, dp_ref, ip_ref, st_ref, pr_ref, sin_ref,
-            tot_ref, rch_ref, gl_ref, bias_ref.at[group], dx_ref, halo_ref, gain_grad_ref,
-            wst.at[1], wst.at[2], gsrc, ssrc, acc, dc_ref, cl_ref, dl_ref, ol_ref, il_ref, gain2_ref,
+            tot_ref, rch_ref, gl_ref, bias_ref.at[group], dxl_ref, dxs_ref, halo_out, behind, pairs,
+            gain_grad_ref, wst.at[1], wst.at[2], gsrc, ssrc, acc, dc_ref, cl_ref, dl_ref, ol_ref, il_ref, gain2_ref,
             lambda: stashed(groups, before), lambda: stashed(groups, after),
         )
 
     @pl.when(step == pl.num_programs(0) - 1)
     def _():
         exchange.drain(groups)
+        behind.wait()
+        rows = slice(lrows - HALO, lrows)
+        dxl_ref[rows, :] = dxl_ref[rows, :] + halo_in[...]
         if scatter is not None:
             scatter.drain()
         final = [
@@ -1155,27 +1253,10 @@
     return pl.BlockSpec(shape, lambda g: (0,) * len(shape), pipeline_mode=pl.Buffered(1))
 
 
-def kept(shape):
-    return pl.BlockSpec(shape, lambda g: (0,) * len(shape))
-
-
-def columns(rows, width):
-    return pl.BlockSpec((rows, width), lambda g: (0, g))
-
-
 def params(limit, **more):
     return pltpu.CompilerParams(
         dimension_semantics=("arbitrary",), vmem_limit_bytes=int(limit * MIB), **more
     )
-
-
-def pair_blocks(weight):
-    blocks, width, _ = weight.shape
-    pairs = weight.reshape(blocks // 2, 2, width, width)
-    zero = jnp.zeros_like(pairs[:, 0])
-    top = jnp.concatenate([pairs[:, 0], zero], axis=2)
-    low = jnp.concatenate([zero, pairs[:, 1]], axis=2)
-    return jnp.concatenate([top, low], axis=1)
 
 
 def to_slots(parts, count):
@@ -1197,24 +1278,6 @@
     own = lax.psum_scatter(flat_grads, ("seq", "row"), scatter_dimension=0, tiled=True)
     own = own.astype(F32).reshape(number, -1, depth)
     return [own[i] for i in range(number)]
-
-
-def entering(ends, reverse):
-    count = lax.axis_size("seq")
-    place = lax.axis_index("seq")
-    got = lax.all_gather(ends, "seq")
-    state = jnp.zeros_like(ends[0])
-    for hop in range(count - 1):
-        source = count - 1 - hop if reverse else hop
-        ahead = source > place if reverse else source < place
-        state = jnp.where(ahead, got[source, 0] * state + got[source, 1], state)
-    return jnp.broadcast_to(state[None], (8, state.shape[0]))
-
-
-def hop(value, axis, steps):
-    count = lax.axis_size(axis)
-    first, last = (max(0, -steps), min(count, count - steps))
-    return lax.ppermute(value, axis, [(source, source + steps) for source in range(first, last)])
 
 
 def shards(
@@ -1253,119 +1316,118 @@
     width = chans // groups
     per = SLOTS // groups
 
-    long_x = long_tokens.reshape(lrows, depth)
-    halo_x = hop(long_x[lrows - HALO :], "seq", 1)
-    pair_own = [gate_weight.T, input_weight.T]
+    zcount = lax.axis_size("row")
+    seqs = lax.axis_size("seq")
+    fast = seqs == 8 and count == SLOTS
+    hbm = pl.BlockSpec(memory_space=pl.ANY)
+    one_dma = pltpu.SemaphoreType.DMA
+    hshare = ushare // 2
+    blocks, bwidth = decay_gate_weight.shape[0:2]
     mlp_own = [mlp_gate_weight.T, mlp_up_weight.T, mlp_down_weight]
-    zcount = lax.axis_size("row")
-    fast = lax.axis_size("seq") == 8 and count == SLOTS
-    hbm = pl.BlockSpec(memory_space=pl.ANY)
+    channel = [
+        gate_bias, input_bias, conv_weight, conv_bias, decay_gate_bias, input_gate_bias,
+        8.0 * jax.nn.softplus(decay_param), 8.0 * jax.nn.sigmoid(decay_param),
+    ]
+    channel = [c.reshape(-1, chans) for c in channel]
+    gain1 = first_gain[None]
+    gain2 = second_gain[None]
+
+    def early(g):
+        return jnp.minimum(g, groups - 1)
+
+    def after_one(g):
+        return jnp.maximum(g - 1, 0)
+
+    def late(g):
+        return jnp.maximum(g - groups, 0)
+
+    def both_times(g):
+        return lax.rem(g, groups)
+
+    def slot_at(when, which=0):
+        return pl.BlockSpec((per, cshare, depth), lambda g: (when(g), which, 0))
+
+    def blocks_at(when):
+        return pl.BlockSpec((2, bwidth, bwidth), lambda g: (when(g), 0, 0))
+
+    def cols_at(nrows, when):
+        return pl.BlockSpec((nrows, width), lambda g: (0, when(g)))
+
+    lags = (2, 2, 3, 2)
     if fast:
-        (pairw,) = gather_call([jnp.concatenate(pair_own, axis=0)], zcount)
-        hshare = mlp_own[0].shape[0] // 2
-        mlp_first, mlp_second = [
-            jnp.concatenate([w[h * hshare : (h + 1) * hshare] for w in mlp_own]) for h in range(2)
+        front_own = [gate_weight.T, input_weight.T, out_weight, *mlp_own]
+        parts = [(0, 0, cshare, 0, 0), (1, 0, cshare, 0, cshare)]
+        ready = len(row_chunks(parts, 16)) + sum(lags)
+        parts += [(2, 0, cshare, 1, 0)]
+        parts += [(3 + k, 0, hshare, 2, k * hshare) for k in range(3)]
+        chunks = row_chunks(parts, 16)
+        plan = [[]] + spread_out(len(chunks) + sum(lags) + 1 - ready, 1, groups, 4)
+        plan = [[[ready + t for t in p] for p in row] for row in plan]
+        front_links = (zcount, chunks, lags, ready, plan)
+        front_shapes = [
+            shape_of(GRID + (n, depth), BF16) for n in (2 * cshare, cshare, 3 * hshare)
         ]
-        front_own = [out_weight, mlp_first]
-        front_chunks = row_chunks(front_own, 16)
-        lags = (2, 2, 3, 2)
-        plan = spread_out(len(front_chunks) + sum(lags) + 1, 2, 4, 4)
-        front_links = (zcount, front_chunks, lags, plan, len(front_own))
-        front_extra = dict(
-            specs=[hbm] * 2,
-            shapes=[gathered(w, zcount) for w in front_own],
-            scratch=gather_sems(len(front_chunks), zcount),
-            params=dict(collective_id=2, has_side_effects=True),
-        )
+        front_scratch = gather_sems(len(chunks), zcount)
     else:
-        pairw = to_slots(pair_own, count)
+        pairw = to_slots([gate_weight.T, input_weight.T], count)
         outw = to_slots([out_weight], count)
         mlpw = to_slots(mlp_own, count).reshape(GRID + (3, 2, -1, depth))
         w_first, w_second = [mlpw[..., h, :, :].reshape(GRID + (-1, depth)) for h in range(2)]
-        front_own, front_links = [], None
-        front_extra = dict(specs=[], shapes=[], scratch=[], params={})
-    pairw = pairw.reshape(SLOTS, -1, depth)
-    x = jnp.concatenate([halo_x, long_x, short_tokens.reshape(srows, depth)], axis=0)
-    place = lax.axis_index("seq")
-    first = jnp.where(place > 0, 1.0, 0.0).astype(F32).reshape(1, 1)
-    positions = place * lrows + jnp.arange(lrows, dtype=jnp.int32)
-    keep = positions[:, None] < long_length[0]
-    masked = jnp.where(keep, long_cotangent.reshape(lrows, depth), jnp.zeros((), BF16))
-    cot = jnp.concatenate([masked, short_cotangent.reshape(srows, depth)], axis=0)
-    chan = jnp.concatenate(
-        [
-            jnp.stack([gate_bias, input_bias]),
-            conv_weight,
-            jnp.stack(
-                [
-                    conv_bias,
-                    decay_gate_bias,
-                    input_gate_bias,
-                    8.0 * jax.nn.softplus(decay_param),
-                    8.0 * jax.nn.sigmoid(decay_param),
-                ]
-            ),
-            jnp.zeros((5, chans), F32),
-        ],
-        axis=0,
-    )
-    pair_d = pair_blocks(decay_gate_weight)
-    pair_o = pair_blocks(input_gate_weight)
-    gain1 = first_gain[None]
-    gain2 = second_gain[None]
-    scalar = pl.BlockSpec(memory_space=pltpu.SMEM)
-
-    def mix_part(which):
-        return pl.BlockSpec((per, cshare, depth), lambda g: (g, which, 0))
-
-    pair_spec = pl.BlockSpec((1, width, width), lambda g: (g, 0, 0))
-    col = columns(total, width)
-    col_long = columns(HALO + lrows, width)
-    pc_spec = columns(16, width)
-    col8 = columns(8, width)
-
+        front_own = [pairw.reshape(GRID + (-1, depth))]
+        front_links, front_shapes, front_scratch = None, [], []
+
+    col = cols_at(total, after_one)
     wide = shape_of((total, chans), F32)
     narrow = shape_of((HALO + lrows, chans), F32)
-    gp, inner, dp, ip, states, reach, mix_s, ends, normed, *wide_w = pl.pallas_call(
-        functools.partial(front_kernel, ltiles, tiles, front_links),
-        grid=(groups,),
+    gp, inner, dp, ip, states, reach, mix_s, s_in, normed, x, cot, chan, *made = pl.pallas_call(
+        functools.partial(front_kernel, ltiles, tiles, groups, front_links),
+        grid=(1 + groups,),
         in_specs=[
-            scalar, whole((total, depth)), whole((1, depth)), mix_part(0), mix_part(1),
-            pair_spec, pair_spec, pc_spec, *front_extra["specs"],
+            hbm, hbm, hbm, hbm, pl.BlockSpec(memory_space=pltpu.SMEM), whole((1, depth)),
+            *[cols_at(c.shape[0], after_one) for c in channel], blocks_at(after_one),
+            blocks_at(after_one), *[hbm for _ in front_own],
         ],
         out_specs=[
-            col, col, col, col, col, col_long, columns(srows, width), col8,
-            kept((total, depth)), *front_extra["specs"],
+            col, col, col, col, col, cols_at(HALO + lrows, after_one), cols_at(srows, after_one),
+            whole((8, chans)), whole((total, depth)), whole((total, depth)),
+            whole((tokens, depth)), cols_at(16, after_one), *[hbm for _ in front_shapes],
         ],
         out_shape=[
             wide, wide, wide, wide, wide, narrow, shape_of((srows, chans), BF16),
-            shape_of((8, chans), F32), shape_of((total, depth), BF16), *front_extra["shapes"],
+            shape_of((8, chans), F32), shape_of((total, depth), BF16),
+            shape_of((total, depth), BF16), shape_of((tokens, depth), BF16),
+            shape_of((16, chans), F32), *front_shapes,
         ],
         scratch_shapes=[
             pltpu.VMEM((total, width), F32), pltpu.VMEM((total, width), BF16),
-            *front_extra["scratch"],
+            pltpu.VMEM((2,) + GRID[2:] + (2 * cshare, depth), BF16),
+            pltpu.VMEM((2, width, width), BF16), pltpu.VMEM((HALO, depth), BF16),
+            one_dma((4,)), one_dma((2,)), one_dma((2,)), *exchange_scratch(groups, width, seqs),
+            *front_scratch,
         ],
-        compiler_params=params(48, **front_extra["params"]),
+        compiler_params=params(56, collective_id=0, has_side_effects=True),
         name="front",
-    )(first, x, gain1, pairw, pairw, pair_d, pair_o, chan, *front_own)
+    )(
+        long_tokens.reshape(lrows, depth), short_tokens.reshape(srows, depth),
+        long_cotangent.reshape(lrows, depth), short_cotangent.reshape(srows, depth), long_length,
+        gain1, *channel, decay_gate_weight, input_gate_weight, *front_own,
+    )
     if fast:
-        outw, w_first = wide_w
-        outw = outw.reshape(SLOTS, -1, depth)
-
-    s_in = entering(ends[0:2], False)
+        pairw, outw, w_first = made
+    outw = outw.reshape(SLOTS, -1, depth)
+    pairw = pairw.reshape(SLOTS, -1, depth)
 
     steps = 4
     hid = units // steps
     block = GRID[1:] + (3 * ushare // 2, depth)
     wbuf = pltpu.VMEM((2,) + block, BF16)
     dwbuf = pltpu.VMEM(block, BF16)
-    one_dma = pltpu.SemaphoreType.DMA
     if fast:
-        chunks = row_chunks([mlp_second], 16)
+        chunks = row_chunks([(k, hshare, hshare, 0, k * hshare) for k in range(3)], 16)
         waves = len(chunks) + sum(lags) + 1
         plan = spread_out(waves, 3, 3, 8)
         mlp_links = (zcount, chunks, lags, plan)
-        w_last, more_specs, more_shapes = mlp_second, [hbm], [gathered(mlp_second, zcount)]
+        w_last, more_specs, more_shapes = mlp_own, [hbm], [shape_of(w_first.shape, BF16)]
         half_block = (block[0],) + block[2:]
         more_scratch = [
             pltpu.VMEM(half_block, BF16), one_dma((2,)), pltpu.SemaphoreType.REGULAR,
@@ -1374,23 +1436,25 @@
         dw_shape = (2, 2) + half_block
         more_params = dict(collective_id=3, has_side_effects=True)
     else:
-        mlp_links, w_last, more_specs, more_shapes, more_scratch = None, w_second, [], [], []
+        mlp_links, w_last, more_specs, more_shapes, more_scratch = None, [w_second], [], [], []
         dw_shape, more_params = (2, 2) + block, {}
-    out, d_res, rlow, mix_l, gain2_grad, dmlp, *_ = pl.pallas_call(
+    out_l, out_s, d_res, rlow, mix_l, gain2_grad, dmlp, *_ = pl.pallas_call(
         functools.partial(mlp_kernel, ltiles, tokens // TILE, mlp_links),
         grid=(steps,),
         in_specs=[
             whole((total, depth)), whole((tokens, depth)), whole((HALO + lrows, chans)),
             whole((HALO + lrows, chans)), whole((HALO + lrows, chans)), whole((8, chans)),
-            whole((srows, chans)), whole((SLOTS, cshare, depth)), whole((1, depth)), hbm, hbm,
+            whole((srows, chans)), whole((SLOTS, cshare, depth)), whole((1, depth)), hbm,
+            *[hbm for _ in w_last],
         ],
         out_specs=[
-            whole((tokens, depth)), whole((tokens, depth)), whole((tokens, depth)),
+            whole((lrows, depth)), whole((srows, depth)), whole((tokens, depth)), whole((tokens, depth)),
             whole((lrows, chans)), whole((8, depth)), hbm, *more_specs,
         ],
         out_shape=[
-            shape_of((tokens, depth), BF16), shape_of((tokens, depth), F32),
-            shape_of((tokens, depth), BF16), shape_of((lrows, chans), BF16),
+            shape_of((lrows, depth), BF16), shape_of((srows, depth), BF16),
+            shape_of((tokens, depth), F32), shape_of((tokens, depth), BF16),
+            shape_of((lrows, chans), BF16),
             shape_of((8, depth), F32), shape_of(dw_shape, BF16), *more_shapes,
         ],
         scratch_shapes=[
@@ -1402,34 +1466,13 @@
         ],
         compiler_params=params(62, **more_params),
         name="mlp",
-    )(x, cot, states, reach, gp, s_in, mix_s, outw, gain2, w_first, w_last)
-
-    slot_shape = shape_of((SLOTS, cshare, depth), BF16)
-    blocks, bwidth = decay_gate_weight.shape[0:2]
-
-    def early(g):
-        return jnp.minimum(g, groups - 1)
-
-    def late(g):
-        return jnp.maximum(g - groups, 0)
-
-    def both_times(g):
-        return lax.rem(g, groups)
-
-    def slot_at(when, which=0):
-        return pl.BlockSpec((per, cshare, depth), lambda g: (when(g), which, 0))
-
-    def pair_at(when):
-        return pl.BlockSpec((1, width, width), lambda g: (when(g), 0, 0))
-
-    def cols_at(nrows, when):
-        return pl.BlockSpec((nrows, width), lambda g: (0, when(g)))
+    )(x, cot, states, reach, gp, s_in, mix_s, outw, gain2, w_first, *w_last)
 
     gate_shape, sum_shape = GRID + (bwidth // 2, bwidth), GRID + (8, 128)
     grads_shape = shape_of(GRID + (cshare, depth), BF16)
     tail_links, tail_in, tail_specs, tail_shapes, tail_scratch = None, [], [], [], []
     if fast:
-        size, hshare = 16, ushare // 2
+        size = 16
         tail_chunks = []
         number = 0
         for h in range(2):
@@ -1470,24 +1513,24 @@
             one_dma((n,)), links, links, links, links,
             pltpu.VMEM(gate_shape, BF16), pltpu.VMEM(sum_shape, F32),
         ]
-    d_x, d_halo, _, d_out, d_gate, d_input, gate_sums, sums, *shares = pl.pallas_call(
+    dx_l, dx_s, _, d_out, d_gate, d_input, gate_sums, sums, *shares = pl.pallas_call(
         functools.partial(tail_kernel, ltiles, tiles, groups, tail_links),
         grid=(2 * groups,),
         in_specs=[
-            scalar, whole((total, depth)), whole((1, depth)), whole((total, depth)), hbm,
+            whole((total, depth)), whole((1, depth)), whole((total, depth)), hbm,
             whole((tokens, depth)), slot_at(early), slot_at(late, 0), slot_at(late, 1),
-            pair_at(late), pair_at(late), cols_at(16, both_times), cols_at(lrows, early),
+            blocks_at(late), blocks_at(late), cols_at(16, both_times), cols_at(lrows, early),
             cols_at(srows, early), cols_at(total, early), cols_at(total, late),
             cols_at(total, both_times), cols_at(total, late), cols_at(total, both_times),
             cols_at(HALO + lrows, both_times), cols_at(8, both_times), whole((8, depth)),
             *[hbm for _ in tail_in],
         ],
         out_specs=[
-            whole((tokens, depth)), whole((HALO, depth)), whole((8, depth)), hbm, hbm, hbm, hbm, hbm,
+            whole((lrows, depth)), whole((srows, depth)), whole((8, depth)), hbm, hbm, hbm, hbm, hbm,
             *tail_specs,
         ],
         out_shape=[
-            shape_of((tokens, depth), F32), shape_of((HALO, depth), F32), shape_of((8, depth), F32),
+            shape_of((lrows, depth), F32), shape_of((srows, depth), F32), shape_of((8, depth), F32),
             grads_shape, grads_shape, grads_shape, shape_of(gate_shape, BF16),
             shape_of(sum_shape, F32), *tail_shapes,
         ],
@@ -1498,19 +1541,16 @@
             pltpu.VMEM((groups, total, width), BF16), pltpu.VMEM((groups, total, width), F32),
             pltpu.VMEM((groups, HALO + lrows, width), F32), pltpu.VMEM((groups, 8, width), F32),
             pltpu.VMEM((3,) + GRID[2:] + (cshare, depth), BF16), pltpu.VMEM(gate_shape, BF16),
-            pltpu.VMEM(sum_shape, F32), one_dma, one_dma((3,)),
-            *exchange_scratch(groups, width, lax.axis_size("seq")), *tail_scratch,
+            pltpu.VMEM(sum_shape, F32), pltpu.VMEM((2, width, width), BF16),
+            pltpu.VMEM((HALO, depth), F32), pltpu.VMEM((HALO, depth), F32), one_dma((2,)),
+            one_dma((2,)), one_dma((3,)), *exchange_scratch(groups, width, seqs), *tail_scratch,
         ],
         compiler_params=params(63, collective_id=4, has_side_effects=True),
         name="tail",
     )(
-        first, x, gain1, normed, d_res, rlow, outw, pairw, pairw, pair_d, pair_o, chan, mix_l, mix_s,
-        gp, inner, dp, ip, states, reach, s_in, gain2_grad, *tail_in,
+        x, gain1, normed, d_res, rlow, outw, pairw, pairw, decay_gate_weight, input_gate_weight, chan,
+        mix_l, mix_s, gp, inner, dp, ip, states, reach, s_in, gain2_grad, *tail_in,
     )
-
-    ahead = hop(d_halo, "seq", -1)
-    long_grad = d_x[:lrows].at[lrows - HALO :].add(ahead)
-    short_grad = d_x[lrows:]
 
     if fast:
         g_mgate, g_mup, g_down, g_out, g_gate, g_input = shares
@@ -1525,10 +1565,10 @@
     gain_sums = sums[0, 12:14].reshape(2, depth)
     rows = sums.transpose(0, 2, 1, 3).reshape(16, 2048)[0:10, :chans]
     return (
-        out[:lrows].reshape(long_tokens.shape),
-        out[lrows:].reshape(short_tokens.shape),
-        long_grad.reshape(long_tokens.shape),
-        short_grad.reshape(short_tokens.shape),
+        out_l.reshape(long_tokens.shape),
+        out_s.reshape(short_tokens.shape),
+        dx_l.reshape(long_tokens.shape),
+        dx_s.reshape(short_tokens.shape),
         gain_sums[0],
         g_gate.T,
         rows[9],

time: 442 us -> 413 us (0.934)
  blocking collectives: 9.46 us -> 0 us
  local copies, waits for them, and re-layouts: 31.9 us -> 23.7 us
  other arithmetic: 7.54 us -> 0.71 us
    all_gather x1 -> x0, blocking collectives: 9.46 us -> none  [entering(): got = lax.all_gather(ends, 'seq')]
    slice x4 -> x0, local copies, waits for them, and re-layouts: 6.46 us -> none  [the longest x3 5.01 us: shards(): w[h * hshare:(h + 1) * hshare]]
    concatenate x5 -> x0, other arithmetic: 5.65 us -> none  [the longest x1 2.42 us: shards(): jnp.concatenate([halo_x, long_x, short_tokens.reshape(srows, depth)], axi...]
    pallas_call x2 -> x1, Pallas kernels: 113 us -> 113 us  [shards(): pl.pallas_call(functools.partial(front_kernel, ltiles, tiles, groups, fro...]
  transfers between devices with their start and end apart: 2 -> 0, of which waited for: 0 -> 0; matrix products, arithmetic and copies ran while one was open for 4% -> 0% of each run, Pallas kernels for 10% -> 0%
where the time goes in v6:
time: 413 us; the launch traced here: 412 us
  Pallas kernels  386 us (93%)
  local copies, waits for them, and re-layouts  23.7 us (6%)
    pallas_call x1, Pallas kernels, shards(): pl.pallas_call(functools.partial(tail_kernel, ltiles, tiles, groups, tail...  166 us
    pallas_call x1, Pallas kernels, shards(): pl.pallas_call(functools.partial(front_kernel, ltiles, tiles, groups, fro...  113 us
    pallas_call x1, Pallas kernels, shards(): pl.pallas_call(functools.partial(mlp_kernel, ltiles, tokens // TILE, mlp_...  107 us

profile of v6, /device:TPU:0, one launch (start us, length us, event | category | flops | bytes accessed | tf_op | source)
XLA Modules:
  0.0 412.0 jit_solution(11258556837479261220)
XLA Ops:
  1.3 1.3 reshape.113.refs_6_
  2.6 1.3 reshape.114.refs_7_
  3.9 1.3 reshape.115.refs_9_
  5.2 1.3 reshape.116.refs_10_
  6.5 1.3 reshape.117.refs_11_
  7.8 0.7 divide_multiply_fusion
  8.5 0.6 reshape.119.refs_13_
  9.1 0.6 reshape.118.refs_12_
  9.7 113.0 %front.1 = (f32[656,1536]{1,0:T(8,128)}, f32[656,1536]{1,0:T(8,128)}, f32[656,1536]{1,0:T(8,128)}, f32[656,1536]{1,0:T(8,128)}, f32[656,1536]{1,0:T(8,128)}, /*i...) custom-call(bf16[128,1024]{1,0:T(8,128)(2,1)} %bitcast.48, ...), custom_call_target="tpu_custom_call" | custom-call | tf_op jit(solution)/shard_map/front/pallas_call | solution.py:1382
  122.7 106.9 %mlp.1 = (bf16[128,1024]{1,0:T(8,128)(2,1)}, bf16[512,1024]{1,0:T(8,128)(2,1)}, f32[640,1024]{1,0:T(8,128)}, bf16[640,1024]{1,0:T(8,128)(2,1)}, bf16[128,1536]{1...) custom-call(bf16[656,1024]{1,0:T(8,128)(2,1)} %get-tuple-element.53., ...), custom_call_target="tpu_custom_call" | custom-call | tf_op jit(solution)/shard_map/mlp/pallas_call | solution.py:1441
  229.5 166.4 %tail.1 = (f32[128,1024]{1,0:T(8,128)}, f32[512,1024]{1,0:T(8,128)}, f32[8,1024]{1,0:T(8,128)}, bf16[2,2,2,4,48,1024]{5,4,3,2,1,0:T(8,128)(2,1)}, bf16[2,2,2,4,4...) custom-call(bf16[656,1024]{1,0:T(8,128)(2,1)} %get-tuple-element.53., ...), custom_call_target="tpu_custom_call" | custom-call | tf_op jit(solution)/shard_map/tail/pallas_call | solution.py:1516
  395.9 1.3 slice_bitcast_fusion
  397.2 1.4 slice.62
  398.6 1.7 slice_reduce_fusion
  400.3 3.5 fusion.1
  403.9 0.0 copy-done.6
  403.9 0.7 copy.54
  404.6 0.0 copy-done.1
  404.6 1.0 copy.55
  405.5 0.0 copy-done.2
  405.6 0.8 copy.56
  406.4 1.3 copy.57
  407.7 0.0 copy-done.9
  407.7 0.7 copy.58
  408.4 0.0 copy-done.8
  408.4 0.7 copy.59
  409.0 0.0 copy-done.7
  409.1 0.7 copy.60
  409.7 0.0 copy-done.5
  409.7 0.7 copy.61
  410.5 0.7 copy.62
  411.2 0.7 copy.63
  (13 shorter events, 0.0 us)
Async XLA Ops:
  400.3 3.5 copy-start.6
  400.3 4.2 %copy-start.1 = (bf16[512,1024]{1,0:T(8,128)(2,1)S(1)}, bf16[512,1024]{1,0:T(8,128)(2,1)}, u32[]{:S(2)}) copy-start(bf16[512,1024]{1,0:T(8,128)(2,1)} %get-tuple-element.63) | copy-start | bytes 3145732
  403.9 1.7 copy-start.2
  403.9 2.5 copy-start
  405.5 2.1 copy-start.9
  405.5 2.8 copy-start.8
  406.3 2.7 copy-start.7
  406.3 3.4 copy-start.5
  406.4 4.1 %copy-start.4 = (f32[96,1024]{1,0:T(8,128)S(1)}, f32[96,1024]{1,0:T(8,128)}, u32[]{:S(2)}) copy-start(f32[96,1024]{1,0:T(8,128)} %get-tuple-element.83) | copy-start | bytes 1179652
  406.4 4.9 %copy-start.3 = (f32[96,1024]{1,0:T(8,128)S(1)}, f32[96,1024]{1,0:T(8,128)}, u32[]{:S(2)}) copy-start(f32[96,1024]{1,0:T(8,128)} %get-tuple-element.138) | copy-start | bytes 1179652

commit v7 on v6

--- a/solution.py
+++ b/solution.py
@@ -15,6 +15,10 @@
 TILE = 16
 HALO = 16
 MIB = 1024 * 1024
+MLP_AHEAD = 1
+EARLY_PARTS = 2
+EARLY_GAP = 3
+FRONT_PARTS = 3
 TAIL_SLOTS = 10
 CORE_SLOTS = 5
 GELU_A = 0.7978845608028654
@@ -357,7 +361,7 @@
     def local(self):
         c = self.o.peers.place[2]
         if self.kind == HALVED:
-            mine = self.source.at[self.lead, :, :, :, self.rows]
+            mine = self.source.at[self.lead]
         else:
             mine = self.source.at[:, :, c, :, self.rows]
         return pltpu.make_async_copy(mine, self.a.at[self.slot], self.o.csem.at[self.i])
@@ -450,6 +454,12 @@
 def five(number, shape, dtype, zcount):
     lead = [(2, 2, zcount), (2, 2, zcount), (2, zcount), (zcount,), (zcount - 1,)]
     return [pltpu.VMEM((number, *d, *shape), dtype) for d in lead]
+
+
+def halved_scratch(count, slots, depth, zcount):
+    lone = five(slots, (16, depth), BF16, zcount)
+    links = pltpu.SemaphoreType.DMA((count, zcount + 2))
+    return [lone[0], *lone[2:], pltpu.SemaphoreType.DMA((count,)), links, links, links, links]
 
 
 def no_point(k):
@@ -711,30 +721,60 @@
     step = pl.program_id(0)
     last = pl.num_programs(0) - 1
     if links is not None:
-        zcount, chunks, lags, plan = links
+        zcount, chunks, lags, plan, sum_chunks, sum_lags, sum_plan = links
         owns = [w2_ref, *refs[:2]]
         refs = refs[2:]
     outl_ref, outs_ref, dres_ref, rlow_ref, mixl_ref, gain_grad_ref, dw_hbm = refs[:7]
     refs = refs[7:]
     if links is not None:
-        w2_ref = refs[0]
+        w2_ref, early_ref = refs[:2]
+        halved = (refs[-9], None, *refs[-8:-5])
+        buffers = [None, None, None, halved]
+        scatter = Scatter(zcount, [dw_hbm], [early_ref], buffers, refs[-5:], sum_chunks, sum_lags)
+        refs = refs[2:-9]
         gather = Gather(zcount, owns, [w2_ref], refs[-3:], chunks, lags)
         got_ref, sems, credit = refs[-6], refs[-5], refs[-4]
-        refs = refs[1:-6]
-        point = in_turn(gather, step, plan)
+        refs = refs[:-6]
+        gather_point = in_turn(gather, step, plan)
+        scatter_point = in_turn(scatter, step, sum_plan)
+
+        def point(k):
+            gather_point(k)
+            scatter_point(k)
+
     (
-        n2_ref, acc_o, acc_n, g_ref, u_ref, d_ref, h_ref, dg_ref, du_ref, wbuf, dwbuf, wsem, dsem
+        n2_ref, acc_o, acc_n, gu_ref, d_ref, h_ref, dgu_ref, wbuf, dwbuf, wsem, dsem
     ) = refs
     lrows = ltiles * TILE
-    half = g_ref.shape[1] // 2
-    share = wbuf.shape[-2] // 3
-    steps = 2 * GRID[0]
+    hid = h_ref.shape[1]
+    half = hid // 2
+    share = wbuf.shape[-2]
+    rows = 3 * share
+    ready = w1_ref.shape[-2] // rows
+    steps = ready + w2_ref.shape[-2] // rows
 
     def load(s):
-        source = w1_ref if s < steps // 2 else w2_ref
-        return pltpu.make_async_copy(
-            source.at[s % (steps // 2)], wbuf.at[s % 2], wsem.at[s % 2]
-        )
+        source, part = (w1_ref, s) if s < ready else (w2_ref, s - ready)
+        return [
+            pltpu.make_async_copy(
+                source.at[:, :, :, :, pl.ds(part * rows + k * share, share)],
+                wbuf.at[s % 2, k],
+                wsem.at[s % 2, k],
+            )
+            for k in range(3)
+        ]
+
+    def start_load(s):
+        for copy in load(s):
+            copy.start()
+
+    def wait_load(s):
+        for copy in load(s):
+            copy.wait()
+
+    def load_next(s):
+        if s + 1 < steps and s + 1 >= min(2, ready):
+            start_load(s + 1)
 
     def each(todo, first=0):
         for s in range(first, steps):
@@ -747,24 +787,24 @@
         y, x, c, z = gather.peers.place
 
     def store(s):
-        h, q = s // (steps // 2), s % (steps // 2)
-        mine = dwbuf if gather is None else dwbuf.at[:, c]
-        return pltpu.make_async_copy(mine, dw_hbm.at[h, q], dsem)
+        mine = dwbuf if gather is None else dwbuf.at[:, :, :, c]
+        return pltpu.make_async_copy(mine, dw_hbm.at[s], dsem)
 
     def swap():
         return remote(
-            dwbuf.at[:, 1 - c], got_ref, sems.at[0], sems.at[1], gather.peers.other
+            dwbuf.at[:, :, :, 1 - c], got_ref, sems.at[0], sems.at[1], gather.peers.other
         )
 
     def settle(s):
         if gather is not None:
             swap().wait_recv()
 
-            @pl.loop(0, got_ref.shape[0] * got_ref.shape[1])
+            @pl.loop(0, SLOTS // 2)
             def _(k):
-                i, j = k // got_ref.shape[1], k % got_ref.shape[1]
-                both = dwbuf[i, c, j].astype(F32) + got_ref[i, j].astype(F32)
-                dwbuf[i, c, j] = both.astype(BF16)
+                i, j, m = k // (2 * GRID[3]), (k // GRID[3]) % 2, k % GRID[3]
+                for n in range(3):
+                    both = dwbuf[n, i, j, c, m].astype(F32) + got_ref[n, i, j, m].astype(F32)
+                    dwbuf[n, i, j, c, m] = both.astype(BF16)
 
             if s < steps - 1:
                 pl.semaphore_signal(
@@ -782,8 +822,8 @@
 
     @pl.when(step == 0)
     def _():
-        load(0).start()
-        load(1).start()
+        for s in range(min(2, ready)):
+            start_load(s)
         if gather is not None:
             gather.peers.meet()
 
@@ -814,21 +854,18 @@
 
     point(1)
 
-    @pl.when(step == steps // 2)
-    def _():
-        load(steps // 2).start()
-        load(steps // 2 + 1).start()
-
-    each(lambda s: load(s).wait())
+    each(wait_load)
     slot = lax.rem(step, 2)
-    n2 = n2_ref[...]
-    wg = flat(wbuf[slot, ..., 0:share, :])
-    wu = flat(wbuf[slot, ..., share : 2 * share, :])
-    wd = flat(wbuf[slot, ..., 2 * share :, :])
-    g_ref[...] = dot_nt(n2, wg)
-    u_ref[...] = dot_nt(n2, wu)
+
+    def gate_up():
+        return flat(wbuf[slot, 0:2])
+
+    def down():
+        return flat(wbuf[slot, 2])
+
+    gu_ref[...] = dot_nt(n2_ref[...], gate_up())
     point(2)
-    d_ref[...] = dot_nt(cot_ref[...], wd)
+    d_ref[...] = dot_nt(cot_ref[...], down())
     each(lambda s: settle(s - 1), 1)
     point(3)
 
@@ -836,25 +873,25 @@
     def _(i):
         for k in range(2):
             cols = slice(k * half, (k + 1) * half)
-            ge, slope = gelu_pair(g_ref[at(i), cols])
-            u = u_ref[at(i), cols]
+            more = slice(hid + k * half, hid + (k + 1) * half)
+            ge, slope = gelu_pair(gu_ref[at(i), cols])
+            u = gu_ref[at(i), more]
             d = d_ref[at(i), cols]
             h_ref[at(i), cols] = (ge * u).astype(BF16)
-            dg_ref[at(i), cols] = (d * u * slope).astype(BF16)
-            du_ref[at(i), cols] = (d * ge).astype(BF16)
+            dgu_ref[at(i), cols] = (d * u * slope).astype(BF16)
+            dgu_ref[at(i), more] = (d * ge).astype(BF16)
 
     point(4)
-    acc_o[...] += dot_nn(h_ref[...], wd)
-    acc_n[...] += dot_nn(dg_ref[...], wg) + dot_nn(du_ref[...], wu)
+    acc_o[...] += dot_nn(h_ref[...], down())
     point(5)
+    acc_n[...] += dot_nn(dgu_ref[...], gate_up())
+    point(6)
     each(lambda s: clear(s - 1), 1)
-    lead = dwbuf.shape[:-2]
-    rest = (share, dwbuf.shape[-1])
-    for k, (left, right) in enumerate(((dg_ref, n2_ref), (du_ref, n2_ref), (h_ref, cot_ref))):
-        grad = dot_tn(left[...], right[...]).astype(BF16)
-        dwbuf[..., k * share : (k + 1) * share, :] = grad.reshape(lead + rest)
-        if k < 2:
-            point(6 + k)
+    dwbuf[2] = dot_tn(h_ref[...], cot_ref[...]).astype(BF16).reshape(dwbuf.shape[1:])
+    point(7)
+    each(load_next)
+    grad = dot_tn(dgu_ref[...], n2_ref[...]).astype(BF16)
+    dwbuf[0:2] = grad.reshape((2,) + dwbuf.shape[1:])
 
     if gather is not None:
         @pl.when(step > 0)
@@ -881,8 +918,14 @@
         outs_ref[...] = acc_o[lrows:, :].astype(BF16)
         settle(steps - 1)
         clear(steps - 1)
-        if gather is not None:
+
+    point(8)
+    if gather is not None:
+
+        @pl.when(step == last)
+        def _():
             gather.drain()
+            scatter.drain()
 
 
 def back_part(
@@ -1131,7 +1174,7 @@
     nscratch = 23
     if links is not None:
         zcount, chunks, lags, plan = links
-        halved_ref, refs = refs[0], refs[1:]
+        halved_ref, early_ref, refs = refs[0], refs[1], refs[2:]
         outs, shares = refs[:8], refs[8:14]
         scratch, pool = refs[14 : 14 + nscratch], refs[14 + nscratch :]
     else:
@@ -1156,6 +1199,12 @@
         )
         back_point = in_turn(scatter, step, plan[:groups])
         last_point = in_turn(scatter, step, plan[groups:], groups)
+
+        @pl.when(step == 0)
+        def _():
+            rows = early_ref.shape[0] // 3
+            for k in range(3):
+                shares[k][0:rows, :] = early_ref[k * rows : (k + 1) * rows, :]
 
     def stash(g, k, target):
         return pltpu.make_async_copy(wst.at[k], target.at[g // 2, g % 2], wsem.at[k])
@@ -1321,7 +1370,8 @@
     fast = seqs == 8 and count == SLOTS
     hbm = pl.BlockSpec(memory_space=pl.ANY)
     one_dma = pltpu.SemaphoreType.DMA
-    hshare = ushare // 2
+    steps = ushare // 16
+    ready_parts = max(1, min(steps - 1, FRONT_PARTS))
     blocks, bwidth = decay_gate_weight.shape[0:2]
     mlp_own = [mlp_gate_weight.T, mlp_up_weight.T, mlp_down_weight]
     channel = [
@@ -1359,20 +1409,23 @@
         parts = [(0, 0, cshare, 0, 0), (1, 0, cshare, 0, cshare)]
         ready = len(row_chunks(parts, 16)) + sum(lags)
         parts += [(2, 0, cshare, 1, 0)]
-        parts += [(3 + k, 0, hshare, 2, k * hshare) for k in range(3)]
+        parts += [
+            (3 + k, 16 * p, 16, 2, 48 * p + 16 * k) for p in range(ready_parts) for k in range(3)
+        ]
         chunks = row_chunks(parts, 16)
         plan = [[]] + spread_out(len(chunks) + sum(lags) + 1 - ready, 1, groups, 4)
         plan = [[[ready + t for t in p] for p in row] for row in plan]
         front_links = (zcount, chunks, lags, ready, plan)
         front_shapes = [
-            shape_of(GRID + (n, depth), BF16) for n in (2 * cshare, cshare, 3 * hshare)
+            shape_of(GRID + (n, depth), BF16) for n in (2 * cshare, cshare, 48 * ready_parts)
         ]
         front_scratch = gather_sems(len(chunks), zcount)
     else:
         pairw = to_slots([gate_weight.T, input_weight.T], count)
         outw = to_slots([out_weight], count)
-        mlpw = to_slots(mlp_own, count).reshape(GRID + (3, 2, -1, depth))
-        w_first, w_second = [mlpw[..., h, :, :].reshape(GRID + (-1, depth)) for h in range(2)]
+        mlpw = to_slots(mlp_own, count).reshape(GRID + (3, steps, 16, depth))
+        mlpw = jnp.swapaxes(mlpw, 4, 5).reshape(GRID + (48 * steps, depth))
+        w_first, w_second = jnp.split(mlpw, [48 * ready_parts], axis=4)
         front_own = [pairw.reshape(GRID + (-1, depth))]
         front_links, front_shapes, front_scratch = None, [], []
 
@@ -1417,28 +1470,59 @@
     outw = outw.reshape(SLOTS, -1, depth)
     pairw = pairw.reshape(SLOTS, -1, depth)
 
-    steps = 4
     hid = units // steps
-    block = GRID[1:] + (3 * ushare // 2, depth)
+    block = (3,) + GRID + (16, depth)
     wbuf = pltpu.VMEM((2,) + block, BF16)
     dwbuf = pltpu.VMEM(block, BF16)
     if fast:
-        chunks = row_chunks([(k, hshare, hshare, 0, k * hshare) for k in range(3)], 16)
-        waves = len(chunks) + sum(lags) + 1
-        plan = spread_out(waves, 3, 3, 8)
-        mlp_links = (zcount, chunks, lags, plan)
-        w_last, more_specs, more_shapes = mlp_own, [hbm], [shape_of(w_first.shape, BF16)]
-        half_block = (block[0],) + block[2:]
+        chunks = [
+            (k, 16 * (ready_parts + p), 16, 0, 48 * p + 16 * k)
+            for p in range(steps - ready_parts)
+            for k in range(3)
+        ]
+        plan = [[[] for _ in range(8)] for _ in range(steps)]
+        todo = list(range(len(chunks) + sum(lags)))
+        for s in range(ready_parts - 1, steps - 1):
+            due = 3 * (s - ready_parts + 1) + 3 + sum(lags)
+            now, todo = [t for t in todo if t < due], [t for t in todo if t >= due]
+            first = 0 if s == ready_parts - 1 else s
+            spots = [(q, k) for q in range(first, s + 1) for k in range(8)]
+            for n, t in enumerate(now):
+                lead = min(MLP_AHEAD, len(now) - 1) if first == 0 else 0
+                share = max(0, n - lead) / max(1, len(now) - lead)
+                q, k = spots[int(share * len(spots))]
+                plan[q][k].append(t)
+        soon = [(p, k) for p in range(EARLY_PARTS) for k in range(3)]
+        early_chunks = [
+            (HALVED, n, 0, (p, k), (0, 16), 0, 16 * (k * EARLY_PARTS + p))
+            for n, (p, k) in enumerate(soon)
+        ]
+        early_lags = (1, 2, 2, 2)
+        early_plan = [[[] for _ in range(9)] for _ in range(steps)]
+        spot = 0
+        for t in range(len(soon) + sum(early_lags)):
+            after = 8 * (t // 3 + 1) + 7 if t < len(soon) else 0
+            spot = max(after, spot + EARLY_GAP)
+            q, k = divmod(min(spot, 8 * steps), 8)
+            q, k = (q, k) if q < steps else (steps - 1, 8)
+            early_plan[q][k].append(t)
+        mlp_links = (zcount, chunks, lags, plan, early_chunks, early_lags, early_plan)
+        w_last, more_specs = mlp_own, [hbm, whole((16 * len(soon), depth))]
+        more_shapes = [
+            shape_of(GRID + (48 * (steps - ready_parts), depth), BF16),
+            shape_of((16 * len(soon), depth), F32),
+        ]
+        half_block = block[:3] + block[4:]
         more_scratch = [
             pltpu.VMEM(half_block, BF16), one_dma((2,)), pltpu.SemaphoreType.REGULAR,
-            *gather_sems(len(chunks), zcount),
+            *gather_sems(len(chunks), zcount), *halved_scratch(len(soon), len(soon), depth, zcount),
         ]
-        dw_shape = (2, 2) + half_block
+        dw_shape = (steps,) + half_block
         more_params = dict(collective_id=3, has_side_effects=True)
     else:
         mlp_links, w_last, more_specs, more_shapes, more_scratch = None, [w_second], [], [], []
-        dw_shape, more_params = (2, 2) + block, {}
-    out_l, out_s, d_res, rlow, mix_l, gain2_grad, dmlp, *_ = pl.pallas_call(
+        dw_shape, more_params = (steps,) + block, {}
+    out_l, out_s, d_res, rlow, mix_l, gain2_grad, dmlp, *more_out = pl.pallas_call(
         functools.partial(mlp_kernel, ltiles, tokens // TILE, mlp_links),
         grid=(steps,),
         in_specs=[
@@ -1459,10 +1543,9 @@
         ],
         scratch_shapes=[
             pltpu.VMEM((tokens, depth), BF16), pltpu.VMEM((tokens, depth), F32),
-            pltpu.VMEM((tokens, depth), F32), pltpu.VMEM((tokens, hid), F32),
-            pltpu.VMEM((tokens, hid), F32), pltpu.VMEM((tokens, hid), F32),
-            pltpu.VMEM((tokens, hid), BF16), pltpu.VMEM((tokens, hid), BF16),
-            pltpu.VMEM((tokens, hid), BF16), wbuf, dwbuf, one_dma((2,)), one_dma, *more_scratch,
+            pltpu.VMEM((tokens, depth), F32), pltpu.VMEM((tokens, 2 * hid), F32),
+            pltpu.VMEM((tokens, hid), F32), pltpu.VMEM((tokens, hid), BF16),
+            pltpu.VMEM((tokens, 2 * hid), BF16), wbuf, dwbuf, one_dma((2, 3)), one_dma, *more_scratch,
         ],
         compiler_params=params(62, **more_params),
         name="mlp",
@@ -1475,11 +1558,10 @@
         size = 16
         tail_chunks = []
         number = 0
-        for h in range(2):
-            for start in range(0, 3 * hshare, size):
-                k, offset = divmod(start, hshare)
+        for p in range(EARLY_PARTS, steps):
+            for k in range(3):
                 tail_chunks.append(
-                    (HALVED, number % TAIL_SLOTS, 0, h, (start, size), k, h * hshare + offset)
+                    (HALVED, number % TAIL_SLOTS, 0, (p, k), (0, size), k, 16 * p)
                 )
                 number += 1
         for which in (1, 2, 3):
@@ -1500,7 +1582,8 @@
         plan = paced(during, 3, marks)
         plan[-1][-1] += range(during, len(tail_chunks) + sum(tail_lags) + 1)
         tail_links = (zcount, tail_chunks, tail_lags, plan)
-        tail_in, tail_specs = [dmlp], [whole((ushare, depth))] * 3 + [whole((cshare, depth))] * 3
+        early_sums = more_out[1]
+        tail_in, tail_specs = [dmlp, early_sums], [whole((ushare, depth))] * 3 + [whole((cshare, depth))] * 3
         tail_shapes = [shape_of((ushare, depth), F32)] * 3 + [shape_of((cshare, depth), F32)] * 3
         lone = five(TAIL_SLOTS, (size, depth), BF16, zcount)
         lone[1] = five(CORE_SLOTS, (size, depth), BF16, zcount)[1]
@@ -1523,7 +1606,7 @@
             cols_at(srows, early), cols_at(total, early), cols_at(total, late),
             cols_at(total, both_times), cols_at(total, late), cols_at(total, both_times),
             cols_at(HALO + lrows, both_times), cols_at(8, both_times), whole((8, depth)),
-            *[hbm for _ in tail_in],
+            *([hbm, whole(early_sums.shape)] if fast else []),
         ],
         out_specs=[
             whole((lrows, depth)), whole((srows, depth)), whole((8, depth)), hbm, hbm, hbm, hbm, hbm,
@@ -1555,7 +1638,7 @@
     if fast:
         g_mgate, g_mup, g_down, g_out, g_gate, g_input = shares
     else:
-        dmlp = dmlp.reshape(2, SLOTS, 3, -1, depth).transpose(1, 2, 0, 3, 4)
+        dmlp = dmlp.reshape(steps, 3, SLOTS, -1, depth).transpose(2, 1, 0, 3, 4)
         g_mgate, g_mup, g_down = scatter_slots(dmlp.reshape(SLOTS, -1, depth), 3, count)
         dmix = jnp.concatenate([d_gate, d_input, d_out], axis=4).reshape(SLOTS, -1, depth)
         g_gate, g_input, g_out = scatter_slots(dmix, 3, count)

time: 413 us -> 394 us (0.954)
  Pallas kernels: 386 us -> 368 us
    pallas_call x1, Pallas kernels: 166 us -> 148 us  [shards(): pl.pallas_call(functools.partial(tail_kernel, ltiles, tiles, groups, tail...]
where the time goes in v7:
time: 394 us; the launch traced here: 393 us
  Pallas kernels  368 us (93%)
  local copies, waits for them, and re-layouts  23.7 us (6%)
    pallas_call x1, Pallas kernels, shards(): pl.pallas_call(functools.partial(tail_kernel, ltiles, tiles, groups, tail...  148 us
    pallas_call x1, Pallas kernels, shards(): pl.pallas_call(functools.partial(front_kernel, ltiles, tiles, groups, fro...  113 us
    pallas_call x1, Pallas kernels, shards(): pl.pallas_call(functools.partial(mlp_kernel, ltiles, tokens // TILE, mlp_...  107 us
    unnamed x30, local copies, waits for them, and re-layouts  8.1 us

profile of v7, /device:TPU:0, one launch (start us, length us, event | category | flops | bytes accessed | tf_op | source)
XLA Modules:
  0.0 393.4 jit_solution(942200944189113953)
XLA Ops:
  1.3 1.3 reshape.113.refs_6_
  2.6 1.3 reshape.114.refs_7_
  3.9 1.3 reshape.115.refs_9_
  5.2 1.3 reshape.116.refs_10_
  6.5 1.3 reshape.117.refs_11_
  7.8 0.7 divide_multiply_fusion
  8.5 0.6 reshape.119.refs_13_
  9.1 0.6 reshape.118.refs_12_
  9.7 113.0 %front.1 = (f32[656,1536]{1,0:T(8,128)}, f32[656,1536]{1,0:T(8,128)}, f32[656,1536]{1,0:T(8,128)}, f32[656,1536]{1,0:T(8,128)}, f32[656,1536]{1,0:T(8,128)}, /*i...) custom-call(bf16[128,1024]{1,0:T(8,128)(2,1)} %bitcast.48, ...), custom_call_target="tpu_custom_call" | custom-call | tf_op jit(solution)/shard_map/front/pallas_call | solution.py:1435
  122.7 106.6 %mlp.1 = (bf16[128,1024]{1,0:T(8,128)(2,1)}, bf16[512,1024]{1,0:T(8,128)(2,1)}, f32[640,1024]{1,0:T(8,128)}, bf16[640,1024]{1,0:T(8,128)(2,1)}, bf16[128,1536]{1...) custom-call(bf16[656,1024]{1,0:T(8,128)(2,1)} %get-tuple-element.54., ...), custom_call_target="tpu_custom_call" | custom-call | tf_op jit(solution)/shard_map/mlp/pallas_call | solution.py:1525
  229.3 148.0 %tail.1 = (f32[128,1024]{1,0:T(8,128)}, f32[512,1024]{1,0:T(8,128)}, f32[8,1024]{1,0:T(8,128)}, bf16[2,2,2,4,48,1024]{5,4,3,2,1,0:T(8,128)(2,1)}, bf16[2,2,2,4,4...) custom-call(bf16[656,1024]{1,0:T(8,128)(2,1)} %get-tuple-element.54., ...), custom_call_target="tpu_custom_call" | custom-call | tf_op jit(solution)/shard_map/tail/pallas_call | solution.py:1599
  377.3 1.3 slice_bitcast_fusion
  378.6 1.4 slice.62
  380.0 1.7 slice_reduce_fusion
  381.8 3.5 fusion.1
  385.3 0.0 copy-done.6
  385.3 0.7 copy.54
  386.0 0.0 copy-done.1
  386.0 1.0 copy.55
  387.0 0.0 copy-done.2
  387.0 0.8 copy.56
  387.8 0.0 copy-done
  387.8 0.0 copy-start.3
  387.8 1.3 copy.57
  389.1 0.0 copy-done.9
  389.1 0.7 copy.58
  389.8 0.7 copy.59
  390.5 0.7 copy.60
  391.2 0.7 copy.61
  391.9 0.0 copy-done.4
  391.9 0.7 copy.62
  392.7 0.7 copy.63
  (13 shorter events, 0.0 us)
Async XLA Ops:
  381.8 3.5 copy-start.6
  381.8 4.2 %copy-start.1 = (bf16[512,1024]{1,0:T(8,128)(2,1)S(1)}, bf16[512,1024]{1,0:T(8,128)(2,1)}, u32[]{:S(2)}) copy-start(bf16[512,1024]{1,0:T(8,128)(2,1)} %get-tuple-element.64) | copy-start | bytes 3145732
  385.3 1.7 copy-start.2
  385.3 2.5 copy-start
  387.0 2.1 copy-start.9
  387.0 2.8 copy-start.8
  387.8 2.7 copy-start.7
  387.8 3.4 copy-start.5
  387.8 4.1 %copy-start.4 = (f32[96,1024]{1,0:T(8,128)S(1)}, f32[96,1024]{1,0:T(8,128)}, u32[]{:S(2)}) copy-start(f32[96,1024]{1,0:T(8,128)} %get-tuple-element.85) | copy-start | bytes 1179652
  387.8 4.9 %copy-start.3 = (f32[96,1024]{1,0:T(8,128)S(1)}, f32[96,1024]{1,0:T(8,128)}, u32[]{:S(2)}) copy-start(f32[96,1024]{1,0:T(8,128)} %get-tuple-element.140) | copy-start | bytes 1179652

commit v8 on v7

--- a/solution.py
+++ b/solution.py
@@ -19,7 +19,7 @@
 EARLY_PARTS = 2
 EARLY_GAP = 3
 FRONT_PARTS = 3
-TAIL_SLOTS = 10
+TAIL_SLOTS = 11
 CORE_SLOTS = 5
 GELU_A = 0.7978845608028654
 GELU_B = 0.044715
@@ -551,7 +551,7 @@
         refs = refs[6:18] + refs[21:-3]
         point = in_turn(gather, step, plan)
     gp, inn, dp, ip, st, pr, mix, sin_ref, nm_ref, x_ref, cot_ref, pc_ref = refs[:12]
-    cv_ref, cl_ref, wbuf, pairs, halo, isem, wsem, hsem, *swap = refs[12:]
+    cv_ref, cl_ref, wbuf, pairs, halo, all_pc, isem, wsem, hsem, *swap = refs[12:]
     exchange = Exchange(*swap)
     lrows = ltiles * TILE
     place = exchange.place
@@ -580,6 +580,12 @@
             long_ref.at[pl.ds(lrows - HALO, HALO)], halo, hsem.at[0], hsem.at[1], exchange.peer(1)
         )
         ahead.start()
+        row = 0
+        for ref in channel_refs:
+            value = ref[...] if len(ref.shape) == 2 else ref[...].reshape(1, ref.shape[0])
+            all_pc[row : row + value.shape[0], :] = value
+            row += value.shape[0]
+        all_pc[row:, :] = jnp.zeros((16 - row, all_pc.shape[1]), F32)
         todo = [] if gather is None else list(range(ready))
 
         def some(count):
@@ -621,10 +627,9 @@
             @pl.when(step == g + 1)
             def _(g=g):
                 load(g).wait()
-
-        for k, ref in zip((GB, IB, CW, CB, DB, OB, C8, S8), channel_refs):
-            pc_ref[k : k + ref.shape[0], :] = ref[...]
-        pc_ref[S8 + 1 :, :] = jnp.zeros((15 - S8, pc_ref.shape[1]), F32)
+                width = pc_ref.shape[1]
+                pc_ref[...] = all_pc[:, g * width : (g + 1) * width]
+
         pair_up(pairs.at[0], wd_ref)
         pair_up(pairs.at[1], wo_ref)
         slot = lax.rem(step - 1, 2)
@@ -1294,6 +1299,40 @@
             copy.wait()
 
 
+def finish_kernel(number, *refs):
+    ins, (gates_ref, sums_ref) = refs[:number], refs[number : number + 2]
+    outs = refs[number + 2 : 2 * number + 2]
+    gd_ref, go_ref, gain1_ref, gain2_ref, conv_ref, *rows = refs[2 * number + 2 : -number - 3]
+    *held, table, sem_in, sem_out = refs[-number - 3 :]
+    copies = []
+    for k, (a, h, b) in enumerate(zip(ins, held, outs)):
+        copies.append(
+            (
+                pltpu.make_async_copy(a, h, sem_in.at[k]),
+                pltpu.make_async_copy(h, b, sem_out.at[k]),
+            )
+        )
+        copies[-1][0].start()
+    for come, go in copies:
+        come.wait()
+        go.start()
+    gd_ref[...] = gates_ref[0].astype(F32)
+    go_ref[...] = gates_ref[1].astype(F32)
+    for h in range(2):
+        for k in range(16):
+            table[8 * h : 8 * h + 8, 128 * k : 128 * k + 128] = sums_ref[h, k]
+    chans = conv_ref.shape[1]
+    conv_ref[...] = table[1:5, 0:chans]
+    for r, ref in zip((0, 5, 6, 7, 8, 9), rows):
+        ref[...] = table[r : r + 1, 0:chans].reshape(chans)
+    for k, ref in enumerate((gain1_ref, gain2_ref)):
+        for i in range(8):
+            table[0:1, 128 * i : 128 * i + 128] = sums_ref[0, 12 + k, i : i + 1, :]
+        ref[...] = table[0:1, 0:1024].reshape(1024)
+    for _, go in copies:
+        go.wait()
+
+
 def shape_of(shape, dtype):
     return jax.ShapeDtypeStruct(shape, dtype)
 
@@ -1378,7 +1417,6 @@
         gate_bias, input_bias, conv_weight, conv_bias, decay_gate_bias, input_gate_bias,
         8.0 * jax.nn.softplus(decay_param), 8.0 * jax.nn.sigmoid(decay_param),
     ]
-    channel = [c.reshape(-1, chans) for c in channel]
     gain1 = first_gain[None]
     gain2 = second_gain[None]
 
@@ -1437,8 +1475,8 @@
         grid=(1 + groups,),
         in_specs=[
             hbm, hbm, hbm, hbm, pl.BlockSpec(memory_space=pltpu.SMEM), whole((1, depth)),
-            *[cols_at(c.shape[0], after_one) for c in channel], blocks_at(after_one),
-            blocks_at(after_one), *[hbm for _ in front_own],
+            *[whole(c.shape) for c in channel], blocks_at(after_one),
+            blocks_at(after_one), *[whole(w.shape) if fast else hbm for w in front_own],
         ],
         out_specs=[
             col, col, col, col, col, cols_at(HALO + lrows, after_one), cols_at(srows, after_one),
@@ -1455,7 +1493,7 @@
             pltpu.VMEM((total, width), F32), pltpu.VMEM((total, width), BF16),
             pltpu.VMEM((2,) + GRID[2:] + (2 * cshare, depth), BF16),
             pltpu.VMEM((2, width, width), BF16), pltpu.VMEM((HALO, depth), BF16),
-            one_dma((4,)), one_dma((2,)), one_dma((2,)), *exchange_scratch(groups, width, seqs),
+            pltpu.VMEM((16, chans), F32), one_dma((4,)), one_dma((2,)), one_dma((2,)), *exchange_scratch(groups, width, seqs),
             *front_scratch,
         ],
         compiler_params=params(56, collective_id=0, has_side_effects=True),
@@ -1529,7 +1567,7 @@
             whole((total, depth)), whole((tokens, depth)), whole((HALO + lrows, chans)),
             whole((HALO + lrows, chans)), whole((HALO + lrows, chans)), whole((8, chans)),
             whole((srows, chans)), whole((SLOTS, cshare, depth)), whole((1, depth)), hbm,
-            *[hbm for _ in w_last],
+            *[whole(w.shape) if fast else hbm for w in w_last],
         ],
         out_specs=[
             whole((lrows, depth)), whole((srows, depth)), whole((tokens, depth)), whole((tokens, depth)),
@@ -1574,7 +1612,7 @@
                     (CORE, number % TAIL_SLOTS, which, None, (start, size), 2 + which, start)
                 )
                 number += 1
-        tail_lags = (1, 2, 2, 2, 1, 1, 1, 1)
+        tail_lags = (1, 3, 3, 3, 1, 1, 1, 1)
         marks = [[5.0 * g + t for t in (0.0, 1.5, 4.0)] for g in range(groups)]
         marks += [
             [5.0 * groups + 12.5 * g + t for t in (0.0, 5.0, 6.0, 9.0, 10.5, 12.5)] for g in range(groups)
@@ -1643,29 +1681,48 @@
         dmix = jnp.concatenate([d_gate, d_input, d_out], axis=4).reshape(SLOTS, -1, depth)
         g_gate, g_input, g_out = scatter_slots(dmix, 3, count)
         gate_sums, sums = lax.psum((gate_sums.astype(F32), sums), ("seq", "row"))
-    gate_sums = gate_sums.reshape(2, blocks, bwidth, bwidth).astype(F32)
-    sums = sums.reshape(2, 16, 8, 128)
-    gain_sums = sums[0, 12:14].reshape(2, depth)
-    rows = sums.transpose(0, 2, 1, 3).reshape(16, 2048)[0:10, :chans]
+    large = [out_l, out_s, dx_l, dx_s, g_gate, g_input, g_out, g_mgate, g_mup, g_down]
+    vector = shape_of((chans,), F32)
+    gate_grad = shape_of((blocks, bwidth, bwidth), F32)
+    gain_grad = shape_of((depth,), F32)
+    vmem = pl.BlockSpec(memory_space=pltpu.VMEM)
+    (
+        out_l, out_s, dx_l, dx_s, g_gate, g_input, g_out, g_mgate, g_mup, g_down, decay_grad,
+        open_grad, gain1_grad, gain2_grad, conv_grad, input_bias_grad, conv_bias_grad,
+        decay_bias_grad, open_bias_grad, param_grad, gate_bias_grad,
+    ) = pl.pallas_call(
+        functools.partial(finish_kernel, len(large)),
+        in_specs=[hbm] * len(large) + [vmem, vmem],
+        out_specs=[hbm] * len(large) + [vmem] * 11,
+        out_shape=[shape_of(a.shape, a.dtype) for a in large]
+        + [gate_grad, gate_grad, gain_grad, gain_grad, shape_of(conv_weight.shape, F32)]
+        + [vector] * 6,
+        scratch_shapes=[
+            *[pltpu.VMEM(a.shape, a.dtype) for a in large], pltpu.VMEM((16, 2048), F32),
+            one_dma((len(large),)), one_dma((len(large),)),
+        ],
+        compiler_params=pltpu.CompilerParams(vmem_limit_bytes=62 * MIB),
+        name="finish",
+    )(*large, gate_sums.reshape(2, blocks, bwidth, bwidth), sums.reshape(2, 16, 8, 128))
     return (
         out_l.reshape(long_tokens.shape),
         out_s.reshape(short_tokens.shape),
         dx_l.reshape(long_tokens.shape),
         dx_s.reshape(short_tokens.shape),
-        gain_sums[0],
+        gain1_grad,
         g_gate.T,
-        rows[9],
+        gate_bias_grad,
         g_input.T,
-        rows[0],
-        rows[1:5],
-        rows[5],
-        gate_sums[0],
-        rows[6],
-        gate_sums[1],
-        rows[7],
-        rows[8],
+        input_bias_grad,
+        conv_grad,
+        conv_bias_grad,
+        decay_grad,
+        decay_bias_grad,
+        open_grad,
+        open_bias_grad,
+        param_grad,
         g_out,
-        gain_sums[1],
+        gain2_grad,
         g_mgate.T,
         g_mup.T,
         g_down,

time: 394 us -> 377 us (0.957)
  local copies, waits for them, and re-layouts: 23.7 us -> 0 us
  Pallas kernels: 368 us -> 374 us
    unnamed x30 -> x0, local copies, waits for them, and re-layouts: 8.1 us -> none
    reshape x7 -> x0, local copies, waits for them, and re-layouts: 7.67 us -> none  [shards(): channel = [c.reshape(-1, chans) for c in channel]]
    pallas_call x0 -> x1, Pallas kernels: none -> 7.56 us  [shards(): pl.pallas_call(functools.partial(finish_kernel, len(large)), in_specs=[hb...]
    slice x3 -> x0, local copies, waits for them, and re-layouts: 6.65 us -> none  [the longest x1 3.52 us: shards(): gate_sums[1]]
where the time goes in v8:
time: 377 us; the launch traced here: 376 us
  Pallas kernels  374 us (99%)
    pallas_call x1, Pallas kernels, shards(): pl.pallas_call(functools.partial(tail_kernel, ltiles, tiles, groups, tail...  146 us
    pallas_call x1, Pallas kernels, shards(): pl.pallas_call(functools.partial(front_kernel, ltiles, tiles, groups, fro...  113 us
    pallas_call x1, Pallas kernels, shards(): pl.pallas_call(functools.partial(mlp_kernel, ltiles, tokens // TILE, mlp_...  107 us
    pallas_call x1, Pallas kernels, shards(): pl.pallas_call(functools.partial(finish_kernel, len(large)), in_specs=[hb...  7.56 us

profile of v8, /device:TPU:0, one launch (start us, length us, event | category | flops | bytes accessed | tf_op | source)
XLA Modules:
  0.0 376.5 jit_solution(15149484154681111404)
XLA Ops:
  1.3 1.3 divide_multiply_fusion
  2.6 112.8 %front.1 = (f32[656,1536]{1,0:T(8,128)}, f32[656,1536]{1,0:T(8,128)}, f32[656,1536]{1,0:T(8,128)}, f32[656,1536]{1,0:T(8,128)}, f32[656,1536]{1,0:T(8,128)}, /*i...) custom-call(bf16[128,1024]{1,0:T(8,128)(2,1)} %bitcast.33, ...), custom_call_target="tpu_custom_call" | custom-call | tf_op jit(solution)/shard_map/front/pallas_call | solution.py:1473
  115.5 107.0 %mlp.1 = (bf16[128,1024]{1,0:T(8,128)(2,1)}, bf16[512,1024]{1,0:T(8,128)(2,1)}, f32[640,1024]{1,0:T(8,128)}, bf16[640,1024]{1,0:T(8,128)(2,1)}, bf16[128,1536]{1...) custom-call(bf16[656,1024]{1,0:T(8,128)(2,1)} %get-tuple-element.75., ...), custom_call_target="tpu_custom_call" | custom-call | tf_op jit(solution)/shard_map/mlp/pallas_call | solution.py:1563
  222.5 146.2 %tail.1 = (f32[128,1024]{1,0:T(8,128)}, f32[512,1024]{1,0:T(8,128)}, f32[8,1024]{1,0:T(8,128)}, bf16[2,2,2,4,48,1024]{5,4,3,2,1,0:T(8,128)(2,1)}, bf16[2,2,2,4,4...) custom-call(bf16[656,1024]{1,0:T(8,128)(2,1)} %get-tuple-element.75., ...), custom_call_target="tpu_custom_call" | custom-call | tf_op jit(solution)/shard_map/tail/pallas_call | solution.py:1637
  368.7 7.6 %finish.1 = (bf16[128,1024]{1,0:T(8,128)(2,1)}, bf16[512,1024]{1,0:T(8,128)(2,1)}, f32[128,1024]{1,0:T(8,128)}, f32[512,1024]{1,0:T(8,128)}, f32[48,1024]{1,0:T(...) custom-call(bf16[128,1024]{1,0:T(8,128)(2,1)} %get-tuple-element.84., ...), custom_call_target="tpu_custom_call" | custom-call | tf_op jit(solution)/shard_map/finish/pallas_call | solution.py:1693

commit v9 on v8

--- a/solution.py
+++ b/solution.py
@@ -18,6 +18,8 @@
 MLP_AHEAD = 1
 EARLY_PARTS = 2
 EARLY_GAP = 3
+FRONT_LEFT = 9
+FRONT_DELAY = 3
 FRONT_PARTS = 3
 TAIL_SLOTS = 11
 CORE_SLOTS = 5
@@ -207,18 +209,21 @@
             self.go(stage, lambda d: d.wait_send())
 
 
-def wave_of(t, count, lags):
+def wave_of(t, count, lags, urgent=None, delay=0):
+    urgent = count if urgent is None else urgent
     for stage in range(len(lags), -1, -1):
         piece = t - sum(lags[:stage])
-        if 0 <= piece < count:
+        if 0 <= piece < urgent:
             yield piece, stage
+        elif urgent <= piece - delay < count:
+            yield piece - delay, stage
 
 
 class Gather:
-    def __init__(self, zcount, ins, outs, sems, chunks, lags):
+    def __init__(self, zcount, ins, outs, sems, chunks, lags, urgent=None, delay=0):
+        self.order = (len(chunks), lags, urgent, delay)
         self.csem, self.ssem, self.rsem = sems
         self.peers = Peers(zcount)
-        self.lags = lags
         y, x, c, z = self.peers.place
         self.spreads, self.copies = [], []
         for i, (which, start, size, target, offset) in enumerate(chunks):
@@ -236,10 +241,9 @@
 
             self.spreads.append(Spread(self.peers, own, full, send, recv))
             self.copies.append(pltpu.make_async_copy(own, full(y, x, c, z), self.csem.at[i]))
-        self.waves = len(chunks) + sum(lags) + 1
 
     def wave(self, t):
-        for i, stage in wave_of(t, len(self.spreads), self.lags):
+        for i, stage in wave_of(t, *self.order):
             if stage == 0:
                 self.copies[i].start()
             elif stage == 1:
@@ -536,22 +540,25 @@
     (
         long_ref, short_ref, lcot_ref, scot_ref, length_ref, gain_ref, *channel_refs
     ) = refs[:14]
-    wd_ref, wo_ref = refs[14:16]
-    refs = refs[16:]
+    wd_ref, wo_ref, gain2_ref = refs[14:17]
+    refs = refs[17:]
     step = pl.program_id(0)
     point, gather = no_point, None
     zcount = 1
     if links is None:
-        pairw, refs = refs[0], refs[1:]
+        pairw, outw, refs = refs[0], refs[1], refs[2:]
     else:
-        zcount, chunks, lags, ready, plan = links
-        owns, made = refs[:6], refs[18:21]
-        pairw = made[0]
-        gather = Gather(zcount, owns, made, refs[-3:], chunks, lags)
-        refs = refs[6:18] + refs[21:-3]
+        zcount, chunks, lags, urgent, ready, plan = links
+        owns, made = refs[:6], refs[21:24]
+        pairw, outw = made[:2]
+        gather = Gather(zcount, owns, made, refs[-3:], chunks, lags, urgent, FRONT_DELAY)
+        refs = refs[6:21] + refs[24:-3]
         point = in_turn(gather, step, plan)
     gp, inn, dp, ip, st, pr, mix, sin_ref, nm_ref, x_ref, cot_ref, pc_ref = refs[:12]
-    cv_ref, cl_ref, wbuf, pairs, halo, all_pc, isem, wsem, hsem, *swap = refs[12:]
+    resid_ref, n2_ref, mixl_ref = refs[12:15]
+    (
+        cv_ref, cl_ref, wbuf, pairs, halo, all_pc, mixes, longs, wobuf, isem, wsem, hsem, osem, *swap
+    ) = refs[15:]
     exchange = Exchange(*swap)
     lrows = ltiles * TILE
     place = exchange.place
@@ -650,12 +657,58 @@
 
         point(3)
 
+    @pl.when(step > 0)
+    def _():
+        g = step - 1
+        mixes[g] = mix[...]
+        for k, ref in enumerate((st, pr, gp)):
+            longs[k, g] = ref[HALO : HALO + lrows, :]
+
+    whole_out = pltpu.make_async_copy(outw, wobuf, osem)
+
+    @pl.when(step == groups)
+    def _():
+        whole_out.start()
+        width = gp.shape[1]
+        for g in range(groups):
+            cols = slice(g * width, (g + 1) * width)
+            state = exchange.entering(g, False)
+            sin_ref[:, cols] = jnp.broadcast_to(state, (8, width))
+            states = longs[0, g] + longs[1, g] * state
+            mixl_ref[:, cols] = (states * gelu(longs[2, g])).astype(BF16)
+        whole_out.wait()
+
+    point(4)
+
     @pl.when(step == groups)
     def _():
         width = gp.shape[1]
         for g in range(groups):
-            state = exchange.entering(g, False)
-            sin_ref[:, g * width : (g + 1) * width] = jnp.broadcast_to(state, (8, width))
+            part = flat(wobuf[g // 2, g % 2])
+            top = dot_nn(mixl_ref[:, g * width : (g + 1) * width], part)
+            low = dot_nn(mixes[g], part)
+            if g == 0:
+                resid_ref[0:lrows, :] = top
+                resid_ref[lrows:, :] = low
+            else:
+                resid_ref[0:lrows, :] += top
+                resid_ref[lrows:, :] += low
+
+    point(5)
+
+    @pl.when(step == groups)
+    def _():
+        @pl.loop(0, tiles - 1)
+        def _(i):
+            r = resid_ref[at(i), :] + x_ref[at(1 + i), :].astype(F32)
+            resid_ref[at(i), :] = r
+            s = lax.rsqrt(jnp.mean(r * r, axis=1, keepdims=True) + EPSILON)
+            n2_ref[at(i), :] = (r * s * gain2_ref[...]).astype(BF16)
+
+    point(6)
+
+    @pl.when(step == groups)
+    def _():
         exchange.drain(groups)
         if gather is not None:
             gather.drain()
@@ -718,10 +771,8 @@
 
 
 def mlp_kernel(ltiles, tiles, links, *refs):
-    (
-        x_ref, cot_ref, st_ref, pr_ref, gp_ref, sin_ref, mixs_ref, wo_ref, gain_ref, w1_ref, w2_ref
-    ) = refs[:11]
-    refs = refs[11:]
+    resid_ref, n2_ref, cot_ref, gain_ref, w1_ref, w2_ref = refs[:6]
+    refs = refs[6:]
     point, gather = no_point, None
     step = pl.program_id(0)
     last = pl.num_programs(0) - 1
@@ -729,8 +780,8 @@
         zcount, chunks, lags, plan, sum_chunks, sum_lags, sum_plan = links
         owns = [w2_ref, *refs[:2]]
         refs = refs[2:]
-    outl_ref, outs_ref, dres_ref, rlow_ref, mixl_ref, gain_grad_ref, dw_hbm = refs[:7]
-    refs = refs[7:]
+    outl_ref, outs_ref, dres_ref, rlow_ref, gain_grad_ref, dw_hbm = refs[:6]
+    refs = refs[6:]
     if links is not None:
         w2_ref, early_ref = refs[:2]
         halved = (refs[-9], None, *refs[-8:-5])
@@ -748,7 +799,7 @@
             scatter_point(k)
 
     (
-        n2_ref, acc_o, acc_n, gu_ref, d_ref, h_ref, dgu_ref, wbuf, dwbuf, wsem, dsem
+        acc_o, acc_n, gu_ref, d_ref, h_ref, dgu_ref, wbuf, dwbuf, wsem, dsem
     ) = refs
     lrows = ltiles * TILE
     hid = h_ref.shape[1]
@@ -836,25 +887,7 @@
 
     @pl.when(step == 0)
     def _():
-        s_in = sin_ref[0:1, :]
-
-        @pl.loop(0, ltiles)
-        def _(i):
-            s = st_ref[at(1 + i), :] + pr_ref[at(1 + i), :] * s_in
-            mixl_ref[at(i), :] = (s * gelu(gp_ref[at(1 + i), :])).astype(BF16)
-
-        wo = flat(wo_ref[...])
-        dres_ref[0:lrows, :] = dot_nn(mixl_ref[...], wo)
-        dres_ref[lrows:, :] = dot_nn(mixs_ref[...], wo)
-
-        @pl.loop(0, tiles)
-        def _(i):
-            r = dres_ref[at(i), :] + x_ref[at(1 + i), :].astype(F32)
-            dres_ref[at(i), :] = r
-            acc_o[at(i), :] = r
-            s = lax.rsqrt(jnp.mean(r * r, axis=1, keepdims=True) + EPSILON)
-            n2_ref[at(i), :] = (r * s * gain_ref[...]).astype(BF16)
-
+        acc_o[...] = resid_ref[...]
         acc_n[...] = jnp.zeros_like(acc_n)
 
     point(1)
@@ -908,7 +941,7 @@
     @pl.when(step == last)
     def _():
         def one(i, total):
-            r = dres_ref[at(i), :]
+            r = resid_ref[at(i), :]
             dn = acc_n[at(i), :]
             s = lax.rsqrt(jnp.mean(r * r, axis=1, keepdims=True) + EPSILON)
             e = dn * gain_ref[...]
@@ -935,7 +968,8 @@
 
 def back_part(
     ltiles, tiles, point, rlow_ref, wo_ref, mixl_ref, mixs_ref, gp_ref, st_ref, pr_ref, sin_ref,
-    dp_ref, pc_ref, dwo_ref, gl_ref, tot_ref, rch_ref, end_ref, bias_ref, dm_ref, free,
+    dp_ref, pc_ref, dwo_ref, gl_ref, tot_ref, rch_ref, end_ref, bias_ref, dm_ref, free, nm_ref,
+    dwg_ref,
 ):
     point(0)
     lrows = ltiles * TILE
@@ -992,12 +1026,13 @@
     )
     end_ref[...] = jnp.concatenate([reach, c, jnp.zeros((6, width), F32)], axis=0)
     bias_ref[...] = bias
+    dwg_ref[...] = dot_tn(gl_ref[...], nm_ref[...]).astype(BF16).reshape(dwg_ref.shape)
 
 
 def last_part(
     ltiles, tiles, groups, point, exchange, residual, x_ref, gain_ref, nm_ref, wg_ref, wi_ref,
     wd_ref, wo_ref, pc_ref, in_ref, dp_ref, ip_ref, st_ref, pr_ref, sin_ref, tot_ref, rch_ref,
-    gl_ref, bias_ref, dxl_ref, dxs_ref, halo_ref, behind, pairs, gain_grad_ref, dwg_ref, dwi_ref,
+    gl_ref, bias_ref, dxl_ref, dxs_ref, halo_ref, behind, pairs, gain_grad_ref, dwi_ref,
     gg_ref, small_ref, acc, dc_ref, cl_ref, dl_ref, ol_ref, il_ref, gain2_ref, free, keep,
 ):
     width = in_ref.shape[1]
@@ -1115,7 +1150,6 @@
     free()
     nm = nm_ref[...]
     dwi_ref[...] = dot_tn(il_ref[...], nm).astype(BF16).reshape(dwi_ref.shape)
-    dwg_ref[...] = dot_tn(gl_ref[...], nm).astype(BF16).reshape(dwg_ref.shape)
     keep()
     point(4)
     part = dot_nn(gl_ref[...], flat(wg_ref[...])) + dot_nn(il_ref[...], flat(wi_ref[...]))
@@ -1239,15 +1273,24 @@
     def _():
         meet_all(exchange, 1 if scatter is None else zcount)
 
+    def freed(g):
+        if g > 0:
+            stash(g - 1, 0, dwo_hbm).wait()
+            stash(g - 1, 1, dwg_hbm).wait()
+
+    def kept(g):
+        stash(g, 0, dwo_hbm).start()
+        stash(g, 1, dwg_hbm).start()
+
     @pl.when(step < groups)
     def _():
         back_part(
             ltiles, tiles, back_point, rlow_ref, w_ref, mixl_ref, mixs_ref, gp_ref, st_ref, pr_ref,
             sin_ref, dp_ref, pc_ref, wst.at[0], gl_ref, tot_ref, rch_ref, exchange.mine.at[group],
             bias_ref.at[group], acc.at[0 : rlow_ref.shape[0], 0:width],
-            lambda: stashed(0, lambda g: stash(g - 1, 0, dwo_hbm).wait() if g > 0 else None),
+            lambda: stashed(0, freed), nm_ref, wst.at[1],
         )
-        stashed(0, lambda g: stash(g, 0, dwo_hbm).start())
+        stashed(0, kept)
         for g in range(groups):
 
             @pl.when(step == g)
@@ -1260,24 +1303,22 @@
         @pl.when(step == groups)
         def _():
             stash(groups - 1, 0, dwo_hbm).wait()
+            stash(groups - 1, 1, dwg_hbm).wait()
 
         def before(g):
             if g > 0:
-                stash(g - 1, 1, dwg_hbm).wait()
                 stash(g - 1, 2, dwi_hbm).wait()
 
         def after(g):
-            stash(g, 1, dwg_hbm).start()
             stash(g, 2, dwi_hbm).start()
             if g == groups - 1:
-                stash(g, 1, dwg_hbm).wait()
                 stash(g, 2, dwi_hbm).wait()
 
         last_part(
             ltiles, tiles, groups, last_point, exchange, residual, x_ref, gain_ref, nm_ref,
             wg_ref, wi_ref, wd_ref, wo_ref, pc_ref, in_ref, dp_ref, ip_ref, st_ref, pr_ref, sin_ref,
             tot_ref, rch_ref, gl_ref, bias_ref.at[group], dxl_ref, dxs_ref, halo_out, behind, pairs,
-            gain_grad_ref, wst.at[1], wst.at[2], gsrc, ssrc, acc, dc_ref, cl_ref, dl_ref, ol_ref, il_ref, gain2_ref,
+            gain_grad_ref, wst.at[2], gsrc, ssrc, acc, dc_ref, cl_ref, dl_ref, ol_ref, il_ref, gain2_ref,
             lambda: stashed(groups, before), lambda: stashed(groups, after),
         )
 
@@ -1445,15 +1486,22 @@
     if fast:
         front_own = [gate_weight.T, input_weight.T, out_weight, *mlp_own]
         parts = [(0, 0, cshare, 0, 0), (1, 0, cshare, 0, cshare)]
-        ready = len(row_chunks(parts, 16)) + sum(lags)
+        urgent = len(row_chunks(parts, 16))
+        ready = urgent + sum(lags)
         parts += [(2, 0, cshare, 1, 0)]
         parts += [
             (3 + k, 16 * p, 16, 2, 48 * p + 16 * k) for p in range(ready_parts) for k in range(3)
         ]
         chunks = row_chunks(parts, 16)
-        plan = [[]] + spread_out(len(chunks) + sum(lags) + 1 - ready, 1, groups, 4)
+        waves = len(chunks) + FRONT_DELAY + sum(lags)
+        marks = [[4 * g + k for k in range(4)] for g in range(groups)]
+        plan = paced(waves - ready - FRONT_LEFT, 1, marks)
+        plan = [[]] + plan
+        left = list(range(waves - ready - FRONT_LEFT, waves - ready))
+        cut = FRONT_LEFT // 3
+        plan[-1] += [left[:cut], left[cut : 2 * cut], left[2 * cut :]]
         plan = [[[ready + t for t in p] for p in row] for row in plan]
-        front_links = (zcount, chunks, lags, ready, plan)
+        front_links = (zcount, chunks, lags, urgent, ready, plan)
         front_shapes = [
             shape_of(GRID + (n, depth), BF16) for n in (2 * cshare, cshare, 48 * ready_parts)
         ]
@@ -1464,36 +1512,44 @@
         mlpw = to_slots(mlp_own, count).reshape(GRID + (3, steps, 16, depth))
         mlpw = jnp.swapaxes(mlpw, 4, 5).reshape(GRID + (48 * steps, depth))
         w_first, w_second = jnp.split(mlpw, [48 * ready_parts], axis=4)
-        front_own = [pairw.reshape(GRID + (-1, depth))]
+        front_own = [w.reshape(GRID + (-1, depth)) for w in (pairw, outw)]
         front_links, front_shapes, front_scratch = None, [], []
 
     col = cols_at(total, after_one)
     wide = shape_of((total, chans), F32)
     narrow = shape_of((HALO + lrows, chans), F32)
-    gp, inner, dp, ip, states, reach, mix_s, s_in, normed, x, cot, chan, *made = pl.pallas_call(
+    (
+        gp, inner, dp, ip, states, reach, mix_s, s_in, normed, x, cot, chan, residual, normed2,
+        mix_l, *made,
+    ) = pl.pallas_call(
         functools.partial(front_kernel, ltiles, tiles, groups, front_links),
         grid=(1 + groups,),
         in_specs=[
             hbm, hbm, hbm, hbm, pl.BlockSpec(memory_space=pltpu.SMEM), whole((1, depth)),
             *[whole(c.shape) for c in channel], blocks_at(after_one),
-            blocks_at(after_one), *[whole(w.shape) if fast else hbm for w in front_own],
+            blocks_at(after_one), whole((1, depth)),
+            *[whole(w.shape) if fast else hbm for w in front_own],
         ],
         out_specs=[
             col, col, col, col, col, cols_at(HALO + lrows, after_one), cols_at(srows, after_one),
             whole((8, chans)), whole((total, depth)), whole((total, depth)),
-            whole((tokens, depth)), cols_at(16, after_one), *[hbm for _ in front_shapes],
+            whole((tokens, depth)), cols_at(16, after_one), whole((tokens, depth)),
+            whole((tokens, depth)), whole((lrows, chans)), *[hbm for _ in front_shapes],
         ],
         out_shape=[
             wide, wide, wide, wide, wide, narrow, shape_of((srows, chans), BF16),
             shape_of((8, chans), F32), shape_of((total, depth), BF16),
             shape_of((total, depth), BF16), shape_of((tokens, depth), BF16),
-            shape_of((16, chans), F32), *front_shapes,
+            shape_of((16, chans), F32), shape_of((tokens, depth), F32),
+            shape_of((tokens, depth), BF16), shape_of((lrows, chans), BF16), *front_shapes,
         ],
         scratch_shapes=[
             pltpu.VMEM((total, width), F32), pltpu.VMEM((total, width), BF16),
             pltpu.VMEM((2,) + GRID[2:] + (2 * cshare, depth), BF16),
             pltpu.VMEM((2, width, width), BF16), pltpu.VMEM((HALO, depth), BF16),
-            pltpu.VMEM((16, chans), F32), one_dma((4,)), one_dma((2,)), one_dma((2,)), *exchange_scratch(groups, width, seqs),
+            pltpu.VMEM((16, chans), F32), pltpu.VMEM((groups, srows, width), BF16),
+            pltpu.VMEM((3, groups, lrows, width), F32), pltpu.VMEM(GRID + (cshare, depth), BF16),
+            one_dma((4,)), one_dma((2,)), one_dma((2,)), one_dma, *exchange_scratch(groups, width, seqs),
             *front_scratch,
         ],
         compiler_params=params(56, collective_id=0, has_side_effects=True),
@@ -1501,7 +1557,7 @@
     )(
         long_tokens.reshape(lrows, depth), short_tokens.reshape(srows, depth),
         long_cotangent.reshape(lrows, depth), short_cotangent.reshape(srows, depth), long_length,
-        gain1, *channel, decay_gate_weight, input_gate_weight, *front_own,
+        gain1, *channel, decay_gate_weight, input_gate_weight, gain2, *front_own,
     )
     if fast:
         pairw, outw, w_first = made
@@ -1560,34 +1616,32 @@
     else:
         mlp_links, w_last, more_specs, more_shapes, more_scratch = None, [w_second], [], [], []
         dw_shape, more_params = (steps,) + block, {}
-    out_l, out_s, d_res, rlow, mix_l, gain2_grad, dmlp, *more_out = pl.pallas_call(
+    out_l, out_s, d_res, rlow, gain2_grad, dmlp, *more_out = pl.pallas_call(
         functools.partial(mlp_kernel, ltiles, tokens // TILE, mlp_links),
         grid=(steps,),
         in_specs=[
-            whole((total, depth)), whole((tokens, depth)), whole((HALO + lrows, chans)),
-            whole((HALO + lrows, chans)), whole((HALO + lrows, chans)), whole((8, chans)),
-            whole((srows, chans)), whole((SLOTS, cshare, depth)), whole((1, depth)), hbm,
+            whole((tokens, depth)), whole((tokens, depth)), whole((tokens, depth)),
+            whole((1, depth)), hbm,
             *[whole(w.shape) if fast else hbm for w in w_last],
         ],
         out_specs=[
             whole((lrows, depth)), whole((srows, depth)), whole((tokens, depth)), whole((tokens, depth)),
-            whole((lrows, chans)), whole((8, depth)), hbm, *more_specs,
+            whole((8, depth)), hbm, *more_specs,
         ],
         out_shape=[
             shape_of((lrows, depth), BF16), shape_of((srows, depth), BF16),
             shape_of((tokens, depth), F32), shape_of((tokens, depth), BF16),
-            shape_of((lrows, chans), BF16),
             shape_of((8, depth), F32), shape_of(dw_shape, BF16), *more_shapes,
         ],
         scratch_shapes=[
-            pltpu.VMEM((tokens, depth), BF16), pltpu.VMEM((tokens, depth), F32),
-            pltpu.VMEM((tokens, depth), F32), pltpu.VMEM((tokens, 2 * hid), F32),
+            pltpu.VMEM((tokens, depth), F32), pltpu.VMEM((tokens, depth), F32),
+            pltpu.VMEM((tokens, 2 * hid), F32),
             pltpu.VMEM((tokens, hid), F32), pltpu.VMEM((tokens, hid), BF16),
             pltpu.VMEM((tokens, 2 * hid), BF16), wbuf, dwbuf, one_dma((2, 3)), one_dma, *more_scratch,
         ],
         compiler_params=params(62, **more_params),
         name="mlp",
-    )(x, cot, states, reach, gp, s_in, mix_s, outw, gain2, w_first, *w_last)
+    )(residual, normed2, cot, gain2, w_first, *w_last)
 
     gate_shape, sum_shape = GRID + (bwidth // 2, bwidth), GRID + (8, 128)
     grads_shape = shape_of(GRID + (cshare, depth), BF16)
@@ -1603,7 +1657,7 @@
                 )
                 number += 1
         for which in (1, 2, 3):
-            if which == 2:
+            if which == 3:
                 tail_chunks.append((SUMS, 0, 5, None, (0, 8), 7, 0))
                 tail_chunks.append((GATES, 0, 4, None, (0, bwidth // 2), 6, 0))
                 during = len(tail_chunks) - 2
@@ -1613,9 +1667,9 @@
                 )
                 number += 1
         tail_lags = (1, 3, 3, 3, 1, 1, 1, 1)
-        marks = [[5.0 * g + t for t in (0.0, 1.5, 4.0)] for g in range(groups)]
+        marks = [[6.0 * g + t for t in (0.0, 1.5, 4.0)] for g in range(groups)]
         marks += [
-            [5.0 * groups + 12.5 * g + t for t in (0.0, 5.0, 6.0, 9.0, 10.5, 12.5)] for g in range(groups)
+            [6.0 * groups + 11.5 * g + t for t in (0.0, 5.0, 6.0, 9.0, 9.5, 11.5)] for g in range(groups)
         ]
         plan = paced(during, 3, marks)
         plan[-1][-1] += range(during, len(tail_chunks) + sum(tail_lags) + 1)

time: 377 us -> 373 us (0.989)
  Pallas kernels: 374 us -> 368 us
    pallas_call x1, Pallas kernels: 107 us -> 100 us  [shards(): pl.pallas_call(functools.partial(mlp_kernel, ltiles, tokens // TILE, mlp_...]
where the time goes in v9:
time: 373 us; the launch traced here: 371 us
  Pallas kernels  368 us (99%)
    pallas_call x1, Pallas kernels, shards(): pl.pallas_call(functools.partial(tail_kernel, ltiles, tiles, groups, tail...  149 us
    pallas_call x1, Pallas kernels, shards(): pl.pallas_call(functools.partial(front_kernel, ltiles, tiles, groups, fro...  111 us
    pallas_call x1, Pallas kernels, shards(): pl.pallas_call(functools.partial(mlp_kernel, ltiles, tokens // TILE, mlp_...  100 us
    pallas_call x1, Pallas kernels, shards(): pl.pallas_call(functools.partial(finish_kernel, len(large)), in_specs=[hb...  7.56 us

profile of v9, /device:TPU:0, one launch (start us, length us, event | category | flops | bytes accessed | tf_op | source)
XLA Modules:
  0.0 370.7 jit_solution(15770299303050330930)
XLA Ops:
  1.3 1.3 divide_multiply_fusion
  2.6 111.0 %front.1 = (f32[656,1536]{1,0:T(8,128)}, f32[656,1536]{1,0:T(8,128)}, f32[656,1536]{1,0:T(8,128)}, f32[656,1536]{1,0:T(8,128)}, f32[656,1536]{1,0:T(8,128)}, /*i...) custom-call(bf16[128,1024]{1,0:T(8,128)(2,1)} %bitcast.32, ...), custom_call_target="tpu_custom_call" | custom-call | tf_op jit(solution)/shard_map/front/pallas_call | solution.py:1524
  113.7 100.5 %mlp.1 = (bf16[128,1024]{1,0:T(8,128)(2,1)}, bf16[512,1024]{1,0:T(8,128)(2,1)}, f32[640,1024]{1,0:T(8,128)}, bf16[640,1024]{1,0:T(8,128)(2,1)}, f32[8,1024]{1,0:...) custom-call(f32[640,1024]{1,0:T(8,128)} %get-tuple-element.77.refs_0, ...), custom_call_target="tpu_custom_call" | custom-call | tf_op jit(solution)/shard_map/mlp/pallas_call | solution.py:1619
  214.2 148.8 %tail.1 = (f32[128,1024]{1,0:T(8,128)}, f32[512,1024]{1,0:T(8,128)}, f32[8,1024]{1,0:T(8,128)}, bf16[2,2,2,4,48,1024]{5,4,3,2,1,0:T(8,128)(2,1)}, bf16[2,2,2,4,4...) custom-call(bf16[656,1024]{1,0:T(8,128)(2,1)} %get-tuple-element.83., ...), custom_call_target="tpu_custom_call" | custom-call | tf_op jit(solution)/shard_map/tail/pallas_call | solution.py:1691
  363.0 7.6 %finish.1 = (bf16[128,1024]{1,0:T(8,128)(2,1)}, bf16[512,1024]{1,0:T(8,128)(2,1)}, f32[128,1024]{1,0:T(8,128)}, f32[512,1024]{1,0:T(8,128)}, f32[48,1024]{1,0:T(...) custom-call(bf16[128,1024]{1,0:T(8,128)(2,1)} %get-tuple-element.81., ...), custom_call_target="tpu_custom_call" | custom-call | tf_op jit(solution)/shard_map/finish/pallas_call | solution.py:1747

commit v10 on v9

--- a/solution.py
+++ b/solution.py
@@ -337,7 +337,7 @@
 
 
 def add_into(into, i, part, j):
-    into[i] = (into[i].astype(F32) + part[j].astype(F32)).astype(into.dtype)
+    into[i] = into[i] + part[j]
 
 
 class Piece:
@@ -859,8 +859,7 @@
             def _(k):
                 i, j, m = k // (2 * GRID[3]), (k // GRID[3]) % 2, k % GRID[3]
                 for n in range(3):
-                    both = dwbuf[n, i, j, c, m].astype(F32) + got_ref[n, i, j, m].astype(F32)
-                    dwbuf[n, i, j, c, m] = both.astype(BF16)
+                    dwbuf[n, i, j, c, m] = dwbuf[n, i, j, c, m] + got_ref[n, i, j, m]
 
             if s < steps - 1:
                 pl.semaphore_signal(

time: 373 us -> 371 us (level)
  no operation moved by 1% of the time
where the time goes in v10:
time: 371 us; the launch traced here: 369 us
  Pallas kernels  366 us (99%)
    pallas_call x1, Pallas kernels, shards(): pl.pallas_call(functools.partial(tail_kernel, ltiles, tiles, groups, tail...  148 us
    pallas_call x1, Pallas kernels, shards(): pl.pallas_call(functools.partial(front_kernel, ltiles, tiles, groups, fro...  111 us
    pallas_call x1, Pallas kernels, shards(): pl.pallas_call(functools.partial(mlp_kernel, ltiles, tokens // TILE, mlp_...  99.7 us
    pallas_call x1, Pallas kernels, shards(): pl.pallas_call(functools.partial(finish_kernel, len(large)), in_specs=[hb...  7.56 us

profile of v10, /device:TPU:0, one launch (start us, length us, event | category | flops | bytes accessed | tf_op | source)
XLA Modules:
  0.0 369.3 jit_solution(17914058599797694227)
XLA Ops:
  1.3 1.3 divide_multiply_fusion
  2.6 111.0 %front.1 = (f32[656,1536]{1,0:T(8,128)}, f32[656,1536]{1,0:T(8,128)}, f32[656,1536]{1,0:T(8,128)}, f32[656,1536]{1,0:T(8,128)}, f32[656,1536]{1,0:T(8,128)}, /*i...) custom-call(bf16[128,1024]{1,0:T(8,128)(2,1)} %bitcast.32, ...), custom_call_target="tpu_custom_call" | custom-call | tf_op jit(solution)/shard_map/front/pallas_call | solution.py:1523
  113.7 99.7 %mlp.1 = (bf16[128,1024]{1,0:T(8,128)(2,1)}, bf16[512,1024]{1,0:T(8,128)(2,1)}, f32[640,1024]{1,0:T(8,128)}, bf16[640,1024]{1,0:T(8,128)(2,1)}, f32[8,1024]{1,0:...) custom-call(f32[640,1024]{1,0:T(8,128)} %get-tuple-element.77.refs_0, ...), custom_call_target="tpu_custom_call" | custom-call | tf_op jit(solution)/shard_map/mlp/pallas_call | solution.py:1618
  213.4 148.2 %tail.1 = (f32[128,1024]{1,0:T(8,128)}, f32[512,1024]{1,0:T(8,128)}, f32[8,1024]{1,0:T(8,128)}, bf16[2,2,2,4,48,1024]{5,4,3,2,1,0:T(8,128)(2,1)}, bf16[2,2,2,4,4...) custom-call(bf16[656,1024]{1,0:T(8,128)(2,1)} %get-tuple-element.83., ...), custom_call_target="tpu_custom_call" | custom-call | tf_op jit(solution)/shard_map/tail/pallas_call | solution.py:1690
  361.6 7.6 %finish.1 = (bf16[128,1024]{1,0:T(8,128)(2,1)}, bf16[512,1024]{1,0:T(8,128)(2,1)}, f32[128,1024]{1,0:T(8,128)}, f32[512,1024]{1,0:T(8,128)}, f32[48,1024]{1,0:T(...) custom-call(bf16[128,1024]{1,0:T(8,128)(2,1)} %get-tuple-element.81., ...), custom_call_target="tpu_custom_call" | custom-call | tf_op jit(solution)/shard_map/finish/pallas_call | solution.py:1746
